TPU v7x, 32 devices: a whole 2x2x4 slice. The times are simulated.
32 devices in a mesh: seq: 4 (over z), ctx: 2 (over x), wt: 4 (over y, core).
Axes of the slice: x: 2, y: 2, z: 4, core: 2. Of those that a mesh axis runs over, the one named last changes fastest.
Arguments:
- tokens: bfloat16 [16, 1024, 512], P(('seq', 'wt'), 'ctx'), may hold values from -6 to 6
- cotangent: bfloat16 [16, 1024, 512], P(('seq', 'wt'), 'ctx'), may hold values from -6 to 6
- deal: int32 [4], replicated, may hold values from 0 to 3, each once
- memory_len: int32 [16, 4], P(('seq', 'wt')), may hold values from 0 to 768, as said below
- neighbours: int32 [16, 1024, 4], P(('seq', 'wt'), 'ctx'), may hold values from 0 to 1023
- w_qkv: bfloat16 [512, 1536], P('wt'), may hold values from -0.25 to 0.25
- w_out: bfloat16 [512, 512], P('wt'), may hold values from -1 to 1
- w_up: bfloat16 [512, 2048], P('wt'), may hold values from -0.25 to 0.25
- w_down: bfloat16 [2048, 512], P('wt'), may hold values from -0.125 to 0.125
- w_memory: bfloat16 [512, 512], P('wt'), may hold values from -0.5 to 0.5
- gain_attn: bfloat16 [512], P('wt'), may hold values from 0.5 to 1.5
- gain_ffn: bfloat16 [512], P('wt'), may hold values from 0.5 to 1.5
- gate_vec: bfloat16 [512], P('wt'), may hold values from -0.25 to 0.25
- slopes: bfloat16 [8], P('wt'), may hold values from 0.019897461 to 0.5
Outputs:
- layer_out: bfloat16 [16, 1024, 512], P(('seq', 'wt'), 'ctx')
- grad_tokens: float32 [16, 1024, 512], P(('seq', 'wt'), 'ctx')
- grad_qkv: float32 [512, 1536], P('wt')
- grad_out: float32 [512, 512], P('wt')
- grad_up: float32 [512, 2048], P('wt')
- grad_down: float32 [2048, 512], P('wt')
- grad_memory: float32 [512, 512], P('wt')
- grad_gain_attn: float32 [512], P('wt')
- grad_gain_ffn: float32 [512], P('wt')
- grad_gate: float32 [512], P('wt')
- grad_slopes: float32 [8], P('wt')
Inputs may be any that keep to these rules, and one draw needn't show every extreme that they name: deal is a permutation of the blocks; device c of ctx holds block slots 2c and 2c + 1. `memory_len`: block 3 of every sequence has the value 1024 - 256.
All inputs are finite; a program needn't handle non-finite values.
Results may differ from a plain program's by a relative error of at most 0.028.
Values may be sent and summed in bfloat16 or wider, within the bound.
No kernel may reach another device: no remote copies, remote signals or barrier semaphores. Data moves between devices by JAX's collectives and lax.ppermute only.
A program may use at most 256 MiB of HBM per device.

v0:
```python
import functools
import math
import jax
import jax.numpy as jnp
from jax import lax
from jax.experimental import pallas as pl
from jax.experimental.pallas import tpu as pltpu
from jax.sharding import PartitionSpec as P

EPSILON = 1e-05
F32 = jnp.float32
BF16 = jnp.bfloat16
NT = (((1,), (1,)), ((), ()))
NN = (((1,), (0,)), ((), ()))
HIDDEN = 1e12
ABSENT = -1e30
VMEM = 56 * 1024 * 1024
CURVE = math.sqrt(2.0 / math.pi)
CUBIC = 0.044715


def product(left, right, dims=NN):
    return lax.dot_general(left, right, dims, preferred_element_type=F32)


def params():
    return pltpu.CompilerParams(vmem_limit_bytes=VMEM)


def like(shape, dtype):
    return jax.ShapeDtypeStruct(shape, dtype)


def in_place():
    return pl.BlockSpec(memory_space=pl.ANY)


def scalar():
    return pl.BlockSpec(memory_space=pltpu.SMEM)


def swap(value, axis, bit):
    size = lax.axis_size(axis)
    return lax.ppermute(value, axis, [(i, i ^ bit) for i in range(size)])


def bits_of(axis):
    bits = []
    bit = 1
    while bit < lax.axis_size(axis):
        bits.append(bit)
        bit *= 2
    return bits


def side_of(axis, bit):
    return (lax.axis_index(axis) // bit) % 2


def hold(value, *before):
    return lax.optimization_barrier((value,) + before)[0]


def add_low(left, right):
    return (left.astype(F32) + right.astype(F32)).astype(BF16)


def halve(part, axis, bit):
    side = side_of(axis, bit)
    both = part.reshape((2, part.shape[0] // 2) + part.shape[1:])
    got = swap(lax.dynamic_index_in_dim(both, 1 - side, 0, False), axis, bit)
    return add_low(lax.dynamic_index_in_dim(both, side, 0, False), got)


def widen(part, axis, bit):
    other = swap(part, axis, bit)
    high = side_of(axis, bit) == 1
    return jnp.concatenate([jnp.where(high, other, part), jnp.where(high, part, other)], axis=0)


def near_halves(part):
    for bit in bits_of("ctx"):
        part = halve(part, "ctx", bit)
    return part


def near_whole(part):
    for bit in reversed(bits_of("ctx")):
        part = widen(part, "ctx", bit)
    return part


def far_halves(part):
    for bit in bits_of("seq"):
        part = halve(part, "seq", bit)
    return part


def far_whole(part):
    for bit in reversed(bits_of("seq")):
        part = widen(part, "seq", bit)
    return part


def far_both(part):
    for bit in bits_of("seq"):
        part = add_low(part, swap(part, "seq", bit))
    return part


def spread(values):
    centred = values - jnp.mean(values, axis=-1, keepdims=True)
    scale = lax.rsqrt(jnp.mean(centred * centred, axis=-1, keepdims=True) + EPSILON)
    return centred * scale, scale


def spread_back(unit, scale, grad):
    along = jnp.mean(grad * unit, axis=-1, keepdims=True)
    return scale * (grad - jnp.mean(grad, axis=-1, keepdims=True) - unit * along)


def lay_rows(width, pieces):
    arrays = [piece[0] for piece in pieces]

    def body(*refs):
        first = 0
        for ref, (_, col) in zip(refs, pieces):
            refs[-1][first : first + ref.shape[0], :] = ref[:, col : col + width]
            first += ref.shape[0]

    total = sum(array.shape[0] for array in arrays)
    vmem = pl.BlockSpec(memory_space=pltpu.VMEM)
    return pl.pallas_call(
        body,
        in_specs=[vmem] * len(arrays),
        out_specs=vmem,
        out_shape=like((total, width), BF16),
        compiler_params=params(),
        cost_estimate=pl.CostEstimate(flops=0, transcendentals=0, bytes_accessed=4 * total * width),
        name="lay_rows",
    )(*arrays)


def project_body(me_ref, own_ref, other_ref, p0, p1, p2, p3, q_ref, k_ref, v_ref, turned_ref, w_ref, small_ref, few, sem):
    step = pl.program_id(0)
    width = own_ref.shape[1]
    shard = p0.shape[0]

    @pl.when(step == 0)
    def _():
        copies = []
        for r, pack in enumerate((p0, p1, p2, p3)):
            place = pl.multiple_of((me_ref[0] ^ r) * shard, shard)
            copies.append(
                pltpu.make_async_copy(pack.at[:, 0 : 3 * width], w_ref.at[pl.ds(place, shard), :], sem.at[2 * r])
            )
            copies.append(
                pltpu.make_async_copy(
                    pack.at[0:16, 3 * width : 3 * width + shard], few.at[:, pl.ds(place, shard)], sem.at[2 * r + 1]
                )
            )
        for copy in copies:
            copy.start()
        for copy in copies:
            copy.wait()
        small_ref[...] = few[...].astype(F32)

    tokens = jnp.where(step == 0, own_ref[...], other_ref[...]).astype(F32)
    unit, _ = spread(tokens)
    a1 = (unit * few[0:1, :].astype(F32)).astype(BF16)
    turned_ref[...] = a1.T

    @pl.when(step == 0)
    def _():
        q = product(a1, w_ref[:, 0:width]).astype(BF16)
        q_ref[...] = (q.astype(F32) * 0.125).astype(BF16)

    k_ref[...] = product(a1, w_ref[:, width : 2 * width]).astype(BF16)
    v_ref[...] = product(a1, w_ref[:, 2 * width : 3 * width]).astype(BF16)


def project(me, own, others, packs):
    rows, width = own.shape
    steps = 1 + others.shape[0] // rows
    whole = lambda i: (0, 0)
    return pl.pallas_call(
        project_body,
        grid=(steps,),
        in_specs=[
            scalar(),
            pl.BlockSpec((rows, width), whole),
            pl.BlockSpec((rows, width), lambda i: (jnp.maximum(i - 1, 0), 0)),
        ]
        + [in_place()] * 4,
        out_specs=[
            pl.BlockSpec((rows, width), whole),
            pl.BlockSpec((rows, width), lambda i: (i, 0)),
            pl.BlockSpec((rows, width), lambda i: (i, 0)),
            pl.BlockSpec((width, rows), lambda i: (0, i)),
            pl.BlockSpec((width, 3 * width), whole),
            pl.BlockSpec((16, width), whole),
        ],
        out_shape=[
            like((rows, width), BF16),
            like((rows * steps, width), BF16),
            like((rows * steps, width), BF16),
            like((width, rows * steps), BF16),
            like((width, 3 * width), BF16),
            like((16, width), F32),
        ],
        scratch_shapes=[pltpu.VMEM((16, width), BF16), pltpu.SemaphoreType.DMA((8,))],
        compiler_params=params(),
        cost_estimate=pl.CostEstimate(flops=6 * rows * steps * width * width, transcendentals=0, bytes_accessed=6000000),
        name="project",
    )(me, own, others, *packs)


def forward_body(rows, small_ref, q_ref, k_ref, v_ref, b_ref, c_ref, o_ref, m_ref, r1_ref, r2_ref, e1_ref, e2_ref):
    low_lanes = lax.broadcasted_iota(jnp.int32, (rows, 128), 1) < 64
    for start in range(0, q_ref.shape[0], rows):
        at = pl.ds(start, rows)
        mixed = []
        for side in range(2):
            slope = small_ref[3:4, side : side + 1]
            q_head = jnp.where(low_lanes == (side == 0), q_ref[at, :], 0).astype(BF16)
            raw = product(q_head, k_ref[...], NT)
            for table in (e1_ref, e2_ref):
                values = raw - slope * b_ref[at, :] if table is e1_ref else raw + c_ref[at, :]
                peak = jnp.max(values, axis=1, keepdims=True)
                shifted = jnp.exp(values - peak)
                total = jnp.sum(shifted, axis=1, keepdims=True)
                weights = shifted.astype(BF16)
                table[side, at, :] = weights
                mixed.append((product(weights, v_ref[...]), 1.0 / total))
        for slot, value_ref, recip_ref in ((0, o_ref, r1_ref), (1, m_ref, r2_ref)):
            recip = jnp.where(low_lanes, mixed[slot][1], mixed[2 + slot][1])
            recip_ref[at, :] = recip
            value_ref[at, :] = jnp.where(low_lanes, mixed[slot][0], mixed[2 + slot][0]) * recip


def attend_forward(small, q, k, v, bias, count):
    row_count, width = q.shape
    key_count = k.shape[0]
    pairs = width // 128
    step_rows = max(64, min(row_count, (512 * 1024) // key_count))
    rows = min(256, step_rows)
    elements = 2 * pairs * row_count * key_count
    own = lambda p, i: (i, p)
    return pl.pallas_call(
        functools.partial(forward_body, rows),
        grid=(pairs, row_count // step_rows),
        in_specs=[
            pl.BlockSpec((16, 128), lambda p, i: (0, p)),
            pl.BlockSpec((step_rows, 128), own),
            pl.BlockSpec((key_count, 128), lambda p, i: (0, p)),
            pl.BlockSpec((key_count, 128), lambda p, i: (0, p)),
            pl.BlockSpec((step_rows, key_count), lambda p, i: (i, 0)),
            pl.BlockSpec((step_rows, key_count), lambda p, i: (i, 0)),
        ],
        out_specs=[pl.BlockSpec((step_rows, 128), own)] * 4
        + [pl.BlockSpec((2, step_rows, key_count), lambda p, i: (p, i, 0))] * 2,
        out_shape=[like((row_count, width), F32)] * 4 + [like((2 * pairs, row_count, key_count), BF16)] * 2,
        compiler_params=params(),
        cost_estimate=pl.CostEstimate(
            flops=elements * 64 * 2 * 3, transcendentals=2 * elements, bytes_accessed=4 * elements
        ),
        name="attend_forward",
    )(small, q, k, v, bias, count)


def middle_body(
    me_ref, small_ref, tokens_ref, cot_ref, o_ref, m_ref, p0, p1, p2, p3,
    out_ref, gh1_ref, go_ref, gm_ref, gate_ref, g0, g1, g2, g3, h0, h1_ref, h2_ref, h3,
    w_out, w_memory, w_down, w_up, act, slope, gu, a2_turned, o_turned, m_turned, sem,
):
    rows, width = tokens_ref.shape
    shard = width // 4
    groups = w_down.shape[0] // width
    copies = []
    for r, pack in enumerate((p0, p1, p2, p3)):
        device = me_ref[0] ^ r
        place = pl.ds(pl.multiple_of(device * shard, shard), shard)
        down = pl.ds(pl.multiple_of(device * width, width), width)
        targets = [w_out.at[place], w_memory.at[place]] + [w_up.at[group, place] for group in range(groups)]
        pieces = [(pack.at[n * shard : (n + 1) * shard], target) for n, target in enumerate(targets)]
        pieces.append((pack.at[len(targets) * shard : len(targets) * shard + width], w_down.at[down]))
        copies.append([pltpu.make_async_copy(*piece, sem.at[r, n]) for n, piece in enumerate(pieces)])
    for part in zip(*copies):
        for copy in part:
            copy.start()
    gain = small_ref[1:2, :]
    gate_vec = small_ref[2:3, :]
    o_low = o_ref[...].astype(BF16)
    m_low = m_ref[...].astype(BF16)
    for copy in copies:
        copy[0].wait()
        copy[1].wait()
    h1 = tokens_ref[...].astype(F32) + product(o_low, w_out[...])
    mem = product(m_low, w_memory[...])
    o_turned[...] = o_low.T
    m_turned[...] = m_low.T
    unit, scale = spread(h1)
    a2 = (unit * gain).astype(BF16)
    a2_turned[...] = a2.T
    for copy in copies:
        for piece in copy[2:]:
            piece.wait()
    h2 = h1
    for group in range(groups):
        u = product(a2, w_up[group])
        square = u * u
        bent = jnp.tanh(CURVE * u * (1.0 + CUBIC * square))
        half = 0.5 * (1.0 + bent)
        active = (u * half).astype(BF16)
        slope[group] = half + 0.5 * u * (1.0 - bent * bent) * (CURVE * (1.0 + 3.0 * CUBIC * square))
        act[group] = active.T
        h2 = h2 + product(active, w_down[group * width : (group + 1) * width, :])
    gate = jax.nn.sigmoid(jnp.sum(h2 * gate_vec, axis=1, keepdims=True))
    apart = mem - h2
    out_ref[...] = (h2 + gate * apart).astype(BF16)
    c = cot_ref[...].astype(F32)
    grad_mem = (c * gate).astype(BF16)
    dz = jnp.sum(c * apart, axis=1, keepdims=True) * gate * (1.0 - gate)
    gh2 = c * (1.0 - gate) + dz * gate_vec
    gate_ref[...] = jnp.broadcast_to(jnp.sum(dz * h2, axis=0, keepdims=True), gate_ref.shape)
    gf = gh2.astype(BF16)
    gm_ref[...] = product(grad_mem, w_memory[...], NT).astype(BF16)
    ga2 = None
    for group in range(groups):
        back = product(gf, w_down[group * width : (group + 1) * width, :], NT)
        low = (back * slope[group]).astype(BF16)
        gu[group] = low
        more = product(low, w_up[group], NT)
        ga2 = more if ga2 is None else ga2 + more
    gh1 = gh2 + spread_back(unit, scale, ga2 * gain)
    gh1_ref[...] = gh1
    ga = gh1.astype(BF16)
    go_ref[...] = product(ga, w_out[...], NT).astype(BF16)
    for r, (grad_ref, up_ref) in enumerate(((g0, h0), (g1, h1_ref), (g2, h2_ref), (g3, h3))):
        device = me_ref[0] ^ r
        place = pl.ds(pl.multiple_of(device * shard, shard), shard)
        grad_ref[0:shard, :] = product(o_turned[place, :], ga).astype(BF16)
        grad_ref[shard : 2 * shard, :] = product(m_turned[place, :], grad_mem).astype(BF16)
        grad_ref[2 * shard : 2 * shard + width, :] = product(act[device], gf).astype(BF16)
        for group in range(groups):
            first = group * shard
            up_ref[first : first + shard, :] = product(a2_turned[place, :], gu[group]).astype(BF16)


def middle(me, small, tokens, cotangent, o, m, packs, groups):
    rows, width = tokens.shape
    shard = width // 4
    vmem = pl.BlockSpec(memory_space=pltpu.VMEM)
    square = lambda dtype: pltpu.VMEM((width, width), dtype)
    return pl.pallas_call(
        middle_body,
        in_specs=[scalar()] + [vmem] * 5 + [in_place()] * 4,
        out_specs=[vmem] * 13,
        out_shape=[
            like((rows, width), BF16),
            like((rows, width), F32),
            like((rows, width), BF16),
            like((rows, width), BF16),
            like((8, width), F32),
        ]
        + [like((2 * shard + width, width), BF16)] * 4
        + [like((groups * shard, width), BF16)] * 4,
        scratch_shapes=[
            square(BF16),
            square(BF16),
            pltpu.VMEM((groups * width, width), BF16),
            pltpu.VMEM((groups, width, width), BF16),
            pltpu.VMEM((groups, width, rows), BF16),
            pltpu.VMEM((groups, rows, width), F32),
            pltpu.VMEM((groups, rows, width), BF16),
            pltpu.VMEM((width, rows), BF16),
            pltpu.VMEM((width, rows), BF16),
            pltpu.VMEM((width, rows), BF16),
            pltpu.SemaphoreType.DMA((4, 3 + groups)),
        ],
        compiler_params=params(),
        cost_estimate=pl.CostEstimate(
            flops=2 * rows * width * width * 3 * 10, transcendentals=4 * rows * width, bytes_accessed=16000000
        ),
        name="middle",
    )(me, small, tokens, cotangent, o, m, *packs)


def backward_body(
    several, rows, q_ref, k_ref, v_ref, go_ref, gm_ref, o_ref, m_ref, r1_ref, r2_ref, b_ref, e1_ref, e2_ref,
    gq_ref, gk_ref, gv_ref, gs_ref,
):
    low_lanes = lax.broadcasted_iota(jnp.int32, (rows, 128), 1) < 64
    keys = k_ref[...]
    vals = v_ref[...]
    totals = [None, None]
    for start in range(0, q_ref.shape[0], rows):
        at = pl.ds(start, rows)
        g1 = (go_ref[at, :].astype(F32) * r1_ref[at, :]).astype(BF16)
        g2 = (gm_ref[at, :].astype(F32) * r2_ref[at, :]).astype(BF16)
        t1 = g1.astype(F32) * o_ref[at, :]
        t2 = g2.astype(F32) * m_ref[at, :]
        q_turned = q_ref[at, :].T
        g1_turned = g1.T
        g2_turned = g2.T
        grads = []
        for side in range(2):
            mine = low_lanes == (side == 0)
            d1 = jnp.sum(jnp.where(mine, t1, 0.0), axis=1, keepdims=True)
            d2 = jnp.sum(jnp.where(mine, t2, 0.0), axis=1, keepdims=True)
            e1 = e1_ref[side, at, :]
            e2 = e2_ref[side, at, :]
            p1 = product(jnp.where(mine, g1, 0).astype(BF16), vals, NT)
            ds1 = e1.astype(F32) * (p1 - d1)
            slope_term = jnp.sum(ds1 * b_ref[at, :], axis=0, keepdims=True)
            p2 = product(jnp.where(mine, g2, 0).astype(BF16), vals, NT)
            ds = (ds1 + e2.astype(F32) * (p2 - d2)).astype(BF16)
            grads.append(product(ds, keys))
            head = slice(64 * side, 64 * side + 64)
            gk = product(q_turned[head, :], ds)
            gv = product(g1_turned[head, :], e1) + product(g2_turned[head, :], e2)
            if start > 0:
                gk, gv, slope_term = (have + more for have, more in zip(totals[side], (gk, gv, slope_term)))
            totals[side] = (gk, gv, slope_term)
        gq = jnp.where(low_lanes, grads[0], grads[1]) * 0.125
        if not several:
            gq_ref[at, :] = gq.astype(gq_ref.dtype)
        else:
            gq_ref[at, :] = jnp.where(pl.program_id(1) == 0, gq, gq_ref[at, :] + gq)
    gk_ref[...] = jnp.concatenate([totals[0][0], totals[1][0]], axis=0).astype(BF16).T
    gv_ref[...] = jnp.concatenate([totals[0][1], totals[1][1]], axis=0).astype(BF16).T
    for side in range(2):
        term = totals[side][2]
        parts = term[:, 0:128]
        for first in range(128, term.shape[1], 128):
            parts = parts + term[:, first : first + 128]
        if not several:
            gs_ref[side : side + 1, :] = parts
        else:
            gs_ref[side : side + 1, :] = jnp.where(pl.program_id(1) == 0, parts, gs_ref[side : side + 1, :] + parts)


def attend_backward(q, k, v, go, gm, saved, bias, first, pairs):
    o, m, r1, r2, e1, e2 = saved
    row_count = q.shape[0]
    key_count = k.shape[0]
    step_keys = min(1024, key_count)
    several = key_count > step_keys
    elements = 2 * pairs * row_count * key_count
    wide = pl.BlockSpec((row_count, 128), lambda p, c: (0, p + first))
    near = pl.BlockSpec((step_keys, 128), lambda p, c: (c, p + first))
    table = pl.BlockSpec((2, row_count, step_keys), lambda p, c: (p + first, 0, c))
    own = pl.BlockSpec((step_keys, 128), lambda p, c: (c, p))
    return pl.pallas_call(
        functools.partial(backward_body, several, 256),
        grid=(pairs, key_count // step_keys),
        in_specs=[wide, near, near, wide, wide, wide, wide, wide, wide]
        + [pl.BlockSpec((row_count, step_keys), lambda p, c: (0, c)), table, table],
        out_specs=[
            pl.BlockSpec((row_count, 128), lambda p, c: (0, p)),
            own,
            own,
            pl.BlockSpec((None, 8, 128), lambda p, c: (p, 0, 0)),
        ],
        out_shape=[
            like((row_count, 128 * pairs), F32 if several else BF16),
            like((key_count, 128 * pairs), BF16),
            like((key_count, 128 * pairs), BF16),
            like((pairs, 8, 128), F32),
        ],
        compiler_params=params(),
        cost_estimate=pl.CostEstimate(flops=elements * 64 * 2 * 6, transcendentals=0, bytes_accessed=4 * elements),
        name="attend_backward",
    )(q, k, v, go, gm, o, m, r1, r2, bias, e1, e2)


def last_body(me_ref, turned_ref, gq_ref, gk_ref, gv_ref, w_ref, gs_ref, gate_ref, near_ref, own_ref, g0, g1, g2, g3):
    rows, width = gq_ref.shape
    shard = width // 4
    gq = gq_ref[...].astype(BF16)
    w_q = w_ref[:, 0:width]
    w_k = w_ref[:, width : 2 * width]
    w_v = w_ref[:, 2 * width : 3 * width]
    for first in range(rows, gk_ref.shape[0], rows):
        at = slice(first, first + rows)
        part = product(gk_ref[at, :], w_k, NT) + product(gv_ref[at, :], w_v, NT)
        near_ref[first - rows : first, :] = part.astype(BF16)
    own_ref[...] = product(gq, w_q, NT) + product(gk_ref[0:rows, :], w_k, NT) + product(gv_ref[0:rows, :], w_v, NT)
    lane = lax.broadcasted_iota(jnp.int32, (16, shard), 1)
    row = lax.broadcasted_iota(jnp.int32, (16, shard), 0)
    for r, grad_ref in enumerate((g0, g1, g2, g3)):
        device = me_ref[0] ^ r
        start = pl.multiple_of(device * shard, shard)
        a1 = turned_ref[pl.ds(start, shard), :]
        grad_ref[:, 0:width] = product(a1[:, 0:rows], gq).astype(BF16)
        grad_ref[:, width : 2 * width] = product(a1, gk_ref[...]).astype(BF16)
        grad_ref[:, 2 * width : 3 * width] = product(a1, gv_ref[...]).astype(BF16)
        sums = -jnp.sum(gs_ref[device, 0:2, :], axis=1, keepdims=True)
        block = jnp.where((row == 0) & (lane == 0), sums[0:1, :], 0.0)
        block = jnp.where((row == 0) & (lane == 1), sums[1:2, :], block)
        block = jnp.where(row == 1, gate_ref[0:1, pl.ds(start, shard)], block)
        grad_ref[:, 3 * width : 3 * width + shard] = jnp.zeros((shard, shard), BF16)
        grad_ref[0:16, 3 * width : 3 * width + shard] = block.astype(BF16)


def last(me, turned, gq, gk, gv, w, gs, gate):
    rows, width = gq.shape
    shard = width // 4
    vmem = pl.BlockSpec(memory_space=pltpu.VMEM)
    return pl.pallas_call(
        last_body,
        in_specs=[scalar()] + [vmem] * 7,
        out_specs=[vmem] * 6,
        out_shape=[like((gk.shape[0] - rows, width), BF16), like((rows, width), F32)]
        + [like((shard, 3 * width + shard), BF16)] * 4,
        compiler_params=params(),
        cost_estimate=pl.CostEstimate(
            flops=12 * gk.shape[0] * width * width, transcendentals=0, bytes_accessed=10000000
        ),
        name="last",
    )(me, turned, gq, gk, gv, w, gs, gate)


def finish_body(tokens_ref, small_ref, gh1_ref, own_ref, away_ref, out_ref):
    unit, scale = spread(tokens_ref[...].astype(F32))
    grad = (own_ref[...] + away_ref[...].astype(F32)) * small_ref[0:1, :]
    out_ref[...] = gh1_ref[...] + spread_back(unit, scale, grad)


def finish(tokens, small, gh1, own, away):
    vmem = pl.BlockSpec(memory_space=pltpu.VMEM)
    return pl.pallas_call(
        finish_body,
        in_specs=[vmem] * 5,
        out_specs=vmem,
        out_shape=like(gh1.shape, F32),
        compiler_params=params(),
        cost_estimate=pl.CostEstimate(flops=0, transcendentals=0, bytes_accessed=4000000),
        name="finish",
    )(tokens, small, gh1, own, away)


def on_device(
    tokens, cotangent, deal, memory_len, neighbours,
    w_qkv, w_out, w_up, w_down, w_memory, gain_attn, gain_ffn, gate_vec, slopes,
):
    _, row_count, width = tokens.shape
    tokens = tokens.reshape(row_count, width)
    cotangent = cotangent.reshape(row_count, width)
    neighbours = neighbours.reshape(row_count, -1)
    block_count = deal.shape[0]
    ctx_size = lax.axis_size("ctx")
    own_blocks = block_count // ctx_size
    block_len = row_count // own_blocks
    shard = gain_attn.shape[0]
    heads_here = slopes.shape[0]
    groups = w_up.shape[1] // width
    me = lax.axis_index("wt").astype(jnp.int32).reshape(1)

    short = jnp.concatenate(
        [gain_attn[None], gain_ffn[None], gate_vec[None], jnp.pad(slopes, (0, shard - heads_here))[None]], axis=0
    )
    pack = jnp.concatenate([w_qkv, jnp.pad(short, ((0, shard - 4), (0, 0)))], axis=1)
    pack_far = swap(pack, "wt", 2)
    others = swap(tokens, "ctx", 1)
    for bit in bits_of("ctx")[1:]:
        both = jnp.concatenate([tokens, others], axis=0)
        others = jnp.concatenate([others, swap(both, "ctx", bit)], axis=0)
    pack_near = swap(pack, "wt", 1)
    wide = lay_rows(width, [(w_out, 0), (w_memory, 0)] + [(w_up, width * g) for g in range(groups)] + [(w_down, 0)])

    offsets = jnp.arange(block_len, dtype=jnp.int32)
    owners = lax.axis_index("ctx") ^ jnp.arange(ctx_size, dtype=jnp.int32)
    slots = (owners[:, None] * own_blocks + jnp.arange(own_blocks, dtype=jnp.int32)[None, :]).reshape(-1)
    block_ids = jnp.arange(block_count, dtype=jnp.int32)
    slot_hot = (slots[:, None] == block_ids[None, :]).astype(jnp.int32)
    key_blocks = jnp.sum(slot_hot * deal[None, :], axis=1)
    key_pos = (key_blocks[:, None] * block_len + offsets[None, :]).reshape(-1)
    my_blocks = key_blocks[:own_blocks]
    row_pos = key_pos[:row_count]
    memory_hot = (my_blocks[:, None] == block_ids[None, :]).astype(jnp.int32)
    my_memory = jnp.sum(memory_hot * memory_len, axis=1)
    row_start = jnp.repeat(my_blocks * block_len, block_len)
    row_low = row_start - jnp.repeat(my_memory, block_len)
    distance = jnp.log1p(jnp.abs(row_pos[:, None] - key_pos[None, :]).astype(F32))
    visible = (key_pos[None, :] >= row_low[:, None]) & (key_pos[None, :] < (row_start + block_len)[:, None])
    bias = jnp.where(visible, distance, HIDDEN)
    hits = jnp.sum((neighbours[:, :, None] == key_pos[None, None, :]).astype(F32), axis=1)
    count = jnp.where(hits > 0.0, jnp.log(jnp.maximum(hits, 1.0)), ABSENT)

    pack_both = swap(hold(pack_far, bias, count), "wt", 1)
    wide_far = swap(hold(wide, pack_far), "wt", 2)
    wide_near = swap(wide, "wt", 1)

    q, k, v, turned, full_qkv, small = project(me, tokens, others, (pack, pack_near, pack_far, pack_both))
    saved = attend_forward(small, q, k, v, bias, count)
    wide_both = swap(hold(wide_far, saved[0]), "wt", 1)
    wides = (wide, wide_near, wide_far, wide_both)
    layer_out, gh1, go, gm, gate, g0, g1, g2, g3, h0, h1, h2, h3 = middle(
        me, small, tokens, cotangent, saved[0], saved[1], wides, groups
    )

    g_far = add_low(g2, swap(g3, "wt", 1))
    g_one = swap(g1, "wt", 1)
    g_got = swap(g_far, "wt", 2)
    gq, gk, gv, gs = attend_backward(q, k, v, hold(go, g_far), gm, saved, bias, 0, width // 128)
    g_sum = add_low(add_low(g0, g_one), g_got)
    h1, h3 = (hold(value, gq) for value in (h1, h3))
    h_far = add_low(h2, swap(h3, "wt", 1))
    h_one = swap(h1, "wt", 1)
    h_got = swap(h_far, "wt", 2)
    near, own, q0, q1, q2, q3 = last(me, turned, hold(gq, g_got), gk, gv, full_qkv, gs, gate)
    h_sum = add_low(add_low(h0, h_one), h_got)
    q_three = swap(q3, "wt", 1)
    q_one = swap(q1, "wt", 1)
    for bit in reversed(bits_of("ctx")[1:]):
        both = jnp.concatenate([own.astype(BF16), near], axis=0)
        fold = bit * row_count
        folded = both[:fold].astype(F32) + swap(both[fold:], "ctx", bit).astype(F32)
        own, near = folded[:row_count], folded[row_count:].astype(BF16)
    away = swap(near, "ctx", 1)
    q_far = swap(add_low(q2, q_three), "wt", 2)
    q_sum = add_low(add_low(q0, q_one), q_far)
    q_sum = near_whole(far_both(near_halves(q_sum)))
    g_sum = near_whole(far_whole(far_halves(near_halves(g_sum))))
    h_sum = near_whole(far_whole(far_halves(near_halves(h_sum))))
    grad_tokens = finish(tokens, small, gh1, own, away)

    t_qkv = q_sum[:, : 3 * width].astype(F32)
    t_slopes = q_sum[0, 3 * width : 3 * width + heads_here].astype(F32)
    t_gate = q_sum[1, 3 * width : 3 * width + shard].astype(F32)
    t_out = g_sum[:shard].astype(F32)
    t_memory = g_sum[shard : 2 * shard].astype(F32)
    t_down = g_sum[2 * shard : 2 * shard + width].astype(F32)
    t_up = jnp.concatenate([h_sum[shard * g : shard * (g + 1)] for g in range(groups)], axis=1).astype(F32)
    t_gain_one = jnp.sum(t_qkv * w_qkv.astype(F32), axis=1) / gain_attn.astype(F32)
    t_gain_two = jnp.sum(t_up * w_up.astype(F32), axis=1) / gain_ffn.astype(F32)
    return (
        layer_out[None], grad_tokens[None], t_qkv, t_out, t_up, t_down, t_memory,
        t_gain_one, t_gain_two, t_gate, t_slopes,
    )


def solution(mesh):
    rows = P(("seq", "wt"), "ctx", None)
    weight = P("wt", None)
    vector = P("wt")
    return jax.shard_map(
        on_device,
        mesh=mesh,
        in_specs=(rows, rows, P(), P(("seq", "wt"), None), rows) + (weight,) * 5 + (vector,) * 4,
        out_specs=(rows, rows) + (weight,) * 5 + (vector,) * 4,
        check_vma=False,
    )
```

profile of v0, /device:TPU:0, one launch (start us, length us, event | category | flops | bytes accessed | tf_op | source)
XLA Modules:
  0.0 201.3 jit_solution(6762054851280202972)
XLA Ops:
  3.0 3.0 %collective-permute-start.2 = (bf16[128,1664]{1,0:T(8,128)(2,1)S(1)}, bf16[128,1664]{1,0:T(8,128)(2,1)S(1)}, u32[]{:S(2)}, u32[]{:S(2)}) collective-permute-start(bf16[128,1664]{1,0:T(8,128)(2,1)S(1)} %pad_maximum_fusion.1.p0), channel_id=1, source_target_pairs={{0,2},{1,3},{2,0},{3,1},{4,6},{5,7},{6,4},{7,5},{8,10},{9,11},{10,... | collective-permute-start | bytes 1277960 | tf_op jit(solution)/shard_map/ppermute | solution.py:44
  9.6 3.2 %lay_rows.1.p0 = bf16[1280,512]{1,0:T(8,128)(2,1)} custom-call(bf16[128,512]{1,0:T(8,128)(2,1)} %refs_0_.1, bf16[128,512]{1,0:T(8,128)(2,1)} %refs_1_.1, bf16[128,2048]{1,0:T(8,128)(2,1)} %refs_5_.1, bf16[128,2048]{1,0:T(8,128)(2,1)} %refs_5_.1, bf16[128,2048]{1,0:T(8,128)(2,1)} %refs_5_.1, bf16[128,2048]{1,0:T(8,128)(2,1)} %refs_5_.1, bf16[512,512]{1,0:T(8,128)(2,1)} %refs_6_.1), custom_call_target="tpu_custom_call" | custom-call | bytes 2621440 | tf_op jit(solution)/shard_map/lay_rows/pallas_call | solution.py:133
  14.0 1.9 collective-permute-done.2.p2
  15.9 1.7 collective-permute-start.5
  17.6 1.7 log_select_fusion.c_ref
  19.4 2.6 %log-plus-one_select_fusion.b_ref = f32[512,1024]{1,0:T(8,128)} fusion(s32[512]{0:T(512)S(1)} %bitcast.101, s32[1024]{0:T(1024)S(1)} %bitcast.97, s32[512]{0:T(512)S(1)} %bitcast.100, s32[512]{0:T(512)S(1)} %bitcast.99), kind=kLoop, calls=%fused_computation.2 | loop fusion | flops 3670016 | bytes 2107392 | tf_op jit(solution)/shard_map/jit(_where)/select_n | solution.py:587
  23.9 6.6 %project.1 = (bf16[512,512]{1,0:T(8,128)(2,1)}, bf16[1024,512]{1,0:T(8,128)(2,1)}, bf16[1024,512]{1,0:T(8,128)(2,1)}, bf16[512,1024]{1,0:T(8,128)(2,1)}, bf16[512,1536]{1,0:T(8,128)(2,1)}, /*index=5*/f32[16,512]{1,0:T(8,128)}) custom-call(s32[1]{0:T(128)} %bitcast.me_ref, bf16[512,512]{1,0:T(8,128)(2,1)} %bitcast.93, ...), custom_call_target="tpu_custom_call" | custom-call | flops 1610612736 | bytes 6000000 | tf_op jit(solution)/shard_map/project/pallas_call | solution.py:186
  30.5 19.7 %attend_forward.1 = (f32[512,512]{1,0:T(8,128)}, f32[512,512]{1,0:T(8,128)}, f32[512,512]{1,0:T(8,128)}, f32[512,512]{1,0:T(8,128)}, bf16[8,512,1024]{2,1,0:T(8,128)(2,1)}, /*index=5*/bf16[8,512,1024]{2,1,0:T(8,128)(2,1)}) custom-call(f32[16,512]{1,0:T(8,128)} %get-tuple-element.54.small_ref, bf16[512,512]{1,0:T(8,128)(2,1)} %get-tuple-element.55.q_ref, ...), custom_call_target="tpu_custom_call" | custom-call | flops 1610612736 | bytes 16777216 | tf_op jit(solution)/shard_map/attend_forward/pallas_call | solution.py:249
  50.5 2.9 %collective-permute-done.6.p3 = bf16[1280,512]{1,0:T(8,128)(2,1)S(1)} collective-permute-done((bf16[1280,512]{1,0:T(8,128)(2,1)S(1)}, bf16[1280,512]{1,0:T(8,128)(2,1)S(1)}, u32[]{:S(2)}, u32[]{:S(2)}) %collective-permute-start.6) | collective-permute-done | bytes 1310752 | tf_op jit(solution)/shard_map/ppermute | solution.py:44
  54.4 15.0 %middle.1 = (bf16[512,512]{1,0:T(8,128)(2,1)}, f32[512,512]{1,0:T(8,128)}, bf16[512,512]{1,0:T(8,128)(2,1)}, bf16[512,512]{1,0:T(8,128)(2,1)}, f32[8,512]{1,0:T(...) custom-call(s32[1]{0:T(128)} %bitcast.me_ref, ...), custom_call_target="tpu_custom_call" | custom-call | flops 8053063680 | bytes 16000000 | tf_op jit(solution)/shard_map/middle/pallas_call | solution.py:355
  69.6 2.3 %collective-permute-done.7 = bf16[768,512]{1,0:T(8,128)(2,1)S(1)} collective-permute-done((bf16[768,512]{1,0:T(8,128)(2,1)}, bf16[768,512]{1,0:T(8,128)(2,1)S(1)}, u32[]{:S(2)}, u32[]{:S(2)}) %collective-permute-start.7) | collective-permute-done | bytes 786464 | tf_op jit(solution)/shard_map/ppermute | solution.py:44
  73.3 19.6 %attend_backward.1 = (bf16[512,512]{1,0:T(8,128)(2,1)}, bf16[1024,512]{1,0:T(8,128)(2,1)}, bf16[1024,512]{1,0:T(8,128)(2,1)}, f32[4,8,128]{2,1,0:T(8,128)}) custom-call(bf16[512,512]{1,0:T(8,128)(2,1)} %get-tuple-element.55.q_ref, bf16[1024,512]{1,0:T(8,128)(2,1)} %get-tuple-element.56.k_ref, bf16[1024,512]{1,0:T(8,128)(2,1)} %get-tuple-element.57.v_ref, ...), custom_call_target="tpu_custom_call" | custom-call | flops 3221225472 | bytes 16777216 | tf_op jit(solution)/shard_map/attend_backward/pallas_call | solution.py:454
  96.9 16.9 %collective-permute-done.8 = bf16[768,512]{1,0:T(8,128)(2,1)S(1)} collective-permute-done((bf16[768,512]{1,0:T(8,128)(2,1)S(1)}, bf16[768,512]{1,0:T(8,128)(2,1)S(1)}, u32[]{:S(2)}, u32[]{:S(2)}) %collective-permute-start.8) | collective-permute-done | bytes 786464 | tf_op jit(solution)/shard_map/ppermute | solution.py:44
  114.2 1.6 collective-permute-start.18
  115.8 7.0 %last.1 = (bf16[512,512]{1,0:T(8,128)(2,1)}, f32[512,512]{1,0:T(8,128)}, bf16[128,1664]{1,0:T(8,128)(2,1)}, bf16[128,1664]{1,0:T(8,128)(2,1)}, bf16[128,1664]{1,0:T(8,128)(2,1)}, /*index=5*/bf16[128,1664]{1,0:T(8,128)(2,1)}) custom-call(s32[1]{0:T(128)} %bitcast.me_ref, bf16[512,1024]{1,0:T(8,128)(2,1)} %get-tuple-element.64.turned_ref, ...), custom_call_target="tpu_custom_call" | custom-call | flops 3221225472 | bytes 10000000 | tf_op jit(solution)/shard_map/last/pallas_call | solution.py:510
  124.5 1.5 collective-permute-start.27
  126.2 1.7 collective-permute-start.19
  128.6 14.4 %collective-permute-done.27 = bf16[256,512]{1,0:T(8,128)(2,1)S(1)} collective-permute-done((bf16[256,512]{1,0:T(8,128)(2,1)S(1)}, bf16[256,512]{1,0:T(8,128)(2,1)S(1)}, u32[]{:S(2)}, u32[]{:S(2)}) %collective-permute-start.27) | collective-permute-done | bytes 262176 | tf_op jit(solution)/shard_map/ppermute | solution.py:44
  143.0 1.7 collective-permute-start.28
  145.5 3.6 %finish.1 = f32[512,512]{1,0:T(8,128)} custom-call(bf16[512,512]{1,0:T(8,128)(2,1)} %bitcast.95, f32[16,512]{1,0:T(8,128)} %get-tuple-element.54.small_ref, f32[512,512]{1,0:T(8,128)} %get-tuple-element.63.gh1_ref, f32[512,512]{1,0:T(8,128)} %get-tuple-element.81.own_ref, bf16[512,512]{1,0:T(8,128)(2,1)} %copy-done.5), custom_call_target="tpu_custom_call" | custom-call | bytes 4000000 | tf_op jit(solution)/shard_map/finish/pallas_call | solution.py:532
  149.2 2.6 %collective-permute-start.29 = (bf16[64,512]{1,0:T(8,128)(2,1)S(1)}, bf16[64,512]{1,0:T(8,128)(2,1)S(1)}, u32[]{:S(2)}, u32[]{:S(2)}) collective-permute-start(bf16[64,512]{1,0:T(8,128)(2,1)S(1)} %dynamic-slice_bitcast_fusion.6), channel_id=1, source_target_pairs={{0,16},{8,24},{16,0},{24,8},{1,17},{9,25},{17,1},{25,9},{2,18},{10... | collective-permute-start | bytes 196616 | tf_op jit(solution)/shard_map/ppermute | solution.py:44
  152.3 6.3 %collective-permute-done.29 = bf16[64,512]{1,0:T(8,128)(2,1)S(1)} collective-permute-done((bf16[64,512]{1,0:T(8,128)(2,1)S(1)}, bf16[64,512]{1,0:T(8,128)(2,1)S(1)}, u32[]{:S(2)}, u32[]{:S(2)}) %collective-permute-start.29) | collective-permute-done | bytes 65568 | tf_op jit(solution)/shard_map/ppermute | solution.py:44
  158.7 2.0 collective-permute-done.20
  161.7 3.3 %collective-permute-done.30 = bf16[64,512]{1,0:T(8,128)(2,1)S(1)} collective-permute-done((bf16[64,512]{1,0:T(8,128)(2,1)S(1)}, bf16[64,512]{1,0:T(8,128)(2,1)S(1)}, u32[]{:S(2)}, u32[]{:S(2)}) %collective-permute-start.30) | collective-permute-done | bytes 65568 | tf_op jit(solution)/shard_map/ppermute | solution.py:44
  165.1 2.4 %collective-permute-done.21 = bf16[96,512]{1,0:T(8,128)(2,1)S(1)} collective-permute-done((bf16[96,512]{1,0:T(8,128)(2,1)S(1)}, bf16[96,512]{1,0:T(8,128)(2,1)S(1)}, u32[]{:S(2)}, u32[]{:S(2)}) %collective-permute-start.21) | collective-permute-done | bytes 98336 | tf_op jit(solution)/shard_map/ppermute | solution.py:44
  168.4 2.9 %collective-permute-done.31 = bf16[128,512]{1,0:T(8,128)(2,1)S(1)} collective-permute-done((bf16[128,512]{1,0:T(8,128)(2,1)S(1)}, bf16[128,512]{1,0:T(8,128)(2,1)S(1)}, u32[]{:S(2)}, u32[]{:S(2)}) %collective-permute-start.31) | collective-permute-done | bytes 131104 | tf_op jit(solution)/shard_map/ppermute | solution.py:44
  174.1 1.9 collective-permute-done.13
  176.1 2.1 %collective-permute-start.14 = (bf16[64,1664]{1,0:T(8,128)(2,1)S(1)}, bf16[64,1664]{1,0:T(8,128)(2,1)S(1)}, u32[]{:S(2)}, u32[]{:S(2)}) collective-permute-start(bf16[64,1664]{1,0:T(8,128)(2,1)S(1)} %fusion.3), channel_id=1, source_target_pairs={{0,8},{8,0},{16,24},{24,16},{1,9},{9,1},{17,25},{25,17},{2,10},{10... | collective-permute-start | bytes 638984 | tf_op jit(solution)/shard_map/ppermute | solution.py:44
  178.2 3.5 %collective-permute-done.32 = bf16[256,512]{1,0:T(8,128)(2,1)S(1)} collective-permute-done((bf16[256,512]{1,0:T(8,128)(2,1)S(1)}, bf16[256,512]{1,0:T(8,128)(2,1)S(1)}, u32[]{:S(2)}, u32[]{:S(2)}) %collective-permute-start.32) | collective-permute-done | bytes 262176 | tf_op jit(solution)/shard_map/ppermute | solution.py:44
  183.5 3.1 %collective-permute-start.15 = (bf16[64,1664]{1,0:T(8,128)(2,1)S(1)}, bf16[64,1664]{1,0:T(8,128)(2,1)S(1)}, u32[]{:S(2)}, u32[]{:S(2)}) collective-permute-start(bf16[64,1664]{1,0:T(8,128)(2,1)S(1)} %add_convert_fusion.10), channel_id=1, source_target_pairs={{0,16},{8,24},{16,0},{24,8},{1,17},{9,25},{17,1},{25,9},{2,18},{10... | collective-permute-start | bytes 638984 | tf_op jit(solution)/shard_map/ppermute | solution.py:44
  188.6 4.2 %collective-permute-done.15 = bf16[64,1664]{1,0:T(8,128)(2,1)S(1)} collective-permute-done((bf16[64,1664]{1,0:T(8,128)(2,1)S(1)}, bf16[64,1664]{1,0:T(8,128)(2,1)S(1)}, u32[]{:S(2)}, u32[]{:S(2)}) %collective-permute-start.15) | collective-permute-done | bytes 213024 | tf_op jit(solution)/shard_map/ppermute | solution.py:44
  194.1 4.6 %collective-permute-done.16 = bf16[64,1664]{1,0:T(8,128)(2,1)S(1)} collective-permute-done((bf16[64,1664]{1,0:T(8,128)(2,1)S(1)}, bf16[64,1664]{1,0:T(8,128)(2,1)S(1)}, u32[]{:S(2)}, u32[]{:S(2)}) %collective-permute-start.16) | collective-permute-done | bytes 213024 | tf_op jit(solution)/shard_map/ppermute | solution.py:44
  (134 shorter events, 32.7 us)
Async XLA Ops:
  3.0 12.8 %collective-permute-start.2 = (bf16[128,1664]{1,0:T(8,128)(2,1)S(1)}, bf16[128,1664]{1,0:T(8,128)(2,1)S(1)}, u32[]{:S(2)}, u32[]{:S(2)}) collective-permute-start(bf16[128,1664]{1,0:T(8,128)(2,1)S(1)} %pad_maximum_fusion.1.p0), channel_id=1, source_target_pairs={{0,2},{1,3},{2,0},{3,1},{4,6},{5,7},{6,4},{7,5},{8,10},{9,11},{10,... | collective-permute-start | bytes 1277960 | tf_op jit(solution)/shard_map/ppermute | solution.py:44
  6.1 16.4 %collective-permute-start.1 = (bf16[128,1664]{1,0:T(8,128)(2,1)S(1)}, bf16[128,1664]{1,0:T(8,128)(2,1)}, u32[]{:S(2)}, u32[]{:S(2)}) collective-permute-start(bf16[128,1664]{1,0:T(8,128)(2,1)S(1)} %pad_maximum_fusion.1.p0), channel_id=1, source_target_pairs={{0,1},{1,0},{2,3},{3,2},{4,5},{5,4},{6,7},{7,6},{8,9},{9,8},{10,11... | collective-permute-start | bytes 1277960 | tf_op jit(solution)/shard_map/ppermute | solution.py:44
  6.1 16.4 %collective-permute-start = (bf16[512,512]{1,0:T(8,128)(2,1)}, bf16[512,512]{1,0:T(8,128)(2,1)}, u32[]{:S(2)}, u32[]{:S(2)}) collective-permute-start(bf16[512,512]{1,0:T(8,128)(2,1)} %bitcast.92), channel_id=1, source_target_pairs={{0,4},{4,0},{1,5},{5,1},{2,6},{6,2},{3,7},{7,3},{8,12},{12,8},{9,1... | collective-permute-start | bytes 1572872 | tf_op jit(solution)/shard_map/ppermute | solution.py:44
  15.9 34.3 %collective-permute-start.5 = (bf16[1280,512]{1,0:T(8,128)(2,1)S(1)}, bf16[1280,512]{1,0:T(8,128)(2,1)S(1)}, u32[]{:S(2)}, u32[]{:S(2)}) collective-permute-start(bf16[1280,512]{1,0:T(8,128)(2,1)S(1)} %copy-done.2), channel_id=1, source_target_pairs={{0,2},{1,3},{2,0},{3,1},{4,6},{5,7},{6,4},{7,5},{8,10},{9,11},{10,... | collective-permute-start | bytes 3932168 | tf_op jit(solution)/shard_map/ppermute | solution.py:44
  22.0 28.5 %collective-permute-start.4 = (bf16[1280,512]{1,0:T(8,128)(2,1)S(1)}, bf16[1280,512]{1,0:T(8,128)(2,1)}, u32[]{:S(2)}, u32[]{:S(2)}) collective-permute-start(bf16[1280,512]{1,0:T(8,128)(2,1)S(1)} %copy-done.2), channel_id=1, source_target_pairs={{0,1},{1,0},{2,3},{3,2},{4,5},{5,4},{6,7},{7,6},{8,9},{9,8},{10,11... | collective-permute-start | bytes 3932168 | tf_op jit(solution)/shard_map/ppermute | solution.py:44
  50.2 3.1 %collective-permute-start.6 = (bf16[1280,512]{1,0:T(8,128)(2,1)S(1)}, bf16[1280,512]{1,0:T(8,128)(2,1)S(1)}, u32[]{:S(2)}, u32[]{:S(2)}) collective-permute-start(bf16[1280,512]{1,0:T(8,128)(2,1)S(1)} %collective-permute-done.5.p2), channel_id=1, source_target_pairs={{0,1},{1,0},{2,3},{3,2},{4,5},{5,4},{6,7},{7,6},{8,9},{9,8},{10,11... | collective-permute-start | bytes 3932168 | tf_op jit(solution)/shard_map/ppermute | solution.py:44
  69.4 2.6 %collective-permute-start.7 = (bf16[768,512]{1,0:T(8,128)(2,1)}, bf16[768,512]{1,0:T(8,128)(2,1)S(1)}, u32[]{:S(2)}, u32[]{:S(2)}) collective-permute-start(bf16[768,512]{1,0:T(8,128)(2,1)} %get-tuple-element.67), channel_id=1, source_target_pairs={{0,1},{1,0},{2,3},{3,2},{4,5},{5,4},{6,7},{7,6},{8,9},{9,8},{10,11... | collective-permute-start | bytes 2359304 | tf_op jit(solution)/shard_map/ppermute | solution.py:44
  92.9 2.3 %collective-permute-start.25 = (bf16[512,512]{1,0:T(8,128)(2,1)}, bf16[512,512]{1,0:T(8,128)(2,1)}, u32[]{:S(2)}, u32[]{:S(2)}) collective-permute-start(bf16[512,512]{1,0:T(8,128)(2,1)} %get-tuple-element.94), channel_id=1, source_target_pairs={{0,1},{1,0},{2,3},{3,2},{4,5},{5,4},{6,7},{7,6},{8,9},{9,8},{10,11... | collective-permute-start | bytes 1572872 | tf_op jit(solution)/shard_map/ppermute | solution.py:44
  93.1 3.8 %collective-permute-start.17 = (bf16[768,512]{1,0:T(8,128)(2,1)}, bf16[768,512]{1,0:T(8,128)(2,1)S(1)}, u32[]{:S(2)}, u32[]{:S(2)}) collective-permute-start(bf16[768,512]{1,0:T(8,128)(2,1)} %get-tuple-element.88), channel_id=1, source_target_pairs={{0,1},{1,0},{2,3},{3,2},{4,5},{5,4},{6,7},{7,6},{8,9},{9,8},{10,11... | collective-permute-start | bytes 2359304 | tf_op jit(solution)/shard_map/ppermute | solution.py:44
  93.5 20.4 %collective-permute-start.8 = (bf16[768,512]{1,0:T(8,128)(2,1)S(1)}, bf16[768,512]{1,0:T(8,128)(2,1)S(1)}, u32[]{:S(2)}, u32[]{:S(2)}) collective-permute-start(bf16[768,512]{1,0:T(8,128)(2,1)S(1)} %add_convert_fusion.2), channel_id=1, source_target_pairs={{0,2},{1,3},{2,0},{3,1},{4,6},{5,7},{6,4},{7,5},{8,10},{9,11},{10,... | collective-permute-start | bytes 2359304 | tf_op jit(solution)/shard_map/ppermute | solution.py:44
  93.8 29.5 %collective-permute-start.24 = (bf16[512,512]{1,0:T(8,128)(2,1)}, bf16[512,512]{1,0:T(8,128)(2,1)S(1)}, u32[]{:S(2)}, u32[]{:S(2)}) collective-permute-start(bf16[512,512]{1,0:T(8,128)(2,1)} %get-tuple-element.91), channel_id=1, source_target_pairs={{0,1},{1,0},{2,3},{3,2},{4,5},{5,4},{6,7},{7,6},{8,9},{9,8},{10,11... | collective-permute-start | bytes 1572872 | tf_op jit(solution)/shard_map/ppermute | solution.py:44
  96.5 27.8 %collective-permute-start.26 = (bf16[512,512]{1,0:T(8,128)(2,1)S(1)}, bf16[512,512]{1,0:T(8,128)(2,1)S(1)}, u32[]{:S(2)}, u32[]{:S(2)}) collective-permute-start(bf16[512,512]{1,0:T(8,128)(2,1)S(1)} %add_convert_fusion.4), channel_id=1, source_target_pairs={{0,2},{1,3},{2,0},{3,1},{4,6},{5,7},{6,4},{7,5},{8,10},{9,11},{10,... | collective-permute-start | bytes 1572872 | tf_op jit(solution)/shard_map/ppermute | solution.py:44
  114.2 11.9 %collective-permute-start.18 = (bf16[384,512]{1,0:T(8,128)(2,1)S(1)}, bf16[384,512]{1,0:T(8,128)(2,1)S(1)}, u32[]{:S(2)}, u32[]{:S(2)}) collective-permute-start(bf16[384,512]{1,0:T(8,128)(2,1)S(1)} %dynamic-slice_bitcast_fusion), channel_id=1, source_target_pairs={{0,4},{4,0},{1,5},{5,1},{2,6},{6,2},{3,7},{7,3},{8,12},{12,8},{9,1... | collective-permute-start | bytes 1179656 | tf_op jit(solution)/shard_map/ppermute | solution.py:44
  122.8 5.1 %collective-permute-start.11 = (bf16[128,1664]{1,0:T(8,128)(2,1)}, bf16[128,1664]{1,0:T(8,128)(2,1)S(1)}, u32[]{:S(2)}, u32[]{:S(2)}) collective-permute-start(bf16[128,1664]{1,0:T(8,128)(2,1)} %get-tuple-element.86), channel_id=1, source_target_pairs={{0,1},{1,0},{2,3},{3,2},{4,5},{5,4},{6,7},{7,6},{8,9},{9,8},{10,11... | collective-permute-start | bytes 1277960 | tf_op jit(solution)/shard_map/ppermute | solution.py:44
  122.8 44.8 %collective-permute-start.10 = (bf16[128,1664]{1,0:T(8,128)(2,1)}, bf16[128,1664]{1,0:T(8,128)(2,1)S(1)}, u32[]{:S(2)}, u32[]{:S(2)}) collective-permute-start(bf16[128,1664]{1,0:T(8,128)(2,1)} %get-tuple-element.84), channel_id=1, source_target_pairs={{0,1},{1,0},{2,3},{3,2},{4,5},{5,4},{6,7},{7,6},{8,9},{9,8},{10,11... | collective-permute-start | bytes 1277960 | tf_op jit(solution)/shard_map/ppermute | solution.py:44
  123.3 21.4 %collective-permute-start.9 = (bf16[512,512]{1,0:T(8,128)(2,1)}, bf16[512,512]{1,0:T(8,128)(2,1)S(1)}, u32[]{:S(2)}, u32[]{:S(2)}) collective-permute-start(bf16[512,512]{1,0:T(8,128)(2,1)} %get-tuple-element.82), channel_id=1, source_target_pairs={{0,4},{4,0},{1,5},{5,1},{2,6},{6,2},{3,7},{7,3},{8,12},{12,8},{9,1... | collective-permute-start | bytes 1572872 | tf_op jit(solution)/shard_map/ppermute | solution.py:44
  124.5 18.4 %collective-permute-start.27 = (bf16[256,512]{1,0:T(8,128)(2,1)S(1)}, bf16[256,512]{1,0:T(8,128)(2,1)S(1)}, u32[]{:S(2)}, u32[]{:S(2)}) collective-permute-start(bf16[256,512]{1,0:T(8,128)(2,1)S(1)} %dynamic-slice_bitcast_fusion.1), channel_id=1, source_target_pairs={{0,4},{4,0},{1,5},{5,1},{2,6},{6,2},{3,7},{7,3},{8,12},{12,8},{9,1... | collective-permute-start | bytes 786440 | tf_op jit(solution)/shard_map/ppermute | solution.py:44
  126.2 22.8 %collective-permute-start.19 = (bf16[192,512]{1,0:T(8,128)(2,1)S(1)}, bf16[192,512]{1,0:T(8,128)(2,1)S(1)}, u32[]{:S(2)}, u32[]{:S(2)}) collective-permute-start(bf16[192,512]{1,0:T(8,128)(2,1)S(1)} %dynamic-slice_bitcast_fusion.3), channel_id=1, source_target_pairs={{0,8},{8,0},{16,24},{24,16},{1,9},{9,1},{17,25},{25,17},{2,10},{10... | collective-permute-start | bytes 589832 | tf_op jit(solution)/shard_map/ppermute | solution.py:44
  128.0 39.6 %collective-permute-start.12 = (bf16[128,1664]{1,0:T(8,128)(2,1)S(1)}, bf16[128,1664]{1,0:T(8,128)(2,1)S(1)}, u32[]{:S(2)}, u32[]{:S(2)}) collective-permute-start(bf16[128,1664]{1,0:T(8,128)(2,1)S(1)} %add_convert_fusion.7), channel_id=1, source_target_pairs={{0,2},{1,3},{2,0},{3,1},{4,6},{5,7},{6,4},{7,5},{8,10},{9,11},{10,... | collective-permute-start | bytes 1277960 | tf_op jit(solution)/shard_map/ppermute | solution.py:44
  143.0 6.1 %collective-permute-start.28 = (bf16[128,512]{1,0:T(8,128)(2,1)S(1)}, bf16[128,512]{1,0:T(8,128)(2,1)S(1)}, u32[]{:S(2)}, u32[]{:S(2)}) collective-permute-start(bf16[128,512]{1,0:T(8,128)(2,1)S(1)} %dynamic-slice_bitcast_fusion.4), channel_id=1, source_target_pairs={{0,8},{8,0},{16,24},{24,16},{1,9},{9,1},{17,25},{25,17},{2,10},{10... | collective-permute-start | bytes 393224 | tf_op jit(solution)/shard_map/ppermute | solution.py:44
  149.2 9.4 %collective-permute-start.29 = (bf16[64,512]{1,0:T(8,128)(2,1)S(1)}, bf16[64,512]{1,0:T(8,128)(2,1)S(1)}, u32[]{:S(2)}, u32[]{:S(2)}) collective-permute-start(bf16[64,512]{1,0:T(8,128)(2,1)S(1)} %dynamic-slice_bitcast_fusion.6), channel_id=1, source_target_pairs={{0,16},{8,24},{16,0},{24,8},{1,17},{9,25},{17,1},{25,9},{2,18},{10... | collective-permute-start | bytes 196616 | tf_op jit(solution)/shard_map/ppermute | solution.py:44
  151.8 8.8 %collective-permute-start.20 = (bf16[96,512]{1,0:T(8,128)(2,1)S(1)}, bf16[96,512]{1,0:T(8,128)(2,1)S(1)}, u32[]{:S(2)}, u32[]{:S(2)}) collective-permute-start(bf16[96,512]{1,0:T(8,128)(2,1)S(1)} %dynamic-slice_bitcast_fusion.5), channel_id=1, source_target_pairs={{0,16},{8,24},{16,0},{24,8},{1,17},{9,25},{17,1},{25,9},{2,18},{10... | collective-permute-start | bytes 294920 | tf_op jit(solution)/shard_map/ppermute | solution.py:44
  158.6 6.3 %collective-permute-start.30 = (bf16[64,512]{1,0:T(8,128)(2,1)S(1)}, bf16[64,512]{1,0:T(8,128)(2,1)S(1)}, u32[]{:S(2)}, u32[]{:S(2)}) collective-permute-start(bf16[64,512]{1,0:T(8,128)(2,1)S(1)} %fusion.8), channel_id=1, source_target_pairs={{0,16},{8,24},{16,0},{24,8},{1,17},{9,25},{17,1},{25,9},{2,18},{10... | collective-permute-start | bytes 196616 | tf_op jit(solution)/shard_map/ppermute | solution.py:44
  160.7 6.7 %collective-permute-start.21 = (bf16[96,512]{1,0:T(8,128)(2,1)S(1)}, bf16[96,512]{1,0:T(8,128)(2,1)S(1)}, u32[]{:S(2)}, u32[]{:S(2)}) collective-permute-start(bf16[96,512]{1,0:T(8,128)(2,1)S(1)} %fusion.7), channel_id=1, source_target_pairs={{0,16},{8,24},{16,0},{24,8},{1,17},{9,25},{17,1},{25,9},{2,18},{10... | collective-permute-start | bytes 294920 | tf_op jit(solution)/shard_map/ppermute | solution.py:44
  165.0 6.3 %collective-permute-start.31 = (bf16[128,512]{1,0:T(8,128)(2,1)S(1)}, bf16[128,512]{1,0:T(8,128)(2,1)S(1)}, u32[]{:S(2)}, u32[]{:S(2)}) collective-permute-start(bf16[128,512]{1,0:T(8,128)(2,1)S(1)} %pad_maximum_fusion.6), channel_id=1, source_target_pairs={{0,8},{8,0},{16,24},{24,16},{1,9},{9,1},{17,25},{25,17},{2,10},{10... | collective-permute-start | bytes 393224 | tf_op jit(solution)/shard_map/ppermute | solution.py:44
  167.5 5.9 %collective-permute-start.22 = (bf16[192,512]{1,0:T(8,128)(2,1)S(1)}, bf16[192,512]{1,0:T(8,128)(2,1)S(1)}, u32[]{:S(2)}, u32[]{:S(2)}) collective-permute-start(bf16[192,512]{1,0:T(8,128)(2,1)S(1)} %pad_maximum_fusion.5), channel_id=1, source_target_pairs={{0,8},{8,0},{16,24},{24,16},{1,9},{9,1},{17,25},{25,17},{2,10},{10... | collective-permute-start | bytes 589832 | tf_op jit(solution)/shard_map/ppermute | solution.py:44
  167.8 8.3 %collective-permute-start.13 = (bf16[64,1664]{1,0:T(8,128)(2,1)S(1)}, bf16[64,1664]{1,0:T(8,128)(2,1)S(1)}, u32[]{:S(2)}, u32[]{:S(2)}) collective-permute-start(bf16[64,1664]{1,0:T(8,128)(2,1)S(1)} %dynamic-slice_bitcast_fusion.2), channel_id=1, source_target_pairs={{0,4},{4,0},{1,5},{5,1},{2,6},{6,2},{3,7},{7,3},{8,12},{12,8},{9,1... | collective-permute-start | bytes 638984 | tf_op jit(solution)/shard_map/ppermute | solution.py:44
  171.4 10.3 %collective-permute-start.32 = (bf16[256,512]{1,0:T(8,128)(2,1)S(1)}, bf16[256,512]{1,0:T(8,128)(2,1)S(1)}, u32[]{:S(2)}, u32[]{:S(2)}) collective-permute-start(bf16[256,512]{1,0:T(8,128)(2,1)S(1)} %pad_maximum_fusion.4), channel_id=1, source_target_pairs={{0,4},{4,0},{1,5},{5,1},{2,6},{6,2},{3,7},{7,3},{8,12},{12,8},{9,1... | collective-permute-start | bytes 786440 | tf_op jit(solution)/shard_map/ppermute | solution.py:44
  173.6 13.8 %collective-permute-start.23 = (bf16[384,512]{1,0:T(8,128)(2,1)S(1)}, bf16[384,512]{1,0:T(8,128)(2,1)S(1)}, u32[]{:S(2)}, u32[]{:S(2)}) collective-permute-start(bf16[384,512]{1,0:T(8,128)(2,1)S(1)} %pad_maximum_fusion.3), channel_id=1, source_target_pairs={{0,4},{4,0},{1,5},{5,1},{2,6},{6,2},{3,7},{7,3},{8,12},{12,8},{9,1... | collective-permute-start | bytes 1179656 | tf_op jit(solution)/shard_map/ppermute | solution.py:44
  176.1 7.3 %collective-permute-start.14 = (bf16[64,1664]{1,0:T(8,128)(2,1)S(1)}, bf16[64,1664]{1,0:T(8,128)(2,1)S(1)}, u32[]{:S(2)}, u32[]{:S(2)}) collective-permute-start(bf16[64,1664]{1,0:T(8,128)(2,1)S(1)} %fusion.3), channel_id=1, source_target_pairs={{0,8},{8,0},{16,24},{24,16},{1,9},{9,1},{17,25},{25,17},{2,10},{10... | collective-permute-start | bytes 638984 | tf_op jit(solution)/shard_map/ppermute | solution.py:44
  183.5 9.2 %collective-permute-start.15 = (bf16[64,1664]{1,0:T(8,128)(2,1)S(1)}, bf16[64,1664]{1,0:T(8,128)(2,1)S(1)}, u32[]{:S(2)}, u32[]{:S(2)}) collective-permute-start(bf16[64,1664]{1,0:T(8,128)(2,1)S(1)} %add_convert_fusion.10), channel_id=1, source_target_pairs={{0,16},{8,24},{16,0},{24,8},{1,17},{9,25},{17,1},{25,9},{2,18},{10... | collective-permute-start | bytes 638984 | tf_op jit(solution)/shard_map/ppermute | solution.py:44
  192.8 5.9 %collective-permute-start.16 = (bf16[64,1664]{1,0:T(8,128)(2,1)S(1)}, bf16[64,1664]{1,0:T(8,128)(2,1)S(1)}, u32[]{:S(2)}, u32[]{:S(2)}) collective-permute-start(bf16[64,1664]{1,0:T(8,128)(2,1)S(1)} %add_convert_fusion.9), channel_id=1, source_target_pairs={{0,4},{4,0},{1,5},{5,1},{2,6},{6,2},{3,7},{7,3},{8,12},{12,8},{9,1... | collective-permute-start | bytes 638984 | tf_op jit(solution)/shard_map/ppermute | solution.py:44
  (16 other events, 122.4 us)
where the time goes:
time: 202 us; the launch traced here: 201 us
  waiting for transfers between devices  75.1 us (37%)
  Pallas kernels  74.6 us (37%)
  starting transfers between devices  28.1 us (14%)
  other arithmetic  19.6 us (10%)
  local copies, waits for them, and re-layouts  2.92 us (1%)
    ppermute x33, waiting for transfers between devices, swap(): return lax.ppermute(value, axis, [(i, i ^ bit) for i in range(size)])  75.1 us
    ppermute x33, starting transfers between devices, swap(): return lax.ppermute(value, axis, [(i, i ^ bit) for i in range(size)])  28.1 us
    pallas_call x1, Pallas kernels, attend_forward(): pl.pallas_call(functools.partial(forward_body, rows), grid=(pairs, row_co...  19.7 us
    pallas_call x1, Pallas kernels, attend_backward(): pl.pallas_call(functools.partial(backward_body, several, 256), grid=(pair...  19.6 us
    pallas_call x1, Pallas kernels, middle(): pl.pallas_call(middle_body, in_specs=[scalar()] + [vmem] * 5 + [in_place(...  15 us
    pallas_call x1, Pallas kernels, last(): pl.pallas_call(last_body, in_specs=[scalar()] + [vmem] * 7, out_specs=[vm...  6.98 us
    pallas_call x1, Pallas kernels, project(): pl.pallas_call(project_body, grid=(steps,), in_specs=[scalar(), pl.BlockS...  6.62 us
  transfers between devices with their start and end apart: 33, of which 19 were waited for; matrix products, arithmetic and copies ran while one was open for 7% of the time, Pallas kernels for 20%

commit v1 on v0

--- a/solution.py
+++ b/solution.py
@@ -59,6 +59,35 @@
 
 def hold(value, *before):
     return lax.optimization_barrier((value,) + before)[0]
+
+
+class Order:
+    def __init__(self):
+        self.before = ()
+
+    def arrive(self, *values):
+        held = lax.optimization_barrier(values + self.before)[: len(values)]
+        self.before = held[:1]
+        return held if len(held) > 1 else held[0]
+
+
+def send_half(part, axis, bit):
+    side = side_of(axis, bit)
+    both = part.reshape((2, part.shape[0] // 2) + part.shape[1:])
+    got = swap(lax.dynamic_index_in_dim(both, 1 - side, 0, False), axis, bit)
+    return lax.dynamic_index_in_dim(both, side, 0, False), got
+
+
+def place_half(part, other, axis, bit):
+    high = side_of(axis, bit) == 1
+    return jnp.concatenate([jnp.where(high, other, part), jnp.where(high, part, other)], axis=0)
+
+
+def add_all(own, got):
+    total = own.astype(F32)
+    for value in got:
+        total = total + value.astype(F32)
+    return total.astype(BF16)
 
 
 def add_low(left, right):
@@ -269,7 +298,7 @@
 
 
 def middle_body(
-    me_ref, small_ref, tokens_ref, cot_ref, o_ref, m_ref, p0, p1, p2, p3,
+    slices, me_ref, small_ref, tokens_ref, cot_ref, o_ref, m_ref, p0, p1, p2, p3,
     out_ref, gh1_ref, go_ref, gm_ref, gate_ref, g0, g1, g2, g3, h0, h1_ref, h2_ref, h3,
     w_out, w_memory, w_down, w_up, act, slope, gu, a2_turned, o_turned, m_turned, sem,
 ):
@@ -339,21 +368,28 @@
     for r, (grad_ref, up_ref) in enumerate(((g0, h0), (g1, h1_ref), (g2, h2_ref), (g3, h3))):
         device = me_ref[0] ^ r
         place = pl.ds(pl.multiple_of(device * shard, shard), shard)
-        grad_ref[0:shard, :] = product(o_turned[place, :], ga).astype(BF16)
-        grad_ref[shard : 2 * shard, :] = product(m_turned[place, :], grad_mem).astype(BF16)
-        grad_ref[2 * shard : 2 * shard + width, :] = product(act[device], gf).astype(BF16)
-        for group in range(groups):
-            first = group * shard
-            up_ref[first : first + shard, :] = product(a2_turned[place, :], gu[group]).astype(BF16)
-
-
-def middle(me, small, tokens, cotangent, o, m, packs, groups):
+        parts = [product(o_turned[place, :], ga), product(m_turned[place, :], grad_mem), product(act[device], gf)]
+        lay_slices(grad_ref, slices, [part.astype(BF16) for part in parts])
+        parts = [product(a2_turned[place, :], gu[group]) for group in range(groups)]
+        lay_slices(up_ref, slices, [part.astype(BF16) for part in parts])
+
+
+def lay_slices(target, slices, parts):
+    first = 0
+    for n in range(slices):
+        for part in parts:
+            height = part.shape[0] // slices
+            target[first : first + height, :] = part[n * height : (n + 1) * height, :]
+            first += height
+
+
+def middle(slices, me, small, tokens, cotangent, o, m, packs, groups):
     rows, width = tokens.shape
     shard = width // 4
     vmem = pl.BlockSpec(memory_space=pltpu.VMEM)
     square = lambda dtype: pltpu.VMEM((width, width), dtype)
     return pl.pallas_call(
-        middle_body,
+        functools.partial(middle_body, slices),
         in_specs=[scalar()] + [vmem] * 5 + [in_place()] * 4,
         out_specs=[vmem] * 13,
         out_shape=[
@@ -474,25 +510,17 @@
     )(q, k, v, go, gm, o, m, r1, r2, bias, e1, e2)
 
 
-def last_body(me_ref, turned_ref, gq_ref, gk_ref, gv_ref, w_ref, gs_ref, gate_ref, near_ref, own_ref, g0, g1, g2, g3):
+def weights_body(me_ref, turned_ref, gq_ref, gk_ref, gv_ref, gs_ref, gate_ref, *grad_refs):
     rows, width = gq_ref.shape
     shard = width // 4
-    gq = gq_ref[...].astype(BF16)
-    w_q = w_ref[:, 0:width]
-    w_k = w_ref[:, width : 2 * width]
-    w_v = w_ref[:, 2 * width : 3 * width]
-    for first in range(rows, gk_ref.shape[0], rows):
-        at = slice(first, first + rows)
-        part = product(gk_ref[at, :], w_k, NT) + product(gv_ref[at, :], w_v, NT)
-        near_ref[first - rows : first, :] = part.astype(BF16)
-    own_ref[...] = product(gq, w_q, NT) + product(gk_ref[0:rows, :], w_k, NT) + product(gv_ref[0:rows, :], w_v, NT)
     lane = lax.broadcasted_iota(jnp.int32, (16, shard), 1)
     row = lax.broadcasted_iota(jnp.int32, (16, shard), 0)
-    for r, grad_ref in enumerate((g0, g1, g2, g3)):
+    for r in range(4):
+        grad_ref = grad_refs[r]
         device = me_ref[0] ^ r
         start = pl.multiple_of(device * shard, shard)
         a1 = turned_ref[pl.ds(start, shard), :]
-        grad_ref[:, 0:width] = product(a1[:, 0:rows], gq).astype(BF16)
+        grad_ref[:, 0:width] = product(a1[:, 0:rows], gq_ref[...].astype(BF16)).astype(BF16)
         grad_ref[:, width : 2 * width] = product(a1, gk_ref[...]).astype(BF16)
         grad_ref[:, 2 * width : 3 * width] = product(a1, gv_ref[...]).astype(BF16)
         sums = -jnp.sum(gs_ref[device, 0:2, :], axis=1, keepdims=True)
@@ -503,22 +531,123 @@
         grad_ref[0:16, 3 * width : 3 * width + shard] = block.astype(BF16)
 
 
-def last(me, turned, gq, gk, gv, w, gs, gate):
+def weight_grads(me, turned, gq, gk, gv, gs, gate):
     rows, width = gq.shape
     shard = width // 4
     vmem = pl.BlockSpec(memory_space=pltpu.VMEM)
     return pl.pallas_call(
-        last_body,
-        in_specs=[scalar()] + [vmem] * 7,
-        out_specs=[vmem] * 6,
-        out_shape=[like((gk.shape[0] - rows, width), BF16), like((rows, width), F32)]
-        + [like((shard, 3 * width + shard), BF16)] * 4,
+        weights_body,
+        in_specs=[scalar()] + [vmem] * 6,
+        out_specs=[vmem] * 4,
+        out_shape=[like((shard, 3 * width + shard), BF16)] * 4,
         compiler_params=params(),
         cost_estimate=pl.CostEstimate(
-            flops=12 * gk.shape[0] * width * width, transcendentals=0, bytes_accessed=10000000
+            flops=6 * gk.shape[0] * width * width, transcendentals=0, bytes_accessed=6000000
         ),
-        name="last",
-    )(me, turned, gq, gk, gv, w, gs, gate)
+        name="weight_grads",
+    )(me, turned, gq, gk, gv, gs, gate)
+
+
+def rows_body(gq_ref, gk_ref, gv_ref, w_ref, near_ref, own_ref):
+    rows, width = gq_ref.shape
+    w_k = w_ref[:, width : 2 * width]
+    w_v = w_ref[:, 2 * width : 3 * width]
+    for first in range(rows, gk_ref.shape[0], rows):
+        at = slice(first, first + rows)
+        part = product(gk_ref[at, :], w_k, NT) + product(gv_ref[at, :], w_v, NT)
+        near_ref[first - rows : first, :] = part.astype(BF16)
+    own = product(gq_ref[...].astype(BF16), w_ref[:, 0:width], NT)
+    own_ref[...] = own + product(gk_ref[0:rows, :], w_k, NT) + product(gv_ref[0:rows, :], w_v, NT)
+
+
+def row_grads(gq, gk, gv, w):
+    rows, width = gq.shape
+    vmem = pl.BlockSpec(memory_space=pltpu.VMEM)
+    return pl.pallas_call(
+        rows_body,
+        in_specs=[vmem] * 4,
+        out_specs=[vmem] * 2,
+        out_shape=[like((gk.shape[0] - rows, width), BF16), like((rows, width), F32)],
+        compiler_params=params(),
+        cost_estimate=pl.CostEstimate(
+            flops=6 * gk.shape[0] * width * width, transcendentals=0, bytes_accessed=6000000
+        ),
+        name="row_grads",
+    )(gq, gk, gv, w)
+
+
+def row_sums(table, weight_ref, gain_ref):
+    ones = jnp.ones((8, table.shape[1]), F32)
+    sums = lax.dot_general(
+        ones, table * weight_ref[...].astype(F32), NT, precision=lax.Precision.HIGHEST, preferred_element_type=F32
+    )
+    return sums[0:1, :] / gain_ref[...].astype(F32)
+
+
+def assemble_body(
+    near_ref, far_ref, own_a, own_b, other_a, other_b, up_w_ref, gain_ref, out_ref, memory_ref, down_ref, up_ref, sum_ref
+):
+    width = out_ref.shape[1]
+    groups = up_ref.shape[1] // width
+    short = out_ref.shape[0] // 8
+    tall = down_ref.shape[0] // 8
+    size = own_a.shape[0] // 2
+    for n, part_ref in enumerate((own_a, own_b, other_a, other_b)):
+        side = near_ref[0] if n < 2 else 1 - near_ref[0]
+        pair = far_ref[0] if n % 2 == 0 else 1 - far_ref[0]
+        for p in range(2):
+            place = 4 * side + 2 * pair + p
+            at = pl.ds(pl.multiple_of(place * short, short), short)
+            piece = part_ref[p * size : (p + 1) * size, :].astype(F32)
+            out_ref[at, :] = piece[0:short, :]
+            memory_ref[at, :] = piece[short : 2 * short, :]
+            down_ref[pl.ds(pl.multiple_of(place * tall, tall), tall), :] = piece[2 * short : 2 * short + tall, :]
+            for group in range(groups):
+                first = 2 * short + tall + group * short
+                up_ref[at, group * width : (group + 1) * width] = piece[first : first + short, :]
+    sum_ref[...] = row_sums(up_ref[...], up_w_ref, gain_ref)
+
+
+def assemble(near, far, parts, w_up, gain):
+    width = parts[0].shape[1]
+    shard, columns = w_up.shape
+    vmem = pl.BlockSpec(memory_space=pltpu.VMEM)
+    return pl.pallas_call(
+        assemble_body,
+        in_specs=[scalar(), scalar()] + [vmem] * 6,
+        out_specs=[vmem] * 5,
+        out_shape=[like((shard, width), F32)] * 2
+        + [like((width, width), F32), like((shard, columns), F32), like((1, shard), F32)],
+        compiler_params=params(),
+        cost_estimate=pl.CostEstimate(flops=0, transcendentals=0, bytes_accessed=4000000),
+        name="assemble",
+    )(near, far, *parts, w_up, gain[None])
+
+
+def close_body(near_ref, own_ref, other_ref, w_ref, gain_ref, qkv_ref, gain_sum_ref, gate_ref, slope_ref):
+    half = own_ref.shape[0]
+    wide = qkv_ref.shape[1]
+    for n, part_ref in enumerate((own_ref, other_ref)):
+        side = near_ref[0] if n == 0 else 1 - near_ref[0]
+        qkv_ref[pl.ds(pl.multiple_of(side * half, half), half), :] = part_ref[:, 0:wide].astype(F32)
+    first = jnp.where(near_ref[0] == 0, own_ref[0:16, wide:].astype(F32), other_ref[0:16, wide:].astype(F32))
+    slope_ref[...] = first[0:1, 0 : slope_ref.shape[1]]
+    gate_ref[...] = first[1:2, :]
+    gain_sum_ref[...] = row_sums(qkv_ref[...], w_ref, gain_ref)
+
+
+def close(near, own, other, w_qkv, gain, heads):
+    shard, wide = w_qkv.shape
+    vmem = pl.BlockSpec(memory_space=pltpu.VMEM)
+    return pl.pallas_call(
+        close_body,
+        in_specs=[scalar()] + [vmem] * 4,
+        out_specs=[vmem] * 4,
+        out_shape=[like((shard, wide), F32), like((1, shard), F32), like((1, shard), F32), like((1, heads), F32)],
+        compiler_params=params(),
+        cost_estimate=pl.CostEstimate(flops=0, transcendentals=0, bytes_accessed=2000000),
+        name="close",
+    )(near, own, other, w_qkv, gain[None])
 
 
 def finish_body(tokens_ref, small_ref, gh1_ref, own_ref, away_ref, out_ref):
@@ -556,18 +685,21 @@
     heads_here = slopes.shape[0]
     groups = w_up.shape[1] // width
     me = lax.axis_index("wt").astype(jnp.int32).reshape(1)
+    fast = ctx_size == 2 and lax.axis_size("seq") == 4
+    slices = 8 if fast else 1
 
     short = jnp.concatenate(
         [gain_attn[None], gain_ffn[None], gate_vec[None], jnp.pad(slopes, (0, shard - heads_here))[None]], axis=0
     )
     pack = jnp.concatenate([w_qkv, jnp.pad(short, ((0, shard - 4), (0, 0)))], axis=1)
-    pack_far = swap(pack, "wt", 2)
     others = swap(tokens, "ctx", 1)
     for bit in bits_of("ctx")[1:]:
         both = jnp.concatenate([tokens, others], axis=0)
         others = jnp.concatenate([others, swap(both, "ctx", bit)], axis=0)
+    pack_far = swap(pack, "wt", 2)
     pack_near = swap(pack, "wt", 1)
     wide = lay_rows(width, [(w_out, 0), (w_memory, 0)] + [(w_up, width * g) for g in range(groups)] + [(w_down, 0)])
+    neighbours = hold(neighbours, wide)
 
     offsets = jnp.arange(block_len, dtype=jnp.int32)
     owners = lax.axis_index("ctx") ^ jnp.arange(ctx_size, dtype=jnp.int32)
@@ -582,59 +714,113 @@
     my_memory = jnp.sum(memory_hot * memory_len, axis=1)
     row_start = jnp.repeat(my_blocks * block_len, block_len)
     row_low = row_start - jnp.repeat(my_memory, block_len)
+    hits = jnp.sum((neighbours[:, :, None] == key_pos[None, None, :]).astype(F32), axis=1)
+    count = jnp.where(hits > 0.0, jnp.log(jnp.maximum(hits, 1.0)), ABSENT)
+    pack_far, wide = lax.optimization_barrier((pack_far, wide, count))[:2]
+    pack_both = swap(pack_far, "wt", 1)
+    wide_far = swap(wide, "wt", 2)
+    wide_near = swap(wide, "wt", 1)
+    row_pos = hold(row_pos, pack_far)
     distance = jnp.log1p(jnp.abs(row_pos[:, None] - key_pos[None, :]).astype(F32))
     visible = (key_pos[None, :] >= row_low[:, None]) & (key_pos[None, :] < (row_start + block_len)[:, None])
     bias = jnp.where(visible, distance, HIDDEN)
-    hits = jnp.sum((neighbours[:, :, None] == key_pos[None, None, :]).astype(F32), axis=1)
-    count = jnp.where(hits > 0.0, jnp.log(jnp.maximum(hits, 1.0)), ABSENT)
-
-    pack_both = swap(hold(pack_far, bias, count), "wt", 1)
-    wide_far = swap(hold(wide, pack_far), "wt", 2)
-    wide_near = swap(wide, "wt", 1)
-
-    q, k, v, turned, full_qkv, small = project(me, tokens, others, (pack, pack_near, pack_far, pack_both))
+
+    q, k, v, turned, full_qkv, small = project(
+        me, tokens, hold(others, bias), (pack, pack_near, pack_far, pack_both)
+    )
     saved = attend_forward(small, q, k, v, bias, count)
     wide_both = swap(hold(wide_far, saved[0]), "wt", 1)
     wides = (wide, wide_near, wide_far, wide_both)
     layer_out, gh1, go, gm, gate, g0, g1, g2, g3, h0, h1, h2, h3 = middle(
-        me, small, tokens, cotangent, saved[0], saved[1], wides, groups
+        slices, me, small, tokens, cotangent, saved[0], saved[1], wides, groups
     )
 
+    all_pairs = width // 128
     g_far = add_low(g2, swap(g3, "wt", 1))
     g_one = swap(g1, "wt", 1)
-    g_got = swap(g_far, "wt", 2)
-    gq, gk, gv, gs = attend_backward(q, k, v, hold(go, g_far), gm, saved, bias, 0, width // 128)
-    g_sum = add_low(add_low(g0, g_one), g_got)
-    h1, h3 = (hold(value, gq) for value in (h1, h3))
-    h_far = add_low(h2, swap(h3, "wt", 1))
-    h_one = swap(h1, "wt", 1)
-    h_got = swap(h_far, "wt", 2)
-    near, own, q0, q1, q2, q3 = last(me, turned, hold(gq, g_got), gk, gv, full_qkv, gs, gate)
-    h_sum = add_low(add_low(h0, h_one), h_got)
-    q_three = swap(q3, "wt", 1)
-    q_one = swap(q1, "wt", 1)
-    for bit in reversed(bits_of("ctx")[1:]):
-        both = jnp.concatenate([own.astype(BF16), near], axis=0)
-        fold = bit * row_count
-        folded = both[:fold].astype(F32) + swap(both[fold:], "ctx", bit).astype(F32)
-        own, near = folded[:row_count], folded[row_count:].astype(BF16)
-    away = swap(near, "ctx", 1)
-    q_far = swap(add_low(q2, q_three), "wt", 2)
-    q_sum = add_low(add_low(q0, q_one), q_far)
-    q_sum = near_whole(far_both(near_halves(q_sum)))
-    g_sum = near_whole(far_whole(far_halves(near_halves(g_sum))))
-    h_sum = near_whole(far_whole(far_halves(near_halves(h_sum))))
-    grad_tokens = finish(tokens, small, gh1, own, away)
-
-    t_qkv = q_sum[:, : 3 * width].astype(F32)
-    t_slopes = q_sum[0, 3 * width : 3 * width + heads_here].astype(F32)
-    t_gate = q_sum[1, 3 * width : 3 * width + shard].astype(F32)
-    t_out = g_sum[:shard].astype(F32)
-    t_memory = g_sum[shard : 2 * shard].astype(F32)
-    t_down = g_sum[2 * shard : 2 * shard + width].astype(F32)
-    t_up = jnp.concatenate([h_sum[shard * g : shard * (g + 1)] for g in range(groups)], axis=1).astype(F32)
-    t_gain_one = jnp.sum(t_qkv * w_qkv.astype(F32), axis=1) / gain_attn.astype(F32)
-    t_gain_two = jnp.sum(t_up * w_up.astype(F32), axis=1) / gain_ffn.astype(F32)
+    if fast:
+        h_far = add_low(h2, swap(h3, "wt", 1))
+        h_own = add_low(h0, swap(h1, "wt", 1))
+        g_got = swap(g_far, "wt", 2)
+        far_keep, far_got = send_half(h_far, "ctx", 1)
+        own_keep, own_got = send_half(h_own, "ctx", 1)
+        gq, gk, gv, gs = attend_backward(q, k, v, hold(go, g_far, h_far, h_own), gm, saved, bias, 0, all_pairs)
+        gq, gk, gv, gs, g_got, far_got, own_got = lax.optimization_barrier(
+            (gq, gk, gv, gs, g_got, far_got, own_got)
+        )
+        h_got = swap(add_low(far_keep, far_got), "wt", 2)
+        g_keep, g_near = send_half(add_all(g0, [g_one, g_got]), "ctx", 1)
+        q0, q1, q2, q3 = weight_grads(me, turned, hold(gq, g_keep), gk, gv, gs, gate)
+        q_three, q_one = swap(q3, "wt", 1), swap(q1, "wt", 1)
+        gq, q0, q2, g_near, h_got = lax.optimization_barrier((gq, q0, q2, g_near, h_got))
+        q_far = add_low(q2, q_three)
+        lower = add_low(g_keep, g_near).reshape(4, -1, width)
+        higher = add_all(own_keep, [own_got, h_got]).reshape(4, -1, width)
+        gh_keep, gh_got = send_half(jnp.concatenate([lower, higher], axis=1).reshape(-1, width), "seq", 1)
+        near, own = row_grads(hold(gq, q_far, gh_keep), gk, gv, full_qkv)
+        q_far = swap(q_far, "wt", 2)
+        order = Order()
+        near, gh_got = order.arrive(near, gh_got)
+        gh = add_low(gh_keep, gh_got)
+        gh_keep, gh_got = send_half(gh, "seq", 2)
+        q_keep, q_got = send_half(add_all(q0, [q_one, order.arrive(q_far)]), "ctx", 1)
+        gh = add_low(gh_keep, order.arrive(gh_got))
+        gh_other = swap(gh, "seq", 2)
+        q_sum = add_low(q_keep, order.arrive(q_got))
+        q_got = swap(q_sum, "seq", 1)
+        away = swap(hold(near, q_sum), "ctx", 1)
+        own_a = place_half(gh, order.arrive(gh_other), "seq", 2)
+        own_b = swap(own_a, "seq", 1)
+        q_sum = add_low(q_sum, order.arrive(q_got))
+        q_got = swap(q_sum, "seq", 2)
+        away = order.arrive(away)
+        other_a = swap(hold(own_a, away), "ctx", 1)
+        grad_tokens = finish(tokens, small, gh1, own, away)
+        order.before = (grad_tokens,)
+        own_b = order.arrive(own_b)
+        other_b = swap(own_b, "ctx", 1)
+        q_sum = add_low(q_sum, order.arrive(q_got))
+        q_other = swap(q_sum, "ctx", 1)
+        side = lax.axis_index("ctx").astype(jnp.int32).reshape(1)
+        pair = side_of("seq", 1).astype(jnp.int32).reshape(1)
+        other_a, other_b = order.arrive(other_a, other_b)
+        t_out, t_memory, t_down, t_up, t_gain_two = assemble(
+            side, pair, (own_a, own_b, other_a, other_b), w_up, gain_ffn
+        )
+        order.before = (t_gain_two,)
+        t_qkv, *shorts = close(side, q_sum, order.arrive(q_other), w_qkv, gain_attn, heads_here)
+        t_gain_one, t_gate, t_slopes, t_gain_two = (value.reshape(-1) for value in (*shorts, t_gain_two))
+    else:
+        h_far = add_low(h2, swap(h3, "wt", 1))
+        h_one = swap(h1, "wt", 1)
+        g_sum = add_all(g0, [g_one, swap(g_far, "wt", 2)])
+        h_sum = add_all(h0, [h_one, swap(h_far, "wt", 2)])
+        gq, gk, gv, gs = attend_backward(q, k, v, go, gm, saved, bias, 0, all_pairs)
+        grads = weight_grads(me, turned, gq, gk, gv, gs, gate)
+        near, own = row_grads(gq, gk, gv, full_qkv)
+        for bit in reversed(bits_of("ctx")[1:]):
+            both = jnp.concatenate([own.astype(BF16), near], axis=0)
+            fold = bit * row_count
+            folded = both[:fold].astype(F32) + swap(both[fold:], "ctx", bit).astype(F32)
+            own, near = folded[:row_count], folded[row_count:].astype(BF16)
+        away = swap(near, "ctx", 1)
+        q_far = swap(add_low(grads[2], swap(grads[3], "wt", 1)), "wt", 2)
+        q_sum = add_all(grads[0], [swap(grads[1], "wt", 1), q_far])
+        q_sum = near_whole(far_both(near_halves(q_sum)))
+        g_sum = near_whole(far_whole(far_halves(near_halves(g_sum))))
+        h_sum = near_whole(far_whole(far_halves(near_halves(h_sum))))
+        grad_tokens = finish(tokens, small, gh1, own, away)
+        t_out = g_sum[:shard].astype(F32)
+        t_memory = g_sum[shard : 2 * shard].astype(F32)
+        t_down = g_sum[2 * shard : 2 * shard + width].astype(F32)
+        t_up = jnp.concatenate([h_sum[shard * g : shard * (g + 1)] for g in range(groups)], axis=1).astype(F32)
+        t_qkv = q_sum[:, : 3 * width].astype(F32)
+        t_slopes = q_sum[0, 3 * width : 3 * width + heads_here].astype(F32)
+        t_gate = q_sum[1, 3 * width : 3 * width + shard].astype(F32)
+        t_gain_one = jnp.sum(t_qkv * w_qkv.astype(F32), axis=1) / gain_attn.astype(F32)
+        t_gain_two = jnp.sum(t_up * w_up.astype(F32), axis=1) / gain_ffn.astype(F32)
+
+
     return (
         layer_out[None], grad_tokens[None], t_qkv, t_out, t_up, t_down, t_memory,
         t_gain_one, t_gain_two, t_gate, t_slopes,

time: 202 us -> 168 us (0.83)
  the two profiles are of different devices: /device:TPU:0 before, /device:TPU:28 now
where the time goes in v1:
time: 168 us; the launch traced here: 167 us
  Pallas kernels  83.4 us (50%)
  waiting for transfers between devices  45.8 us (27%)
  starting transfers between devices  21.9 us (13%)
  other arithmetic  11.2 us (7%)
  local copies, waits for them, and re-layouts  3.79 us (2%)
    ppermute x30, waiting for transfers between devices, swap(): return lax.ppermute(value, axis, [(i, i ^ bit) for i in range(size)])  45.8 us
    ppermute x30, starting transfers between devices, swap(): return lax.ppermute(value, axis, [(i, i ^ bit) for i in range(size)])  21.9 us
    pallas_call x1, Pallas kernels, attend_forward(): pl.pallas_call(functools.partial(forward_body, rows), grid=(pairs, row_co...  19.7 us
    pallas_call x1, Pallas kernels, attend_backward(): pl.pallas_call(functools.partial(backward_body, several, 256), grid=(pair...  19.6 us
    pallas_call x1, Pallas kernels, middle(): pl.pallas_call(functools.partial(middle_body, slices), in_specs=[scalar()...  15.1 us
    pallas_call x1, Pallas kernels, project(): pl.pallas_call(project_body, grid=(steps,), in_specs=[scalar(), pl.BlockS...  6.65 us
    pallas_call x1, Pallas kernels, row_grads(): pl.pallas_call(rows_body, in_specs=[vmem] * 4, out_specs=[vmem] * 2, out_...  4.77 us
    pallas_call x1, Pallas kernels, weight_grads(): pl.pallas_call(weights_body, in_specs=[scalar()] + [vmem] * 6, out_specs=...  4.62 us
  transfers between devices with their start and end apart: 30, of which 12 were waited for; matrix products, arithmetic and copies ran while one was open for 6% of the time, Pallas kernels for 39%

profile of v1, /device:TPU:28, one launch (start us, length us, event | category | flops | bytes accessed | tf_op | source)
XLA Modules:
  0.0 167.2 jit_solution(5316445419054748355)
XLA Ops:
  3.6 1.5 collective-permute-start
  6.2 3.2 %lay_rows.1.p0 = bf16[1280,512]{1,0:T(8,128)(2,1)} custom-call(bf16[128,512]{1,0:T(8,128)(2,1)} %refs_0_.1, bf16[128,512]{1,0:T(8,128)(2,1)} %refs_1_.1, bf16[128,2048]{1,0:T(8,128)(2,1)} %up_w_ref.1, bf16[128,2048]{1,0:T(8,128)(2,1)} %up_w_ref.1, bf16[128,2048]{1,0:T(8,128)(2,1)} %up_w_ref.1, bf16[128,2048]{1,0:T(8,128)(2,1)} %up_w_ref.1, ...), custom_call_target="tpu_custom_call" | custom-call | bytes 2621440 | tf_op jit(solution)/shard_map/lay_rows/pallas_call | solution.py:162
  9.4 1.1 convert_reduce_fusion
  10.6 1.7 %log_select_fusion.c_ref = f32[512,1024]{1,0:T(8,128)} fusion(f32[512,1024]{1,0:T(8,128)S(1)} %convert_reduce_fusion), kind=kLoop, calls=%fused_computation.2 | loop fusion | flops 1572864 | bytes 4194304 | tf_op jit(solution)/shard_map/jit(_where)/select_n | solution.py:718
  12.3 2.4 %collective-permute-done.1.p2 = bf16[128,1664]{1,0:T(8,128)(2,1)S(1)} collective-permute-done((bf16[128,1664]{1,0:T(8,128)(2,1)S(1)}, bf16[128,1664]{1,0:T(8,128)(2,1)S(1)}, u32[]{:S(2)}, u32[]{:S(2)}) %collective-permute-start.1) | collective-permute-done | bytes 426016 | tf_op jit(solution)/shard_map/ppermute | solution.py:44
  16.0 2.6 %log-plus-one_select_fusion.b_ref = f32[512,1024]{1,0:T(8,128)} fusion(s32[512]{0:T(512)S(1)} %bitcast.89, s32[1024]{0:T(1024)S(1)} %bitcast.85, s32[512]{0:T(512)S(1)} %bitcast.88, s32[512]{0:T(512)S(1)} %bitcast.87), kind=kLoop, calls=%fused_computation.1 | loop fusion | flops 3670016 | bytes 2107392 | tf_op jit(solution)/shard_map/jit(_where)/select_n | solution.py:726
  18.7 6.7 %project.1 = (bf16[512,512]{1,0:T(8,128)(2,1)}, bf16[1024,512]{1,0:T(8,128)(2,1)}, bf16[1024,512]{1,0:T(8,128)(2,1)}, bf16[512,1024]{1,0:T(8,128)(2,1)}, bf16[512,1536]{1,0:T(8,128)(2,1)}, /*index=5*/f32[16,512]{1,0:T(8,128)}) custom-call(s32[1]{0:T(128)} %bitcast.me_ref, bf16[512,512]{1,0:T(8,128)(2,1)} %bitcast.81, ...), custom_call_target="tpu_custom_call" | custom-call | flops 1610612736 | bytes 6000000 | tf_op jit(solution)/shard_map/project/pallas_call | solution.py:215
  25.3 19.7 %attend_forward.1 = (f32[512,512]{1,0:T(8,128)}, f32[512,512]{1,0:T(8,128)}, f32[512,512]{1,0:T(8,128)}, f32[512,512]{1,0:T(8,128)}, bf16[8,512,1024]{2,1,0:T(8,128)(2,1)}, /*index=5*/bf16[8,512,1024]{2,1,0:T(8,128)(2,1)}) custom-call(f32[16,512]{1,0:T(8,128)} %get-tuple-element.95.small_ref, bf16[512,512]{1,0:T(8,128)(2,1)} %get-tuple-element.96.q_ref, ...), custom_call_target="tpu_custom_call" | custom-call | flops 1610612736 | bytes 16777216 | tf_op jit(solution)/shard_map/attend_forward/pallas_call | solution.py:278
  45.2 2.9 %collective-permute-done.6.p3 = bf16[1280,512]{1,0:T(8,128)(2,1)S(1)} collective-permute-done((bf16[1280,512]{1,0:T(8,128)(2,1)S(1)}, bf16[1280,512]{1,0:T(8,128)(2,1)S(1)}, u32[]{:S(2)}, u32[]{:S(2)}) %collective-permute-start.6) | collective-permute-done | bytes 1310752 | tf_op jit(solution)/shard_map/ppermute | solution.py:44
  49.2 15.1 %middle.1 = (bf16[512,512]{1,0:T(8,128)(2,1)}, f32[512,512]{1,0:T(8,128)}, bf16[512,512]{1,0:T(8,128)(2,1)}, bf16[512,512]{1,0:T(8,128)(2,1)}, f32[8,512]{1,0:T(...) custom-call(s32[1]{0:T(128)} %bitcast.me_ref, ...), custom_call_target="tpu_custom_call" | custom-call | flops 8053063680 | bytes 16000000 | tf_op jit(solution)/shard_map/middle/pallas_call | solution.py:391
  66.4 1.2 add_convert_fusion.2
  67.9 1.6 collective-permute-start.10
  69.5 1.6 collective-permute-start.12
  71.9 19.6 %attend_backward.1 = (bf16[512,512]{1,0:T(8,128)(2,1)}, bf16[1024,512]{1,0:T(8,128)(2,1)}, bf16[1024,512]{1,0:T(8,128)(2,1)}, f32[4,8,128]{2,1,0:T(8,128)}) custom-call(bf16[512,512]{1,0:T(8,128)(2,1)} %get-tuple-element.96.q_ref, bf16[1024,512]{1,0:T(8,128)(2,1)} %get-tuple-element.97.k_ref, bf16[1024,512]{1,0:T(8,128)(2,1)} %get-tuple-element.98.v_ref, ...), custom_call_target="tpu_custom_call" | custom-call | flops 3221225472 | bytes 16777216 | tf_op jit(solution)/shard_map/attend_backward/pallas_call | solution.py:490
  91.9 1.6 collective-permute-start.14
  94.1 4.6 %weight_grads.1 = (bf16[128,1664]{1,0:T(8,128)(2,1)}, bf16[128,1664]{1,0:T(8,128)(2,1)}, bf16[128,1664]{1,0:T(8,128)(2,1)}, bf16[128,1664]{1,0:T(8,128)(2,1)}) custom-call(s32[1]{0:T(128)} %bitcast.me_ref, bf16[512,1024]{1,0:T(8,128)(2,1)} %get-tuple-element.123.turned_ref, bf16[512,512]{1,0:T(8,128)(2,1)} %get-tuple-element.141.gq_ref, ...), custom_call_target="tpu_custom_call" | custom-call | flops 1610612736 | bytes 6000000 | tf_op jit(solution)/shard_map/weight_grads/pallas_call | solution.py:538
  99.2 1.6 collective-permute-done.15
  100.8 1.5 collective-permute-done.14
  104.0 4.8 %row_grads.1 = (bf16[512,512]{1,0:T(8,128)(2,1)}, f32[512,512]{1,0:T(8,128)}) custom-call(bf16[512,512]{1,0:T(8,128)(2,1)} %get-tuple-element.141.gq_ref, bf16[1024,512]{1,0:T(8,128)(2,1)} %get-tuple-element.128.gk_ref, bf16[1024,512]{1,0:T(8,128)(2,1)} %get-tuple-element.129.gv_ref, bf16[512,1536]{1,0:T(8,128)(2,1)} %get-tuple-element.142.w_ref), custom_call_target="tpu_custom_call" | custom-call | flops 1610612736 | bytes 6000000 | tf_op jit(solution)/shard_map/row_grads/pallas_call | solution.py:566
  108.8 1.8 %collective-permute-done.17 = bf16[320,512]{1,0:T(8,128)(2,1)S(1)} collective-permute-done((bf16[320,512]{1,0:T(8,128)(2,1)S(1)}, bf16[320,512]{1,0:T(8,128)(2,1)S(1)}, u32[]{:S(2)}, u32[]{:S(2)}) %collective-permute-start.17) | collective-permute-done | bytes 327712 | tf_op jit(solution)/shard_map/ppermute | solution.py:44
  111.1 2.5 %collective-permute-done.19 = bf16[128,1664]{1,0:T(8,128)(2,1)S(1)} collective-permute-done((bf16[128,1664]{1,0:T(8,128)(2,1)S(1)}, bf16[128,1664]{1,0:T(8,128)(2,1)S(1)}, u32[]{:S(2)}, u32[]{:S(2)}) %collective-permute-start.19) | collective-permute-done | bytes 426016 | tf_op jit(solution)/shard_map/ppermute | solution.py:44
  113.8 1.6 collective-permute-start.20
  115.3 7.2 %collective-permute-done.21 = bf16[160,512]{1,0:T(8,128)(2,1)S(1)} collective-permute-done((bf16[160,512]{1,0:T(8,128)(2,1)S(1)}, bf16[160,512]{1,0:T(8,128)(2,1)S(1)}, u32[]{:S(2)}, u32[]{:S(2)}) %collective-permute-start.21) | collective-permute-done | bytes 163872 | tf_op jit(solution)/shard_map/ppermute | solution.py:44
  122.9 7.6 %collective-permute-done.24 = bf16[160,512]{1,0:T(8,128)(2,1)S(1)} collective-permute-done((bf16[160,512]{1,0:T(8,128)(2,1)S(1)}, bf16[160,512]{1,0:T(8,128)(2,1)S(1)}, u32[]{:S(2)}, u32[]{:S(2)}) %collective-permute-start.24) | collective-permute-done | bytes 163872 | tf_op jit(solution)/shard_map/ppermute | solution.py:44
  130.5 3.4 %collective-permute-start.22 = (bf16[512,512]{1,0:T(8,128)(2,1)S(1)}, bf16[512,512]{1,0:T(8,128)(2,1)S(1)}, u32[]{:S(2)}, u32[]{:S(2)}) collective-permute-start(bf16[512,512]{1,0:T(8,128)(2,1)S(1)} %copy-done.18), channel_id=1, source_target_pairs={{0,4},{4,0},{1,5},{5,1},{2,6},{6,2},{3,7},{7,3},{8,12},{12,8},{9,1... | collective-permute-start | bytes 1572872 | tf_op jit(solution)/shard_map/ppermute | solution.py:44
  134.9 11.5 %collective-permute-done.22.away_ref = bf16[512,512]{1,0:T(8,128)(2,1)S(1)} collective-permute-done((bf16[512,512]{1,0:T(8,128)(2,1)S(1)}, bf16[512,512]{1,0:T(8,128)(2,1)S(1)}, u32[]{:S(2)}, u32[]{:S(2)}) %collective-permute-start.22) | collective-permute-done | bytes 524320 | tf_op jit(solution)/shard_map/ppermute | solution.py:44
  146.5 2.3 %collective-permute-start.28 = (bf16[320,512]{1,0:T(8,128)(2,1)S(1)}, bf16[320,512]{1,0:T(8,128)(2,1)S(1)}, u32[]{:S(2)}, u32[]{:S(2)}) collective-permute-start(bf16[320,512]{1,0:T(8,128)(2,1)S(1)} %pad_maximum_fusion.2.own_a), channel_id=1, source_target_pairs={{0,4},{4,0},{1,5},{5,1},{2,6},{6,2},{3,7},{7,3},{8,12},{12,8},{9,1... | collective-permute-start | bytes 983048 | tf_op jit(solution)/shard_map/ppermute | solution.py:44
  148.7 3.6 %finish.1 = f32[512,512]{1,0:T(8,128)} custom-call(bf16[512,512]{1,0:T(8,128)(2,1)} %bitcast.83, f32[16,512]{1,0:T(8,128)} %get-tuple-element.95.small_ref, f32[512,512]{1,0:T(8,128)} %get-tuple-element.104.gh1_ref, f32[512,512]{1,0:T(8,128)} %get-tuple-element.143.own_ref, bf16[512,512]{1,0:T(8,128)(2,1)} %copy-done.6), custom_call_target="tpu_custom_call" | custom-call | bytes 4000000 | tf_op jit(solution)/shard_map/finish/pallas_call | solution.py:661
  153.2 1.3 collective-permute-start.27
  154.5 4.9 %collective-permute-done.29.other_b = bf16[320,512]{1,0:T(8,128)(2,1)S(1)} collective-permute-done((bf16[320,512]{1,0:T(8,128)(2,1)S(1)}, bf16[320,512]{1,0:T(8,128)(2,1)S(1)}, u32[]{:S(2)}, u32[]{:S(2)}) %collective-permute-start.29) | collective-permute-done | bytes 327712 | tf_op jit(solution)/shard_map/ppermute | solution.py:44
  160.2 3.8 %assemble.1 = (f32[128,512]{1,0:T(8,128)}, f32[128,512]{1,0:T(8,128)}, f32[512,512]{1,0:T(8,128)}, f32[128,2048]{1,0:T(8,128)}, f32[1,128]{1,0:T(1,128)}) custom-call(s32[1]{0:T(128)} %bitcast.31.near_ref, s32[1]{0:T(128)} %bitcast.32.far_ref, bf16[320,512]{1,0:T(8,128)(2,1)} %copy-done.1, bf16[320,512]{1,0:T(8,128)(2,1)} %copy-done.10, ...), custom_call_target="tpu_custom_call" | custom-call | bytes 4000000 | tf_op jit(solution)/shard_map/assemble/pallas_call | solution.py:615
  164.7 2.5 %close.1 = (f32[128,1536]{1,0:T(8,128)}, f32[1,128]{1,0:T(1,128)}, f32[1,128]{1,0:T(1,128)}, f32[1,2]{1,0:T(1,128)}) custom-call(s32[1]{0:T(128)} %bitcast.31.near_ref, bf16[64,1664]{1,0:T(8,128)(2,1)} %copy-done.2, bf16[64,1664]{1,0:T(8,128)(2,1)} %copy-done.13, bf16[128,1536]{1,0:T(8,128)(2,1)} %w_ref.1, bf16[1,128]{1,0:T(2,128)(2,1)} %bitcast.91), custom_call_target="tpu_custom_call" | custom-call | bytes 2000000 | tf_op jit(solution)/shard_map/close/pallas_call | solution.py:642
  (123 shorter events, 17.3 us)
Async XLA Ops:
  3.0 11.6 %collective-permute-start.1 = (bf16[128,1664]{1,0:T(8,128)(2,1)S(1)}, bf16[128,1664]{1,0:T(8,128)(2,1)S(1)}, u32[]{:S(2)}, u32[]{:S(2)}) collective-permute-start(bf16[128,1664]{1,0:T(8,128)(2,1)S(1)} %pad_maximum_fusion.1.p0), channel_id=1, source_target_pairs={{0,2},{1,3},{2,0},{3,1},{4,6},{5,7},{6,4},{7,5},{8,10},{9,11},{10,... | collective-permute-start | bytes 1277960 | tf_op jit(solution)/shard_map/ppermute | solution.py:44
  3.6 15.0 %collective-permute-start.2 = (bf16[128,1664]{1,0:T(8,128)(2,1)S(1)}, bf16[128,1664]{1,0:T(8,128)(2,1)}, u32[]{:S(2)}, u32[]{:S(2)}) collective-permute-start(bf16[128,1664]{1,0:T(8,128)(2,1)S(1)} %pad_maximum_fusion.1.p0), channel_id=1, source_target_pairs={{0,1},{1,0},{2,3},{3,2},{4,5},{5,4},{6,7},{7,6},{8,9},{9,8},{10,11... | collective-permute-start | bytes 1277960 | tf_op jit(solution)/shard_map/ppermute | solution.py:44
  3.6 15.0 %collective-permute-start = (bf16[512,512]{1,0:T(8,128)(2,1)}, bf16[512,512]{1,0:T(8,128)(2,1)}, u32[]{:S(2)}, u32[]{:S(2)}) collective-permute-start(bf16[512,512]{1,0:T(8,128)(2,1)} %bitcast.80), channel_id=1, source_target_pairs={{0,4},{4,0},{1,5},{5,1},{2,6},{6,2},{3,7},{7,3},{8,12},{12,8},{9,1... | collective-permute-start | bytes 1572872 | tf_op jit(solution)/shard_map/ppermute | solution.py:44
  14.7 30.3 %collective-permute-start.5 = (bf16[1280,512]{1,0:T(8,128)(2,1)S(1)}, bf16[1280,512]{1,0:T(8,128)(2,1)S(1)}, u32[]{:S(2)}, u32[]{:S(2)}) collective-permute-start(bf16[1280,512]{1,0:T(8,128)(2,1)S(1)} %copy-done), channel_id=1, source_target_pairs={{0,2},{1,3},{2,0},{3,1},{4,6},{5,7},{6,4},{7,5},{8,10},{9,11},{10,... | collective-permute-start | bytes 3932168 | tf_op jit(solution)/shard_map/ppermute | solution.py:44
  15.5 3.2 %collective-permute-start.3 = (bf16[128,1664]{1,0:T(8,128)(2,1)S(1)}, bf16[128,1664]{1,0:T(8,128)(2,1)}, u32[]{:S(2)}, u32[]{:S(2)}) collective-permute-start(bf16[128,1664]{1,0:T(8,128)(2,1)S(1)} %collective-permute-done.1.p2), channel_id=1, source_target_pairs={{0,1},{1,0},{2,3},{3,2},{4,5},{5,4},{6,7},{7,6},{8,9},{9,8},{10,11... | collective-permute-start | bytes 1277960 | tf_op jit(solution)/shard_map/ppermute | solution.py:44
  15.5 29.7 %collective-permute-start.4 = (bf16[1280,512]{1,0:T(8,128)(2,1)S(1)}, bf16[1280,512]{1,0:T(8,128)(2,1)S(1)}, u32[]{:S(2)}, u32[]{:S(2)}) collective-permute-start(bf16[1280,512]{1,0:T(8,128)(2,1)S(1)} %copy-done), channel_id=1, source_target_pairs={{0,1},{1,0},{2,3},{3,2},{4,5},{5,4},{6,7},{7,6},{8,9},{9,8},{10,11... | collective-permute-start | bytes 3932168 | tf_op jit(solution)/shard_map/ppermute | solution.py:44
  45.0 3.1 %collective-permute-start.6 = (bf16[1280,512]{1,0:T(8,128)(2,1)S(1)}, bf16[1280,512]{1,0:T(8,128)(2,1)S(1)}, u32[]{:S(2)}, u32[]{:S(2)}) collective-permute-start(bf16[1280,512]{1,0:T(8,128)(2,1)S(1)} %collective-permute-done.5.p2), channel_id=1, source_target_pairs={{0,1},{1,0},{2,3},{3,2},{4,5},{5,4},{6,7},{7,6},{8,9},{9,8},{10,11... | collective-permute-start | bytes 3932168 | tf_op jit(solution)/shard_map/ppermute | solution.py:44
  64.2 2.2 %collective-permute-start.9 = (bf16[512,512]{1,0:T(8,128)(2,1)}, bf16[512,512]{1,0:T(8,128)(2,1)S(1)}, u32[]{:S(2)}, u32[]{:S(2)}) collective-permute-start(bf16[512,512]{1,0:T(8,128)(2,1)} %get-tuple-element.111), channel_id=1, source_target_pairs={{0,1},{1,0},{2,3},{3,2},{4,5},{5,4},{6,7},{7,6},{8,9},{9,8},{10,11... | collective-permute-start | bytes 1572872 | tf_op jit(solution)/shard_map/ppermute | solution.py:44
  64.4 3.2 %collective-permute-start.7 = (bf16[768,512]{1,0:T(8,128)(2,1)}, bf16[768,512]{1,0:T(8,128)(2,1)S(1)}, u32[]{:S(2)}, u32[]{:S(2)}) collective-permute-start(bf16[768,512]{1,0:T(8,128)(2,1)} %get-tuple-element.107), channel_id=1, source_target_pairs={{0,1},{1,0},{2,3},{3,2},{4,5},{5,4},{6,7},{7,6},{8,9},{9,8},{10,11... | collective-permute-start | bytes 2359304 | tf_op jit(solution)/shard_map/ppermute | solution.py:44
  64.8 6.3 %collective-permute-start.8 = (bf16[512,512]{1,0:T(8,128)(2,1)}, bf16[512,512]{1,0:T(8,128)(2,1)S(1)}, u32[]{:S(2)}, u32[]{:S(2)}) collective-permute-start(bf16[512,512]{1,0:T(8,128)(2,1)} %get-tuple-element.109), channel_id=1, source_target_pairs={{0,1},{1,0},{2,3},{3,2},{4,5},{5,4},{6,7},{7,6},{8,9},{9,8},{10,11... | collective-permute-start | bytes 1572872 | tf_op jit(solution)/shard_map/ppermute | solution.py:44
  64.9 26.5 %collective-permute-start.13 = (bf16[768,512]{1,0:T(8,128)(2,1)}, bf16[768,512]{1,0:T(8,128)(2,1)S(1)}, u32[]{:S(2)}, u32[]{:S(2)}) collective-permute-start(bf16[768,512]{1,0:T(8,128)(2,1)} %get-tuple-element.125), channel_id=1, source_target_pairs={{0,1},{1,0},{2,3},{3,2},{4,5},{5,4},{6,7},{7,6},{8,9},{9,8},{10,11... | collective-permute-start | bytes 2359304 | tf_op jit(solution)/shard_map/ppermute | solution.py:44
  67.9 23.5 %collective-permute-start.10 = (bf16[768,512]{1,0:T(8,128)(2,1)S(1)}, bf16[768,512]{1,0:T(8,128)(2,1)S(1)}, u32[]{:S(2)}, u32[]{:S(2)}) collective-permute-start(bf16[768,512]{1,0:T(8,128)(2,1)S(1)} %add_convert_fusion.1), channel_id=1, source_target_pairs={{0,2},{1,3},{2,0},{3,1},{4,6},{5,7},{6,4},{7,5},{8,10},{9,11},{10,... | collective-permute-start | bytes 2359304 | tf_op jit(solution)/shard_map/ppermute | solution.py:44
  69.5 21.9 %collective-permute-start.12 = (bf16[256,512]{1,0:T(8,128)(2,1)S(1)}, bf16[256,512]{1,0:T(8,128)(2,1)S(1)}, u32[]{:S(2)}, u32[]{:S(2)}) collective-permute-start(bf16[256,512]{1,0:T(8,128)(2,1)S(1)} %dynamic-slice_bitcast_fusion.4), channel_id=1, source_target_pairs={{0,4},{4,0},{1,5},{5,1},{2,6},{6,2},{3,7},{7,3},{8,12},{12,8},{9,1... | collective-permute-start | bytes 786440 | tf_op jit(solution)/shard_map/ppermute | solution.py:44
  71.3 20.2 %collective-permute-start.11 = (bf16[256,512]{1,0:T(8,128)(2,1)S(1)}, bf16[256,512]{1,0:T(8,128)(2,1)S(1)}, u32[]{:S(2)}, u32[]{:S(2)}) collective-permute-start(bf16[256,512]{1,0:T(8,128)(2,1)S(1)} %dynamic-slice_bitcast_fusion.5), channel_id=1, source_target_pairs={{0,4},{4,0},{1,5},{5,1},{2,6},{6,2},{3,7},{7,3},{8,12},{12,8},{9,1... | collective-permute-start | bytes 786440 | tf_op jit(solution)/shard_map/ppermute | solution.py:44
  71.9 19.6 %copy-start.3 = (bf16[768,512]{1,0:T(8,128)(2,1)S(1)}, bf16[768,512]{1,0:T(8,128)(2,1)}, u32[]{:S(2)}) copy-start(bf16[768,512]{1,0:T(8,128)(2,1)} %get-tuple-element.124) | copy-start | bytes 2359300
  91.9 10.4 %collective-permute-start.14 = (bf16[384,512]{1,0:T(8,128)(2,1)S(1)}, bf16[384,512]{1,0:T(8,128)(2,1)S(1)}, u32[]{:S(2)}, u32[]{:S(2)}) collective-permute-start(bf16[384,512]{1,0:T(8,128)(2,1)S(1)} %get-tuple-element.171), channel_id=1, source_target_pairs={{0,4},{4,0},{1,5},{5,1},{2,6},{6,2},{3,7},{7,3},{8,12},{12,8},{9,1... | collective-permute-start | bytes 1179656 | tf_op jit(solution)/shard_map/ppermute | solution.py:44
  93.5 7.3 %collective-permute-start.15 = (bf16[256,512]{1,0:T(8,128)(2,1)S(1)}, bf16[256,512]{1,0:T(8,128)(2,1)S(1)}, u32[]{:S(2)}, u32[]{:S(2)}) collective-permute-start(bf16[256,512]{1,0:T(8,128)(2,1)S(1)} %fusion.2), channel_id=1, source_target_pairs={{0,2},{1,3},{2,0},{3,1},{4,6},{5,7},{6,4},{7,5},{8,10},{9,11},{10,... | collective-permute-start | bytes 786440 | tf_op jit(solution)/shard_map/ppermute | solution.py:44
  98.7 4.4 %collective-permute-start.16 = (bf16[128,1664]{1,0:T(8,128)(2,1)}, bf16[128,1664]{1,0:T(8,128)(2,1)S(1)}, u32[]{:S(2)}, u32[]{:S(2)}) collective-permute-start(bf16[128,1664]{1,0:T(8,128)(2,1)} %get-tuple-element.137), channel_id=1, source_target_pairs={{0,1},{1,0},{2,3},{3,2},{4,5},{5,4},{6,7},{7,6},{8,9},{9,8},{10,11... | collective-permute-start | bytes 1277960 | tf_op jit(solution)/shard_map/ppermute | solution.py:44
  98.7 14.9 %collective-permute-start.18 = (bf16[128,1664]{1,0:T(8,128)(2,1)}, bf16[128,1664]{1,0:T(8,128)(2,1)S(1)}, u32[]{:S(2)}, u32[]{:S(2)}) collective-permute-start(bf16[128,1664]{1,0:T(8,128)(2,1)} %get-tuple-element.147), channel_id=1, source_target_pairs={{0,1},{1,0},{2,3},{3,2},{4,5},{5,4},{6,7},{7,6},{8,9},{9,8},{10,11... | collective-permute-start | bytes 1277960 | tf_op jit(solution)/shard_map/ppermute | solution.py:44
  102.6 8.0 %collective-permute-start.17 = (bf16[320,512]{1,0:T(8,128)(2,1)S(1)}, bf16[320,512]{1,0:T(8,128)(2,1)S(1)}, u32[]{:S(2)}, u32[]{:S(2)}) collective-permute-start(bf16[320,512]{1,0:T(8,128)(2,1)S(1)} %get-tuple-element.173), channel_id=1, source_target_pairs={{0,8},{8,0},{16,24},{24,16},{1,9},{9,1},{17,25},{25,17},{2,10},{10... | collective-permute-start | bytes 983048 | tf_op jit(solution)/shard_map/ppermute | solution.py:44
  103.4 10.1 %collective-permute-start.19 = (bf16[128,1664]{1,0:T(8,128)(2,1)S(1)}, bf16[128,1664]{1,0:T(8,128)(2,1)S(1)}, u32[]{:S(2)}, u32[]{:S(2)}) collective-permute-start(bf16[128,1664]{1,0:T(8,128)(2,1)S(1)} %add_convert_fusion.5), channel_id=1, source_target_pairs={{0,2},{1,3},{2,0},{3,1},{4,6},{5,7},{6,4},{7,5},{8,10},{9,11},{10,... | collective-permute-start | bytes 1277960 | tf_op jit(solution)/shard_map/ppermute | solution.py:44
  110.6 19.9 %copy-start.18 = (bf16[512,512]{1,0:T(8,128)(2,1)S(1)}, bf16[512,512]{1,0:T(8,128)(2,1)}, u32[]{:S(2)}) copy-start(bf16[512,512]{1,0:T(8,128)(2,1)} %get-tuple-element.152) | copy-start | bytes 1572868
  110.7 11.8 %collective-permute-start.21 = (bf16[160,512]{1,0:T(8,128)(2,1)S(1)}, bf16[160,512]{1,0:T(8,128)(2,1)S(1)}, u32[]{:S(2)}, u32[]{:S(2)}) collective-permute-start(bf16[160,512]{1,0:T(8,128)(2,1)S(1)} %dynamic-slice_bitcast_fusion.7), channel_id=1, source_target_pairs={{0,16},{8,24},{16,0},{24,8},{1,17},{9,25},{17,1},{25,9},{2,18},{10... | collective-permute-start | bytes 491528 | tf_op jit(solution)/shard_map/ppermute | solution.py:44
  113.8 8.9 %collective-permute-start.20 = (bf16[64,1664]{1,0:T(8,128)(2,1)S(1)}, bf16[64,1664]{1,0:T(8,128)(2,1)S(1)}, u32[]{:S(2)}, u32[]{:S(2)}) collective-permute-start(bf16[64,1664]{1,0:T(8,128)(2,1)S(1)} %dynamic-slice_bitcast_fusion.6), channel_id=1, source_target_pairs={{0,4},{4,0},{1,5},{5,1},{2,6},{6,2},{3,7},{7,3},{8,12},{12,8},{9,1... | collective-permute-start | bytes 638984 | tf_op jit(solution)/shard_map/ppermute | solution.py:44
  122.6 7.9 %collective-permute-start.24 = (bf16[160,512]{1,0:T(8,128)(2,1)S(1)}, bf16[160,512]{1,0:T(8,128)(2,1)S(1)}, u32[]{:S(2)}, u32[]{:S(2)}) collective-permute-start(bf16[160,512]{1,0:T(8,128)(2,1)S(1)} %fusion.4), channel_id=1, source_target_pairs={{0,16},{8,24},{16,0},{24,8},{1,17},{9,25},{17,1},{25,9},{2,18},{10... | collective-permute-start | bytes 491528 | tf_op jit(solution)/shard_map/ppermute | solution.py:44
  122.8 12.0 %collective-permute-start.23 = (bf16[64,1664]{1,0:T(8,128)(2,1)S(1)}, bf16[64,1664]{1,0:T(8,128)(2,1)S(1)}, u32[]{:S(2)}, u32[]{:S(2)}) collective-permute-start(bf16[64,1664]{1,0:T(8,128)(2,1)S(1)} %fusion.3), channel_id=1, source_target_pairs={{0,8},{8,0},{16,24},{24,16},{1,9},{9,1},{17,25},{25,17},{2,10},{10... | collective-permute-start | bytes 638984 | tf_op jit(solution)/shard_map/ppermute | solution.py:44
  130.5 16.0 %collective-permute-start.22 = (bf16[512,512]{1,0:T(8,128)(2,1)S(1)}, bf16[512,512]{1,0:T(8,128)(2,1)S(1)}, u32[]{:S(2)}, u32[]{:S(2)}) collective-permute-start(bf16[512,512]{1,0:T(8,128)(2,1)S(1)} %copy-done.18), channel_id=1, source_target_pairs={{0,4},{4,0},{1,5},{5,1},{2,6},{6,2},{3,7},{7,3},{8,12},{12,8},{9,1... | collective-permute-start | bytes 1572872 | tf_op jit(solution)/shard_map/ppermute | solution.py:44
  133.9 18.4 %collective-permute-start.26 = (bf16[320,512]{1,0:T(8,128)(2,1)S(1)}, bf16[320,512]{1,0:T(8,128)(2,1)S(1)}, u32[]{:S(2)}, u32[]{:S(2)}) collective-permute-start(bf16[320,512]{1,0:T(8,128)(2,1)S(1)} %pad_maximum_fusion.2.own_a), channel_id=1, source_target_pairs={{0,8},{8,0},{16,24},{24,16},{1,9},{9,1},{17,25},{25,17},{2,10},{10... | collective-permute-start | bytes 983048 | tf_op jit(solution)/shard_map/ppermute | solution.py:44
  134.8 18.3 %collective-permute-start.25 = (bf16[64,1664]{1,0:T(8,128)(2,1)S(1)}, bf16[64,1664]{1,0:T(8,128)(2,1)S(1)}, u32[]{:S(2)}, u32[]{:S(2)}) collective-permute-start(bf16[64,1664]{1,0:T(8,128)(2,1)S(1)} %add_convert_fusion.9), channel_id=1, source_target_pairs={{0,16},{8,24},{16,0},{24,8},{1,17},{9,25},{17,1},{25,9},{2,18},{10... | collective-permute-start | bytes 638984 | tf_op jit(solution)/shard_map/ppermute | solution.py:44
  146.5 8.1 %collective-permute-start.28 = (bf16[320,512]{1,0:T(8,128)(2,1)S(1)}, bf16[320,512]{1,0:T(8,128)(2,1)S(1)}, u32[]{:S(2)}, u32[]{:S(2)}) collective-permute-start(bf16[320,512]{1,0:T(8,128)(2,1)S(1)} %pad_maximum_fusion.2.own_a), channel_id=1, source_target_pairs={{0,4},{4,0},{1,5},{5,1},{2,6},{6,2},{3,7},{7,3},{8,12},{12,8},{9,1... | collective-permute-start | bytes 983048 | tf_op jit(solution)/shard_map/ppermute | solution.py:44
  152.3 7.1 %collective-permute-start.29 = (bf16[320,512]{1,0:T(8,128)(2,1)S(1)}, bf16[320,512]{1,0:T(8,128)(2,1)S(1)}, u32[]{:S(2)}, u32[]{:S(2)}) collective-permute-start(bf16[320,512]{1,0:T(8,128)(2,1)S(1)} %collective-permute-done.26.own_b), channel_id=1, source_target_pairs={{0,4},{4,0},{1,5},{5,1},{2,6},{6,2},{3,7},{7,3},{8,12},{12,8},{9,1... | collective-permute-start | bytes 983048 | tf_op jit(solution)/shard_map/ppermute | solution.py:44
  153.2 10.8 %collective-permute-start.27 = (bf16[64,1664]{1,0:T(8,128)(2,1)S(1)}, bf16[64,1664]{1,0:T(8,128)(2,1)S(1)}, u32[]{:S(2)}, u32[]{:S(2)}) collective-permute-start(bf16[64,1664]{1,0:T(8,128)(2,1)S(1)} %add_convert_fusion.8.own_ref), channel_id=1, source_target_pairs={{0,4},{4,0},{1,5},{5,1},{2,6},{6,2},{3,7},{7,3},{8,12},{12,8},{9,1... | collective-permute-start | bytes 638984 | tf_op jit(solution)/shard_map/ppermute | solution.py:44
  (19 other events, 93.0 us)

commit v2 on v1

--- a/solution.py
+++ b/solution.py
@@ -23,8 +23,8 @@
     return lax.dot_general(left, right, dims, preferred_element_type=F32)
 
 
-def params():
-    return pltpu.CompilerParams(vmem_limit_bytes=VMEM)
+def params(limit=VMEM):
+    return pltpu.CompilerParams(vmem_limit_bytes=limit)
 
 
 def like(shape, dtype):
@@ -33,6 +33,10 @@
 
 def in_place():
     return pl.BlockSpec(memory_space=pl.ANY)
+
+
+def on_chip(*values):
+    return [pltpu.with_memory_space_constraint(value, pltpu.VMEM) for value in values]
 
 
 def scalar():
@@ -150,20 +154,28 @@
 
 def lay_rows(width, pieces):
     arrays = [piece[0] for piece in pieces]
+    total = sum(array.shape[0] for array in arrays)
 
     def body(*refs):
+        target, sem = refs[len(pieces) :]
+        copies = []
         first = 0
-        for ref, (_, col) in zip(refs, pieces):
-            refs[-1][first : first + ref.shape[0], :] = ref[:, col : col + width]
+        for n, (ref, (_, col)) in enumerate(zip(refs, pieces)):
+            source = ref.at[:, col : col + width]
+            copies.append(pltpu.make_async_copy(source, target.at[first : first + ref.shape[0]], sem.at[n]))
             first += ref.shape[0]
-
-    total = sum(array.shape[0] for array in arrays)
+        for copy in copies:
+            copy.start()
+        for copy in copies:
+            copy.wait()
+
     vmem = pl.BlockSpec(memory_space=pltpu.VMEM)
     return pl.pallas_call(
         body,
         in_specs=[vmem] * len(arrays),
-        out_specs=vmem,
+        out_specs=in_place(),
         out_shape=like((total, width), BF16),
+        scratch_shapes=[pltpu.SemaphoreType.DMA((len(arrays),))],
         compiler_params=params(),
         cost_estimate=pl.CostEstimate(flops=0, transcendentals=0, bytes_accessed=4 * total * width),
         name="lay_rows",
@@ -244,27 +256,37 @@
     )(me, own, others, *packs)
 
 
-def forward_body(rows, small_ref, q_ref, k_ref, v_ref, b_ref, c_ref, o_ref, m_ref, r1_ref, r2_ref, e1_ref, e2_ref):
+def forward_body(
+    rows, small_ref, q_ref, k_ref, v_ref, b_ref, c_ref, o_ref, m_ref, r1_ref, r2_ref, e1_ref, e2_ref, first, second
+):
     low_lanes = lax.broadcasted_iota(jnp.int32, (rows, 128), 1) < 64
-    for start in range(0, q_ref.shape[0], rows):
-        at = pl.ds(start, rows)
-        mixed = []
-        for side in range(2):
-            slope = small_ref[3:4, side : side + 1]
-            q_head = jnp.where(low_lanes == (side == 0), q_ref[at, :], 0).astype(BF16)
-            raw = product(q_head, k_ref[...], NT)
-            for table in (e1_ref, e2_ref):
-                values = raw - slope * b_ref[at, :] if table is e1_ref else raw + c_ref[at, :]
-                peak = jnp.max(values, axis=1, keepdims=True)
-                shifted = jnp.exp(values - peak)
-                total = jnp.sum(shifted, axis=1, keepdims=True)
-                weights = shifted.astype(BF16)
-                table[side, at, :] = weights
-                mixed.append((product(weights, v_ref[...]), 1.0 / total))
-        for slot, value_ref, recip_ref in ((0, o_ref, r1_ref), (1, m_ref, r2_ref)):
-            recip = jnp.where(low_lanes, mixed[slot][1], mixed[2 + slot][1])
-            recip_ref[at, :] = recip
-            value_ref[at, :] = jnp.where(low_lanes, mixed[slot][0], mixed[2 + slot][0]) * recip
+    values = jnp.concatenate([v_ref[...], jnp.ones(v_ref.shape, BF16)], axis=1)
+    items = [(pl.ds(start, rows), side) for start in range(0, q_ref.shape[0], rows) for side in range(2)]
+
+    def scores(n):
+        at, side = items[n]
+        slope = small_ref[3:4, side : side + 1]
+        q_head = jnp.where(low_lanes == (side == 0), q_ref[at, :], 0).astype(BF16)
+        raw = product(q_head, k_ref[...], NT)
+        first[n % 2] = raw - slope * b_ref[at, :]
+        second[n % 2] = raw + c_ref[at, :]
+        return [jnp.max(table[n % 2], axis=1, keepdims=True) for table in (first, second)]
+
+    mixed = {}
+    peaks = scores(0)
+    for n, (at, side) in enumerate(items):
+        later = scores(n + 1) if n + 1 < len(items) else None
+        for slot, (table, kept_ref) in enumerate(((first, e1_ref), (second, e2_ref))):
+            weights = jnp.exp(table[n % 2] - peaks[slot]).astype(BF16)
+            kept_ref[side, at, :] = weights
+            both = product(weights, values)
+            mixed[side, slot] = (both[:, :128], 1.0 / both[:, 128:])
+        peaks = later
+        if side == 1:
+            for slot, value_ref, recip_ref in ((0, o_ref, r1_ref), (1, m_ref, r2_ref)):
+                recip = jnp.where(low_lanes, mixed[0, slot][1], mixed[1, slot][1])
+                recip_ref[at, :] = recip
+                value_ref[at, :] = jnp.where(low_lanes, mixed[0, slot][0], mixed[1, slot][0]) * recip
 
 
 def attend_forward(small, q, k, v, bias, count):
@@ -289,6 +311,7 @@
         out_specs=[pl.BlockSpec((step_rows, 128), own)] * 4
         + [pl.BlockSpec((2, step_rows, key_count), lambda p, i: (p, i, 0))] * 2,
         out_shape=[like((row_count, width), F32)] * 4 + [like((2 * pairs, row_count, key_count), BF16)] * 2,
+        scratch_shapes=[pltpu.VMEM((2, rows, key_count), F32)] * 2,
         compiler_params=params(),
         cost_estimate=pl.CostEstimate(
             flops=elements * 64 * 2 * 3, transcendentals=2 * elements, bytes_accessed=4 * elements
@@ -585,18 +608,18 @@
 
 
 def assemble_body(
-    near_ref, far_ref, own_a, own_b, other_a, other_b, up_w_ref, gain_ref, out_ref, memory_ref, down_ref, up_ref, sum_ref
+    near_ref, far_ref, own_a, own_b, other_a, by_ctx, by_seq, up_w_ref, gain_ref, out_ref, memory_ref, down_ref, up_ref, sum_ref
 ):
     width = out_ref.shape[1]
     groups = up_ref.shape[1] // width
     short = out_ref.shape[0] // 8
     tall = down_ref.shape[0] // 8
     size = own_a.shape[0] // 2
-    for n, part_ref in enumerate((own_a, own_b, other_a, other_b)):
+    for n, (part_ref, first_part) in enumerate(((own_a, 0), (own_b, 0), (other_a, 0), (by_ctx, 0), (by_seq, 1))):
         side = near_ref[0] if n < 2 else 1 - near_ref[0]
-        pair = far_ref[0] if n % 2 == 0 else 1 - far_ref[0]
-        for p in range(2):
-            place = 4 * side + 2 * pair + p
+        pair = far_ref[0] if n % 2 == 0 and n < 4 else 1 - far_ref[0]
+        for p in range(part_ref.shape[0] // size):
+            place = 4 * side + 2 * pair + first_part + p
             at = pl.ds(pl.multiple_of(place * short, short), short)
             piece = part_ref[p * size : (p + 1) * size, :].astype(F32)
             out_ref[at, :] = piece[0:short, :]
@@ -614,14 +637,14 @@
     vmem = pl.BlockSpec(memory_space=pltpu.VMEM)
     return pl.pallas_call(
         assemble_body,
-        in_specs=[scalar(), scalar()] + [vmem] * 6,
+        in_specs=[scalar(), scalar()] + [vmem] * 7,
         out_specs=[vmem] * 5,
         out_shape=[like((shard, width), F32)] * 2
         + [like((width, width), F32), like((shard, columns), F32), like((1, shard), F32)],
         compiler_params=params(),
         cost_estimate=pl.CostEstimate(flops=0, transcendentals=0, bytes_accessed=4000000),
         name="assemble",
-    )(near, far, *parts, w_up, gain[None])
+    )(near, far, *on_chip(*parts), w_up, gain[None])
 
 
 def close_body(near_ref, own_ref, other_ref, w_ref, gain_ref, qkv_ref, gain_sum_ref, gate_ref, slope_ref):
@@ -647,7 +670,7 @@
         compiler_params=params(),
         cost_estimate=pl.CostEstimate(flops=0, transcendentals=0, bytes_accessed=2000000),
         name="close",
-    )(near, own, other, w_qkv, gain[None])
+    )(near, *on_chip(own, other), w_qkv, gain[None])
 
 
 def finish_body(tokens_ref, small_ref, gh1_ref, own_ref, away_ref, out_ref):
@@ -666,7 +689,7 @@
         compiler_params=params(),
         cost_estimate=pl.CostEstimate(flops=0, transcendentals=0, bytes_accessed=4000000),
         name="finish",
-    )(tokens, small, gh1, own, away)
+    )(tokens, small, gh1, own, *on_chip(away))
 
 
 def on_device(
@@ -714,14 +737,17 @@
     my_memory = jnp.sum(memory_hot * memory_len, axis=1)
     row_start = jnp.repeat(my_blocks * block_len, block_len)
     row_low = row_start - jnp.repeat(my_memory, block_len)
-    hits = jnp.sum((neighbours[:, :, None] == key_pos[None, None, :]).astype(F32), axis=1)
-    count = jnp.where(hits > 0.0, jnp.log(jnp.maximum(hits, 1.0)), ABSENT)
+    picks = neighbours.shape[1]
+    hits = sum((neighbours[:, n : n + 1] == key_pos[None, :]).astype(F32) for n in range(picks))
+    count = jnp.where(hits == 1.0, 0.0, ABSENT)
+    for times in range(2, picks + 1):
+        count = jnp.where(hits == float(times), math.log(times), count)
     pack_far, wide = lax.optimization_barrier((pack_far, wide, count))[:2]
     pack_both = swap(pack_far, "wt", 1)
     wide_far = swap(wide, "wt", 2)
     wide_near = swap(wide, "wt", 1)
     row_pos = hold(row_pos, pack_far)
-    distance = jnp.log1p(jnp.abs(row_pos[:, None] - key_pos[None, :]).astype(F32))
+    distance = jnp.log(jnp.abs(row_pos[:, None] - key_pos[None, :]).astype(F32) + 1.0)
     visible = (key_pos[None, :] >= row_low[:, None]) & (key_pos[None, :] < (row_start + block_len)[:, None])
     bias = jnp.where(visible, distance, HIDDEN)
 
@@ -762,30 +788,31 @@
         order = Order()
         near, gh_got = order.arrive(near, gh_got)
         gh = add_low(gh_keep, gh_got)
-        gh_keep, gh_got = send_half(gh, "seq", 2)
+        gh_got = swap(gh, "seq", 2)
         q_keep, q_got = send_half(add_all(q0, [q_one, order.arrive(q_far)]), "ctx", 1)
-        gh = add_low(gh_keep, order.arrive(gh_got))
-        gh_other = swap(gh, "seq", 2)
         q_sum = add_low(q_keep, order.arrive(q_got))
         q_got = swap(q_sum, "seq", 1)
         away = swap(hold(near, q_sum), "ctx", 1)
-        own_a = place_half(gh, order.arrive(gh_other), "seq", 2)
-        own_b = swap(own_a, "seq", 1)
         q_sum = add_low(q_sum, order.arrive(q_got))
         q_got = swap(q_sum, "seq", 2)
+        own_a = add_low(gh, order.arrive(gh_got))
+        own_b = swap(own_a, "seq", 1)
+        other_a = swap(own_a, "ctx", 1)
         away = order.arrive(away)
-        other_a = swap(hold(own_a, away), "ctx", 1)
         grad_tokens = finish(tokens, small, gh1, own, away)
         order.before = (grad_tokens,)
-        own_b = order.arrive(own_b)
-        other_b = swap(own_b, "ctx", 1)
         q_sum = add_low(q_sum, order.arrive(q_got))
         q_other = swap(q_sum, "ctx", 1)
+        own_b = order.arrive(own_b)
+        other_a = order.arrive(other_a)
+        cut = own_b.shape[0] // 2
+        by_seq = swap(other_a[cut:], "seq", 1)
+        by_ctx = swap(own_b[:cut], "ctx", 1)
         side = lax.axis_index("ctx").astype(jnp.int32).reshape(1)
         pair = side_of("seq", 1).astype(jnp.int32).reshape(1)
-        other_a, other_b = order.arrive(other_a, other_b)
+        by_ctx, by_seq = order.arrive(by_ctx, by_seq)
         t_out, t_memory, t_down, t_up, t_gain_two = assemble(
-            side, pair, (own_a, own_b, other_a, other_b), w_up, gain_ffn
+            side, pair, (own_a, own_b, other_a, by_ctx, by_seq), w_up, gain_ffn
         )
         order.before = (t_gain_two,)
         t_qkv, *shorts = close(side, q_sum, order.arrive(q_other), w_qkv, gain_attn, heads_here)

time: 168 us -> 157 us (0.935)
  the two profiles are of different devices: /device:TPU:28 before, /device:TPU:0 now
where the time goes in v2:
time: 157 us
  Pallas kernels  79.2 us (50%)
  starting transfers between devices  33.5 us (21%)
  waiting for transfers between devices  30.2 us (19%)
  other arithmetic  10.8 us (7%)
  local copies, waits for them, and re-layouts  2.13 us (1%)
    ppermute x30, starting transfers between devices, swap(): return lax.ppermute(value, axis, [(i, i ^ bit) for i in range(size)])  33.5 us
    ppermute x30, waiting for transfers between devices, swap(): return lax.ppermute(value, axis, [(i, i ^ bit) for i in range(size)])  30.2 us
    pallas_call x1, Pallas kernels, attend_backward(): pl.pallas_call(functools.partial(backward_body, several, 256), grid=(pair...  19.5 us
    pallas_call x1, Pallas kernels, attend_forward(): pl.pallas_call(functools.partial(forward_body, rows), grid=(pairs, row_co...  16.5 us
    pallas_call x1, Pallas kernels, middle(): pl.pallas_call(functools.partial(middle_body, slices), in_specs=[scalar()...  15.1 us
    pallas_call x1, Pallas kernels, project(): pl.pallas_call(project_body, grid=(steps,), in_specs=[scalar(), pl.BlockS...  6.65 us
    pallas_call x1, Pallas kernels, row_grads(): pl.pallas_call(rows_body, in_specs=[vmem] * 4, out_specs=[vmem] * 2, out_...  4.77 us
    pallas_call x1, Pallas kernels, weight_grads(): pl.pallas_call(weights_body, in_specs=[scalar()] + [vmem] * 6, out_specs=...  4.62 us
  transfers between devices with their start and end apart: 30, of which 14 were waited for; matrix products, arithmetic and copies ran while one was open for 6% of the time, Pallas kernels for 39%

profile of v2, /device:TPU:0, one launch (start us, length us, event | category | flops | bytes accessed | tf_op | source)
XLA Modules:
  0.0 156.9 jit_solution(14355145224152392160)
XLA Ops:
  3.0 3.0 %collective-permute-start.1 = (bf16[128,1664]{1,0:T(8,128)(2,1)S(1)}, bf16[128,1664]{1,0:T(8,128)(2,1)S(1)}, u32[]{:S(2)}, u32[]{:S(2)}) collective-permute-start(bf16[128,1664]{1,0:T(8,128)(2,1)S(1)} %pad_maximum_fusion.1.p0), channel_id=1, source_target_pairs={{0,2},{1,3},{2,0},{3,1},{4,6},{5,7},{6,4},{7,5},{8,10},{9,11},{10,... | collective-permute-start | bytes 1277960 | tf_op jit(solution)/shard_map/ppermute | solution.py:48
  8.6 3.2 %lay_rows.1.p0 = bf16[1280,512]{1,0:T(8,128)(2,1)} custom-call(bf16[128,512]{1,0:T(8,128)(2,1)} %refs_0_.1, bf16[128,512]{1,0:T(8,128)(2,1)} %refs_1_.1, bf16[128,2048]{1,0:T(8,128)(2,1)} %up_w_ref.1, bf16[128,2048]{1,0:T(8,128)(2,1)} %up_w_ref.1, bf16[128,2048]{1,0:T(8,128)(2,1)} %up_w_ref.1, bf16[128,2048]{1,0:T(8,128)(2,1)} %up_w_ref.1, ...), custom_call_target="tpu_custom_call" | custom-call | bytes 2621440 | tf_op jit(solution)/shard_map/lay_rows/pallas_call | solution.py:173
  11.9 2.8 %select_select_fusion.c_ref = f32[512,1024]{1,0:T(8,128)} fusion(s32[1024]{0:T(1024)S(1)} %bitcast.80, s32[512]{0:T(512)S(1)} %bitcast.87, s32[512]{0:T(512)S(1)} %bitcast.88, s32[512]{0:T(512)S(1)} %bitcast.89, s32[512]{0:T(512)S(1)} %bitcast.86), kind=kLoop, calls=%fused_computation.1 | loop fusion | flops 9961472 | bytes 2109440 | tf_op jit(solution)/shard_map/jit(_where)/select_n | solution.py:744
  15.9 1.7 %collective-permute-start.5 = (bf16[1280,512]{1,0:T(8,128)(2,1)S(1)}, bf16[1280,512]{1,0:T(8,128)(2,1)S(1)}, u32[]{:S(2)}, u32[]{:S(2)}) collective-permute-start(bf16[1280,512]{1,0:T(8,128)(2,1)S(1)} %copy-done), channel_id=1, source_target_pairs={{0,2},{1,3},{2,0},{3,1},{4,6},{5,7},{6,4},{7,5},{8,10},{9,11},{10,... | collective-permute-start | bytes 3932168 | tf_op jit(solution)/shard_map/ppermute | solution.py:48
  18.5 2.2 %log_select_fusion.b_ref = f32[512,1024]{1,0:T(8,128)} fusion(s32[512]{0:T(512)S(1)} %bitcast.82, s32[1024]{0:T(1024)S(1)} %bitcast.81, s32[512]{0:T(512)S(1)} %bitcast.84, s32[512]{0:T(512)S(1)} %bitcast.83), kind=kLoop, calls=%fused_computation | loop fusion | flops 4194304 | bytes 2107392 | tf_op jit(solution)/shard_map/jit(_where)/select_n | solution.py:752
  20.8 6.7 %project.1 = (bf16[512,512]{1,0:T(8,128)(2,1)}, bf16[1024,512]{1,0:T(8,128)(2,1)}, bf16[1024,512]{1,0:T(8,128)(2,1)}, bf16[512,1024]{1,0:T(8,128)(2,1)}, bf16[512,1536]{1,0:T(8,128)(2,1)}, /*index=5*/f32[16,512]{1,0:T(8,128)}) custom-call(s32[1]{0:T(128)} %bitcast.me_ref, bf16[512,512]{1,0:T(8,128)(2,1)} %bitcast.77, ...), custom_call_target="tpu_custom_call" | custom-call | flops 1610612736 | bytes 6000000 | tf_op jit(solution)/shard_map/project/pallas_call | solution.py:227
  27.4 16.5 %attend_forward.1 = (f32[512,512]{1,0:T(8,128)}, f32[512,512]{1,0:T(8,128)}, f32[512,512]{1,0:T(8,128)}, f32[512,512]{1,0:T(8,128)}, bf16[8,512,1024]{2,1,0:T(8,128)(2,1)}, /*index=5*/bf16[8,512,1024]{2,1,0:T(8,128)(2,1)}) custom-call(f32[16,512]{1,0:T(8,128)} %get-tuple-element.94.small_ref, bf16[512,512]{1,0:T(8,128)(2,1)} %get-tuple-element.95.q_ref, ...), custom_call_target="tpu_custom_call" | custom-call | flops 1610612736 | bytes 16777216 | tf_op jit(solution)/shard_map/attend_forward/pallas_call | solution.py:300
  44.0 2.0 %collective-permute-done.5.p2 = bf16[1280,512]{1,0:T(8,128)(2,1)S(1)} collective-permute-done((bf16[1280,512]{1,0:T(8,128)(2,1)S(1)}, bf16[1280,512]{1,0:T(8,128)(2,1)S(1)}, u32[]{:S(2)}, u32[]{:S(2)}) %collective-permute-start.5) | collective-permute-done | bytes 1310752 | tf_op jit(solution)/shard_map/ppermute | solution.py:48
  46.0 3.0 %collective-permute-done.6.p3 = bf16[1280,512]{1,0:T(8,128)(2,1)S(1)} collective-permute-done((bf16[1280,512]{1,0:T(8,128)(2,1)S(1)}, bf16[1280,512]{1,0:T(8,128)(2,1)S(1)}, u32[]{:S(2)}, u32[]{:S(2)}) %collective-permute-start.6) | collective-permute-done | bytes 1310752 | tf_op jit(solution)/shard_map/ppermute | solution.py:48
  50.0 15.1 %middle.1 = (bf16[512,512]{1,0:T(8,128)(2,1)}, f32[512,512]{1,0:T(8,128)}, bf16[512,512]{1,0:T(8,128)(2,1)}, bf16[512,512]{1,0:T(8,128)(2,1)}, f32[8,512]{1,0:T(...) custom-call(s32[1]{0:T(128)} %bitcast.me_ref, ...), custom_call_target="tpu_custom_call" | custom-call | flops 8053063680 | bytes 16000000 | tf_op jit(solution)/shard_map/middle/pallas_call | solution.py:414
  70.3 1.6 %collective-permute-start.12 = (bf16[256,512]{1,0:T(8,128)(2,1)S(1)}, bf16[256,512]{1,0:T(8,128)(2,1)S(1)}, u32[]{:S(2)}, u32[]{:S(2)}) collective-permute-start(bf16[256,512]{1,0:T(8,128)(2,1)S(1)} %dynamic-slice_bitcast_fusion.4), channel_id=1, source_target_pairs={{0,4},{4,0},{1,5},{5,1},{2,6},{6,2},{3,7},{7,3},{8,12},{12,8},{9,1... | collective-permute-start | bytes 786440 | tf_op jit(solution)/shard_map/ppermute | solution.py:48
  72.6 19.5 %attend_backward.1 = (bf16[512,512]{1,0:T(8,128)(2,1)}, bf16[1024,512]{1,0:T(8,128)(2,1)}, bf16[1024,512]{1,0:T(8,128)(2,1)}, f32[4,8,128]{2,1,0:T(8,128)}) custom-call(bf16[512,512]{1,0:T(8,128)(2,1)} %get-tuple-element.95.q_ref, bf16[1024,512]{1,0:T(8,128)(2,1)} %get-tuple-element.96.k_ref, bf16[1024,512]{1,0:T(8,128)(2,1)} %get-tuple-element.97.v_ref, ...), custom_call_target="tpu_custom_call" | custom-call | flops 3221225472 | bytes 16777216 | tf_op jit(solution)/shard_map/attend_backward/pallas_call | solution.py:513
  92.6 1.6 %collective-permute-start.14 = (bf16[384,512]{1,0:T(8,128)(2,1)S(1)}, bf16[384,512]{1,0:T(8,128)(2,1)S(1)}, u32[]{:S(2)}, u32[]{:S(2)}) collective-permute-start(bf16[384,512]{1,0:T(8,128)(2,1)S(1)} %get-tuple-element.169), channel_id=1, source_target_pairs={{0,4},{4,0},{1,5},{5,1},{2,6},{6,2},{3,7},{7,3},{8,12},{12,8},{9,1... | collective-permute-start | bytes 1179656 | tf_op jit(solution)/shard_map/ppermute | solution.py:48
  94.8 4.6 %weight_grads.1 = (bf16[128,1664]{1,0:T(8,128)(2,1)}, bf16[128,1664]{1,0:T(8,128)(2,1)}, bf16[128,1664]{1,0:T(8,128)(2,1)}, bf16[128,1664]{1,0:T(8,128)(2,1)}) custom-call(s32[1]{0:T(128)} %bitcast.me_ref, bf16[512,1024]{1,0:T(8,128)(2,1)} %get-tuple-element.122.turned_ref, bf16[512,512]{1,0:T(8,128)(2,1)} %get-tuple-element.140.gq_ref, ...), custom_call_target="tpu_custom_call" | custom-call | flops 1610612736 | bytes 6000000 | tf_op jit(solution)/shard_map/weight_grads/pallas_call | solution.py:561
  100.0 1.6 %collective-permute-done.15 = bf16[256,512]{1,0:T(8,128)(2,1)S(1)} collective-permute-done((bf16[256,512]{1,0:T(8,128)(2,1)S(1)}, bf16[256,512]{1,0:T(8,128)(2,1)S(1)}, u32[]{:S(2)}, u32[]{:S(2)}) %collective-permute-start.15) | collective-permute-done | bytes 262176 | tf_op jit(solution)/shard_map/ppermute | solution.py:48
  104.1 1.5 collective-permute-start.17
  105.7 4.8 %row_grads.1 = (bf16[512,512]{1,0:T(8,128)(2,1)}, f32[512,512]{1,0:T(8,128)}) custom-call(bf16[512,512]{1,0:T(8,128)(2,1)} %get-tuple-element.140.gq_ref, bf16[1024,512]{1,0:T(8,128)(2,1)} %get-tuple-element.127.gk_ref, bf16[1024,512]{1,0:T(8,128)(2,1)} %get-tuple-element.128.gv_ref, bf16[512,1536]{1,0:T(8,128)(2,1)} %get-tuple-element.141.w_ref), custom_call_target="tpu_custom_call" | custom-call | flops 1610612736 | bytes 6000000 | tf_op jit(solution)/shard_map/row_grads/pallas_call | solution.py:589
  110.5 2.3 %collective-permute-done.17 = bf16[320,512]{1,0:T(8,128)(2,1)S(1)} collective-permute-done((bf16[320,512]{1,0:T(8,128)(2,1)S(1)}, bf16[320,512]{1,0:T(8,128)(2,1)S(1)}, u32[]{:S(2)}, u32[]{:S(2)}) %collective-permute-start.17) | collective-permute-done | bytes 327712 | tf_op jit(solution)/shard_map/ppermute | solution.py:48
  113.8 1.5 collective-permute-start.20
  115.4 2.7 %collective-permute-start.22 = (bf16[320,512]{1,0:T(8,128)(2,1)S(1)}, bf16[320,512]{1,0:T(8,128)(2,1)S(1)}, u32[]{:S(2)}, u32[]{:S(2)}) collective-permute-start(bf16[320,512]{1,0:T(8,128)(2,1)S(1)} %add_convert_fusion.8), channel_id=1, source_target_pairs={{0,16},{8,24},{16,0},{24,8},{1,17},{9,25},{17,1},{25,9},{2,18},{10... | collective-permute-start | bytes 983048 | tf_op jit(solution)/shard_map/ppermute | solution.py:48
  118.1 1.6 %collective-permute-done.20 = bf16[64,1664]{1,0:T(8,128)(2,1)S(1)} collective-permute-done((bf16[64,1664]{1,0:T(8,128)(2,1)S(1)}, bf16[64,1664]{1,0:T(8,128)(2,1)S(1)}, u32[]{:S(2)}, u32[]{:S(2)}) %collective-permute-start.20) | collective-permute-done | bytes 213024 | tf_op jit(solution)/shard_map/ppermute | solution.py:48
  119.8 2.4 %collective-permute-start.23 = (bf16[64,1664]{1,0:T(8,128)(2,1)S(1)}, bf16[64,1664]{1,0:T(8,128)(2,1)S(1)}, u32[]{:S(2)}, u32[]{:S(2)}) collective-permute-start(bf16[64,1664]{1,0:T(8,128)(2,1)S(1)} %fusion.3), channel_id=1, source_target_pairs={{0,8},{8,0},{16,24},{24,16},{1,9},{9,1},{17,25},{25,17},{2,10},{10... | collective-permute-start | bytes 638984 | tf_op jit(solution)/shard_map/ppermute | solution.py:48
  123.6 6.7 %collective-permute-done.23 = bf16[64,1664]{1,0:T(8,128)(2,1)S(1)} collective-permute-done((bf16[64,1664]{1,0:T(8,128)(2,1)S(1)}, bf16[64,1664]{1,0:T(8,128)(2,1)S(1)}, u32[]{:S(2)}, u32[]{:S(2)}) %collective-permute-start.23) | collective-permute-done | bytes 213024 | tf_op jit(solution)/shard_map/ppermute | solution.py:48
  130.4 2.5 %collective-permute-start.24 = (bf16[64,1664]{1,0:T(8,128)(2,1)S(1)}, bf16[64,1664]{1,0:T(8,128)(2,1)S(1)}, u32[]{:S(2)}, u32[]{:S(2)}) collective-permute-start(bf16[64,1664]{1,0:T(8,128)(2,1)S(1)} %add_convert_fusion.10), channel_id=1, source_target_pairs={{0,16},{8,24},{16,0},{24,8},{1,17},{9,25},{17,1},{25,9},{2,18},{10... | collective-permute-start | bytes 638984 | tf_op jit(solution)/shard_map/ppermute | solution.py:48
  133.0 2.5 %collective-permute-start.26 = (bf16[320,512]{1,0:T(8,128)(2,1)S(1)}, bf16[320,512]{1,0:T(8,128)(2,1)S(1)}, u32[]{:S(2)}, u32[]{:S(2)}) collective-permute-start(bf16[320,512]{1,0:T(8,128)(2,1)S(1)} %add_convert_fusion.7.own_a), channel_id=1, source_target_pairs={{0,8},{8,0},{16,24},{24,16},{1,9},{9,1},{17,25},{25,17},{2,10},{10... | collective-permute-start | bytes 983048 | tf_op jit(solution)/shard_map/ppermute | solution.py:48
  135.5 1.5 collective-permute-start.27
  137.0 3.4 %finish.1 = f32[512,512]{1,0:T(8,128)} custom-call(bf16[512,512]{1,0:T(8,128)(2,1)} %bitcast.79, f32[16,512]{1,0:T(8,128)} %get-tuple-element.94.small_ref, f32[512,512]{1,0:T(8,128)} %get-tuple-element.103.gh1_ref, f32[512,512]{1,0:T(8,128)} %get-tuple-element.142.own_ref, bf16[512,512]{1,0:T(8,128)(2,1)S(1)} %collective-permute-done.21.away_ref), custom_call_target="tpu_custom_call" | custom-call | bytes 4000000 | tf_op jit(solution)/shard_map/finish/pallas_call | solution.py:684
  140.5 1.6 %collective-permute-done.24 = bf16[64,1664]{1,0:T(8,128)(2,1)S(1)} collective-permute-done((bf16[64,1664]{1,0:T(8,128)(2,1)S(1)}, bf16[64,1664]{1,0:T(8,128)(2,1)S(1)}, u32[]{:S(2)}, u32[]{:S(2)}) %collective-permute-start.24) | collective-permute-done | bytes 213024 | tf_op jit(solution)/shard_map/ppermute | solution.py:48
  142.6 2.1 %collective-permute-done.26.own_b = bf16[320,512]{1,0:T(8,128)(2,1)S(1)} collective-permute-done((bf16[320,512]{1,0:T(8,128)(2,1)S(1)}, bf16[320,512]{1,0:T(8,128)(2,1)S(1)}, u32[]{:S(2)}, u32[]{:S(2)}) %collective-permute-start.26) | collective-permute-done | bytes 327712 | tf_op jit(solution)/shard_map/ppermute | solution.py:48
  146.7 3.4 %collective-permute-done.29.by_seq = bf16[160,512]{1,0:T(8,128)(2,1)S(1)} collective-permute-done((bf16[160,512]{1,0:T(8,128)(2,1)S(1)}, bf16[160,512]{1,0:T(8,128)(2,1)S(1)}, u32[]{:S(2)}, u32[]{:S(2)}) %collective-permute-start.29) | collective-permute-done | bytes 163872 | tf_op jit(solution)/shard_map/ppermute | solution.py:48
  151.5 3.1 %assemble.1 = (f32[128,512]{1,0:T(8,128)}, f32[128,512]{1,0:T(8,128)}, f32[512,512]{1,0:T(8,128)}, f32[128,2048]{1,0:T(8,128)}, f32[1,128]{1,0:T(1,128)}) custom-call(s32[1]{0:T(128)} %bitcast.32.near_ref, s32[1]{0:T(128)} %bitcast.33.far_ref, bf16[320,512]{1,0:T(8,128)(2,1)S(1)} %add_convert_fusion.7.own_a, ...), custom_call_target="tpu_custom_call" | custom-call | bytes 4000000 | tf_op jit(solution)/shard_map/assemble/pallas_call | solution.py:638
  154.6 2.3 %close.1 = (f32[128,1536]{1,0:T(8,128)}, f32[1,128]{1,0:T(1,128)}, f32[1,128]{1,0:T(1,128)}, f32[1,2]{1,0:T(1,128)}) custom-call(s32[1]{0:T(128)} %bitcast.32.near_ref, bf16[64,1664]{1,0:T(8,128)(2,1)S(1)} %add_convert_fusion.9.own_ref, bf16[64,1664]{1,0:T(8,128)(2,1)S(1)} %collective-permute-done.25.other_ref, bf16[128,1536]{1,0:T(8,128)(2,1)} %w_ref.1, ...), custom_call_target="tpu_custom_call" | custom-call | bytes 2000000 | tf_op jit(solution)/shard_map/close/pallas_call | solution.py:665
  (108 shorter events, 24.7 us)
Async XLA Ops:
  3.0 12.8 %collective-permute-start.1 = (bf16[128,1664]{1,0:T(8,128)(2,1)S(1)}, bf16[128,1664]{1,0:T(8,128)(2,1)S(1)}, u32[]{:S(2)}, u32[]{:S(2)}) collective-permute-start(bf16[128,1664]{1,0:T(8,128)(2,1)S(1)} %pad_maximum_fusion.1.p0), channel_id=1, source_target_pairs={{0,2},{1,3},{2,0},{3,1},{4,6},{5,7},{6,4},{7,5},{8,10},{9,11},{10,... | collective-permute-start | bytes 1277960 | tf_op jit(solution)/shard_map/ppermute | solution.py:48
  6.1 14.7 %collective-permute-start.2 = (bf16[128,1664]{1,0:T(8,128)(2,1)S(1)}, bf16[128,1664]{1,0:T(8,128)(2,1)}, u32[]{:S(2)}, u32[]{:S(2)}) collective-permute-start(bf16[128,1664]{1,0:T(8,128)(2,1)S(1)} %pad_maximum_fusion.1.p0), channel_id=1, source_target_pairs={{0,1},{1,0},{2,3},{3,2},{4,5},{5,4},{6,7},{7,6},{8,9},{9,8},{10,11... | collective-permute-start | bytes 1277960 | tf_op jit(solution)/shard_map/ppermute | solution.py:48
  6.1 14.7 %collective-permute-start = (bf16[512,512]{1,0:T(8,128)(2,1)}, bf16[512,512]{1,0:T(8,128)(2,1)}, u32[]{:S(2)}, u32[]{:S(2)}) collective-permute-start(bf16[512,512]{1,0:T(8,128)(2,1)} %bitcast.76), channel_id=1, source_target_pairs={{0,4},{4,0},{1,5},{5,1},{2,6},{6,2},{3,7},{7,3},{8,12},{12,8},{9,1... | collective-permute-start | bytes 1572872 | tf_op jit(solution)/shard_map/ppermute | solution.py:48
  15.9 30.1 %collective-permute-start.5 = (bf16[1280,512]{1,0:T(8,128)(2,1)S(1)}, bf16[1280,512]{1,0:T(8,128)(2,1)S(1)}, u32[]{:S(2)}, u32[]{:S(2)}) collective-permute-start(bf16[1280,512]{1,0:T(8,128)(2,1)S(1)} %copy-done), channel_id=1, source_target_pairs={{0,2},{1,3},{2,0},{3,1},{4,6},{5,7},{6,4},{7,5},{8,10},{9,11},{10,... | collective-permute-start | bytes 3932168 | tf_op jit(solution)/shard_map/ppermute | solution.py:48
  17.9 2.9 %collective-permute-start.3 = (bf16[128,1664]{1,0:T(8,128)(2,1)S(1)}, bf16[128,1664]{1,0:T(8,128)(2,1)}, u32[]{:S(2)}, u32[]{:S(2)}) collective-permute-start(bf16[128,1664]{1,0:T(8,128)(2,1)S(1)} %collective-permute-done.1.p2), channel_id=1, source_target_pairs={{0,1},{1,0},{2,3},{3,2},{4,5},{5,4},{6,7},{7,6},{8,9},{9,8},{10,11... | collective-permute-start | bytes 1277960 | tf_op jit(solution)/shard_map/ppermute | solution.py:48
  18.0 28.0 %collective-permute-start.4 = (bf16[1280,512]{1,0:T(8,128)(2,1)S(1)}, bf16[1280,512]{1,0:T(8,128)(2,1)S(1)}, u32[]{:S(2)}, u32[]{:S(2)}) collective-permute-start(bf16[1280,512]{1,0:T(8,128)(2,1)S(1)} %copy-done), channel_id=1, source_target_pairs={{0,1},{1,0},{2,3},{3,2},{4,5},{5,4},{6,7},{7,6},{8,9},{9,8},{10,11... | collective-permute-start | bytes 3932168 | tf_op jit(solution)/shard_map/ppermute | solution.py:48
  46.0 3.0 %collective-permute-start.6 = (bf16[1280,512]{1,0:T(8,128)(2,1)S(1)}, bf16[1280,512]{1,0:T(8,128)(2,1)S(1)}, u32[]{:S(2)}, u32[]{:S(2)}) collective-permute-start(bf16[1280,512]{1,0:T(8,128)(2,1)S(1)} %collective-permute-done.5.p2), channel_id=1, source_target_pairs={{0,1},{1,0},{2,3},{3,2},{4,5},{5,4},{6,7},{7,6},{8,9},{9,8},{10,11... | collective-permute-start | bytes 3932168 | tf_op jit(solution)/shard_map/ppermute | solution.py:48
  65.1 2.2 %collective-permute-start.9 = (bf16[512,512]{1,0:T(8,128)(2,1)}, bf16[512,512]{1,0:T(8,128)(2,1)S(1)}, u32[]{:S(2)}, u32[]{:S(2)}) collective-permute-start(bf16[512,512]{1,0:T(8,128)(2,1)} %get-tuple-element.110), channel_id=1, source_target_pairs={{0,1},{1,0},{2,3},{3,2},{4,5},{5,4},{6,7},{7,6},{8,9},{9,8},{10,11... | collective-permute-start | bytes 1572872 | tf_op jit(solution)/shard_map/ppermute | solution.py:48
  65.3 3.2 %collective-permute-start.7 = (bf16[768,512]{1,0:T(8,128)(2,1)}, bf16[768,512]{1,0:T(8,128)(2,1)S(1)}, u32[]{:S(2)}, u32[]{:S(2)}) collective-permute-start(bf16[768,512]{1,0:T(8,128)(2,1)} %get-tuple-element.106), channel_id=1, source_target_pairs={{0,1},{1,0},{2,3},{3,2},{4,5},{5,4},{6,7},{7,6},{8,9},{9,8},{10,11... | collective-permute-start | bytes 2359304 | tf_op jit(solution)/shard_map/ppermute | solution.py:48
  65.7 6.2 %collective-permute-start.8 = (bf16[512,512]{1,0:T(8,128)(2,1)}, bf16[512,512]{1,0:T(8,128)(2,1)S(1)}, u32[]{:S(2)}, u32[]{:S(2)}) collective-permute-start(bf16[512,512]{1,0:T(8,128)(2,1)} %get-tuple-element.108), channel_id=1, source_target_pairs={{0,1},{1,0},{2,3},{3,2},{4,5},{5,4},{6,7},{7,6},{8,9},{9,8},{10,11... | collective-permute-start | bytes 1572872 | tf_op jit(solution)/shard_map/ppermute | solution.py:48
  65.8 26.4 %collective-permute-start.13 = (bf16[768,512]{1,0:T(8,128)(2,1)}, bf16[768,512]{1,0:T(8,128)(2,1)S(1)}, u32[]{:S(2)}, u32[]{:S(2)}) collective-permute-start(bf16[768,512]{1,0:T(8,128)(2,1)} %get-tuple-element.124), channel_id=1, source_target_pairs={{0,1},{1,0},{2,3},{3,2},{4,5},{5,4},{6,7},{7,6},{8,9},{9,8},{10,11... | collective-permute-start | bytes 2359304 | tf_op jit(solution)/shard_map/ppermute | solution.py:48
  68.8 23.4 %collective-permute-start.10 = (bf16[768,512]{1,0:T(8,128)(2,1)S(1)}, bf16[768,512]{1,0:T(8,128)(2,1)S(1)}, u32[]{:S(2)}, u32[]{:S(2)}) collective-permute-start(bf16[768,512]{1,0:T(8,128)(2,1)S(1)} %add_convert_fusion.1), channel_id=1, source_target_pairs={{0,2},{1,3},{2,0},{3,1},{4,6},{5,7},{6,4},{7,5},{8,10},{9,11},{10,... | collective-permute-start | bytes 2359304 | tf_op jit(solution)/shard_map/ppermute | solution.py:48
  70.3 21.9 %collective-permute-start.12 = (bf16[256,512]{1,0:T(8,128)(2,1)S(1)}, bf16[256,512]{1,0:T(8,128)(2,1)S(1)}, u32[]{:S(2)}, u32[]{:S(2)}) collective-permute-start(bf16[256,512]{1,0:T(8,128)(2,1)S(1)} %dynamic-slice_bitcast_fusion.4), channel_id=1, source_target_pairs={{0,4},{4,0},{1,5},{5,1},{2,6},{6,2},{3,7},{7,3},{8,12},{12,8},{9,1... | collective-permute-start | bytes 786440 | tf_op jit(solution)/shard_map/ppermute | solution.py:48
  72.0 20.1 %collective-permute-start.11 = (bf16[256,512]{1,0:T(8,128)(2,1)S(1)}, bf16[256,512]{1,0:T(8,128)(2,1)S(1)}, u32[]{:S(2)}, u32[]{:S(2)}) collective-permute-start(bf16[256,512]{1,0:T(8,128)(2,1)S(1)} %dynamic-slice_bitcast_fusion.5), channel_id=1, source_target_pairs={{0,4},{4,0},{1,5},{5,1},{2,6},{6,2},{3,7},{7,3},{8,12},{12,8},{9,1... | collective-permute-start | bytes 786440 | tf_op jit(solution)/shard_map/ppermute | solution.py:48
  72.6 19.6 %copy-start.1 = (bf16[768,512]{1,0:T(8,128)(2,1)S(1)}, bf16[768,512]{1,0:T(8,128)(2,1)}, u32[]{:S(2)}) copy-start(bf16[768,512]{1,0:T(8,128)(2,1)} %get-tuple-element.123) | copy-start | bytes 2359300
  92.6 10.4 %collective-permute-start.14 = (bf16[384,512]{1,0:T(8,128)(2,1)S(1)}, bf16[384,512]{1,0:T(8,128)(2,1)S(1)}, u32[]{:S(2)}, u32[]{:S(2)}) collective-permute-start(bf16[384,512]{1,0:T(8,128)(2,1)S(1)} %get-tuple-element.169), channel_id=1, source_target_pairs={{0,4},{4,0},{1,5},{5,1},{2,6},{6,2},{3,7},{7,3},{8,12},{12,8},{9,1... | collective-permute-start | bytes 1179656 | tf_op jit(solution)/shard_map/ppermute | solution.py:48
  94.3 7.3 %collective-permute-start.15 = (bf16[256,512]{1,0:T(8,128)(2,1)S(1)}, bf16[256,512]{1,0:T(8,128)(2,1)S(1)}, u32[]{:S(2)}, u32[]{:S(2)}) collective-permute-start(bf16[256,512]{1,0:T(8,128)(2,1)S(1)} %fusion.2), channel_id=1, source_target_pairs={{0,2},{1,3},{2,0},{3,1},{4,6},{5,7},{6,4},{7,5},{8,10},{9,11},{10,... | collective-permute-start | bytes 786440 | tf_op jit(solution)/shard_map/ppermute | solution.py:48
  99.4 3.8 %collective-permute-start.16 = (bf16[128,1664]{1,0:T(8,128)(2,1)}, bf16[128,1664]{1,0:T(8,128)(2,1)S(1)}, u32[]{:S(2)}, u32[]{:S(2)}) collective-permute-start(bf16[128,1664]{1,0:T(8,128)(2,1)} %get-tuple-element.136), channel_id=1, source_target_pairs={{0,1},{1,0},{2,3},{3,2},{4,5},{5,4},{6,7},{7,6},{8,9},{9,8},{10,11... | collective-permute-start | bytes 1277960 | tf_op jit(solution)/shard_map/ppermute | solution.py:48
  99.5 14.1 %collective-permute-start.18 = (bf16[128,1664]{1,0:T(8,128)(2,1)}, bf16[128,1664]{1,0:T(8,128)(2,1)S(1)}, u32[]{:S(2)}, u32[]{:S(2)}) collective-permute-start(bf16[128,1664]{1,0:T(8,128)(2,1)} %get-tuple-element.146), channel_id=1, source_target_pairs={{0,1},{1,0},{2,3},{3,2},{4,5},{5,4},{6,7},{7,6},{8,9},{9,8},{10,11... | collective-permute-start | bytes 1277960 | tf_op jit(solution)/shard_map/ppermute | solution.py:48
  103.4 10.2 %collective-permute-start.19 = (bf16[128,1664]{1,0:T(8,128)(2,1)S(1)}, bf16[128,1664]{1,0:T(8,128)(2,1)S(1)}, u32[]{:S(2)}, u32[]{:S(2)}) collective-permute-start(bf16[128,1664]{1,0:T(8,128)(2,1)S(1)} %add_convert_fusion.5), channel_id=1, source_target_pairs={{0,2},{1,3},{2,0},{3,1},{4,6},{5,7},{6,4},{7,5},{8,10},{9,11},{10,... | collective-permute-start | bytes 1277960 | tf_op jit(solution)/shard_map/ppermute | solution.py:48
  104.1 8.6 %collective-permute-start.17 = (bf16[320,512]{1,0:T(8,128)(2,1)S(1)}, bf16[320,512]{1,0:T(8,128)(2,1)S(1)}, u32[]{:S(2)}, u32[]{:S(2)}) collective-permute-start(bf16[320,512]{1,0:T(8,128)(2,1)S(1)} %get-tuple-element.171), channel_id=1, source_target_pairs={{0,8},{8,0},{16,24},{24,16},{1,9},{9,1},{17,25},{25,17},{2,10},{10... | collective-permute-start | bytes 983048 | tf_op jit(solution)/shard_map/ppermute | solution.py:48
  110.5 11.7 %copy-start.11 = (bf16[512,512]{1,0:T(8,128)(2,1)S(1)}, bf16[512,512]{1,0:T(8,128)(2,1)}, u32[]{:S(2)}) copy-start(bf16[512,512]{1,0:T(8,128)(2,1)} %get-tuple-element.149) | copy-start | bytes 1572868
  113.8 5.9 %collective-permute-start.20 = (bf16[64,1664]{1,0:T(8,128)(2,1)S(1)}, bf16[64,1664]{1,0:T(8,128)(2,1)S(1)}, u32[]{:S(2)}, u32[]{:S(2)}) collective-permute-start(bf16[64,1664]{1,0:T(8,128)(2,1)S(1)} %dynamic-slice_bitcast_fusion.6), channel_id=1, source_target_pairs={{0,4},{4,0},{1,5},{5,1},{2,6},{6,2},{3,7},{7,3},{8,12},{12,8},{9,1... | collective-permute-start | bytes 638984 | tf_op jit(solution)/shard_map/ppermute | solution.py:48
  115.4 14.9 %collective-permute-start.22 = (bf16[320,512]{1,0:T(8,128)(2,1)S(1)}, bf16[320,512]{1,0:T(8,128)(2,1)S(1)}, u32[]{:S(2)}, u32[]{:S(2)}) collective-permute-start(bf16[320,512]{1,0:T(8,128)(2,1)S(1)} %add_convert_fusion.8), channel_id=1, source_target_pairs={{0,16},{8,24},{16,0},{24,8},{1,17},{9,25},{17,1},{25,9},{2,18},{10... | collective-permute-start | bytes 983048 | tf_op jit(solution)/shard_map/ppermute | solution.py:48
  119.8 10.6 %collective-permute-start.23 = (bf16[64,1664]{1,0:T(8,128)(2,1)S(1)}, bf16[64,1664]{1,0:T(8,128)(2,1)S(1)}, u32[]{:S(2)}, u32[]{:S(2)}) collective-permute-start(bf16[64,1664]{1,0:T(8,128)(2,1)S(1)} %fusion.3), channel_id=1, source_target_pairs={{0,8},{8,0},{16,24},{24,16},{1,9},{9,1},{17,25},{25,17},{2,10},{10... | collective-permute-start | bytes 638984 | tf_op jit(solution)/shard_map/ppermute | solution.py:48
  122.1 14.9 %collective-permute-start.21 = (bf16[512,512]{1,0:T(8,128)(2,1)S(1)}, bf16[512,512]{1,0:T(8,128)(2,1)S(1)}, u32[]{:S(2)}, u32[]{:S(2)}) collective-permute-start(bf16[512,512]{1,0:T(8,128)(2,1)S(1)} %copy-done.11), channel_id=1, source_target_pairs={{0,4},{4,0},{1,5},{5,1},{2,6},{6,2},{3,7},{7,3},{8,12},{12,8},{9,1... | collective-permute-start | bytes 1572872 | tf_op jit(solution)/shard_map/ppermute | solution.py:48
  130.4 11.6 %collective-permute-start.24 = (bf16[64,1664]{1,0:T(8,128)(2,1)S(1)}, bf16[64,1664]{1,0:T(8,128)(2,1)S(1)}, u32[]{:S(2)}, u32[]{:S(2)}) collective-permute-start(bf16[64,1664]{1,0:T(8,128)(2,1)S(1)} %add_convert_fusion.10), channel_id=1, source_target_pairs={{0,16},{8,24},{16,0},{24,8},{1,17},{9,25},{17,1},{25,9},{2,18},{10... | collective-permute-start | bytes 638984 | tf_op jit(solution)/shard_map/ppermute | solution.py:48
  133.0 11.7 %collective-permute-start.26 = (bf16[320,512]{1,0:T(8,128)(2,1)S(1)}, bf16[320,512]{1,0:T(8,128)(2,1)S(1)}, u32[]{:S(2)}, u32[]{:S(2)}) collective-permute-start(bf16[320,512]{1,0:T(8,128)(2,1)S(1)} %add_convert_fusion.7.own_a), channel_id=1, source_target_pairs={{0,8},{8,0},{16,24},{24,16},{1,9},{9,1},{17,25},{25,17},{2,10},{10... | collective-permute-start | bytes 983048 | tf_op jit(solution)/shard_map/ppermute | solution.py:48
  135.5 9.2 %collective-permute-start.27 = (bf16[320,512]{1,0:T(8,128)(2,1)S(1)}, bf16[320,512]{1,0:T(8,128)(2,1)S(1)}, u32[]{:S(2)}, u32[]{:S(2)}) collective-permute-start(bf16[320,512]{1,0:T(8,128)(2,1)S(1)} %add_convert_fusion.7.own_a), channel_id=1, source_target_pairs={{0,4},{4,0},{1,5},{5,1},{2,6},{6,2},{3,7},{7,3},{8,12},{12,8},{9,1... | collective-permute-start | bytes 983048 | tf_op jit(solution)/shard_map/ppermute | solution.py:48
  142.1 12.5 %collective-permute-start.25 = (bf16[64,1664]{1,0:T(8,128)(2,1)S(1)}, bf16[64,1664]{1,0:T(8,128)(2,1)S(1)}, u32[]{:S(2)}, u32[]{:S(2)}) collective-permute-start(bf16[64,1664]{1,0:T(8,128)(2,1)S(1)} %add_convert_fusion.9.own_ref), channel_id=1, source_target_pairs={{0,4},{4,0},{1,5},{5,1},{2,6},{6,2},{3,7},{7,3},{8,12},{12,8},{9,1... | collective-permute-start | bytes 638984 | tf_op jit(solution)/shard_map/ppermute | solution.py:48
  144.8 5.4 %collective-permute-start.29 = (bf16[160,512]{1,0:T(8,128)(2,1)S(1)}, bf16[160,512]{1,0:T(8,128)(2,1)S(1)}, u32[]{:S(2)}, u32[]{:S(2)}) collective-permute-start(bf16[160,512]{1,0:T(8,128)(2,1)S(1)} %slice.35), channel_id=1, source_target_pairs={{0,8},{8,0},{16,24},{24,16},{1,9},{9,1},{17,25},{25,17},{2,10},{10... | collective-permute-start | bytes 491528 | tf_op jit(solution)/shard_map/ppermute | solution.py:48
  146.0 5.5 %collective-permute-start.28 = (bf16[160,512]{1,0:T(8,128)(2,1)S(1)}, bf16[160,512]{1,0:T(8,128)(2,1)S(1)}, u32[]{:S(2)}, u32[]{:S(2)}) collective-permute-start(bf16[160,512]{1,0:T(8,128)(2,1)S(1)} %slice.34), channel_id=1, source_target_pairs={{0,4},{4,0},{1,5},{5,1},{2,6},{6,2},{3,7},{7,3},{8,12},{12,8},{9,1... | collective-permute-start | bytes 491528 | tf_op jit(solution)/shard_map/ppermute | solution.py:48
  (12 other events, 53.7 us)

commit v3 on v2

--- a/solution.py
+++ b/solution.py
@@ -187,32 +187,35 @@
     width = own_ref.shape[1]
     shard = p0.shape[0]
 
+    copies = []
+    shorts = []
+    for r, pack in enumerate((p0, p1, p2, p3)):
+        place = pl.multiple_of((me_ref[0] ^ r) * shard, shard)
+        copies.append(pltpu.make_async_copy(pack.at[:, 0 : 3 * width], w_ref.at[pl.ds(place, shard), :], sem.at[2 * r]))
+        source = pack.at[0:16, 3 * width : 3 * width + shard]
+        shorts.append(pltpu.make_async_copy(source, few.at[:, pl.ds(place, shard)], sem.at[2 * r + 1]))
+
     @pl.when(step == 0)
     def _():
-        copies = []
-        for r, pack in enumerate((p0, p1, p2, p3)):
-            place = pl.multiple_of((me_ref[0] ^ r) * shard, shard)
-            copies.append(
-                pltpu.make_async_copy(pack.at[:, 0 : 3 * width], w_ref.at[pl.ds(place, shard), :], sem.at[2 * r])
-            )
-            copies.append(
-                pltpu.make_async_copy(
-                    pack.at[0:16, 3 * width : 3 * width + shard], few.at[:, pl.ds(place, shard)], sem.at[2 * r + 1]
-                )
-            )
-        for copy in copies:
+        for copy in shorts + copies:
             copy.start()
+
+    tokens = jnp.where(step == 0, own_ref[...], other_ref[...]).astype(F32)
+    unit, _ = spread(tokens)
+
+    @pl.when(step == 0)
+    def _():
+        for copy in shorts:
+            copy.wait()
+        small_ref[...] = few[...].astype(F32)
+
+    a1 = (unit * few[0:1, :].astype(F32)).astype(BF16)
+    turned_ref[...] = a1.T
+
+    @pl.when(step == 0)
+    def _():
         for copy in copies:
             copy.wait()
-        small_ref[...] = few[...].astype(F32)
-
-    tokens = jnp.where(step == 0, own_ref[...], other_ref[...]).astype(F32)
-    unit, _ = spread(tokens)
-    a1 = (unit * few[0:1, :].astype(F32)).astype(BF16)
-    turned_ref[...] = a1.T
-
-    @pl.when(step == 0)
-    def _():
         q = product(a1, w_ref[:, 0:width]).astype(BF16)
         q_ref[...] = (q.astype(F32) * 0.125).astype(BF16)
 
@@ -442,7 +445,7 @@
             flops=2 * rows * width * width * 3 * 10, transcendentals=4 * rows * width, bytes_accessed=16000000
         ),
         name="middle",
-    )(me, small, tokens, cotangent, o, m, *packs)
+    )(me, small, tokens, cotangent, o, m, *packs[:3], *on_chip(packs[3]))
 
 
 def backward_body(
@@ -810,12 +813,13 @@
         by_ctx = swap(own_b[:cut], "ctx", 1)
         side = lax.axis_index("ctx").astype(jnp.int32).reshape(1)
         pair = side_of("seq", 1).astype(jnp.int32).reshape(1)
-        by_ctx, by_seq = order.arrive(by_ctx, by_seq)
+        by_seq = order.arrive(by_seq)
+        t_qkv, *shorts = close(side, q_sum, order.arrive(q_other), w_qkv, gain_attn, heads_here)
+        order.before = (t_qkv,)
+        by_ctx = order.arrive(by_ctx)
         t_out, t_memory, t_down, t_up, t_gain_two = assemble(
             side, pair, (own_a, own_b, other_a, by_ctx, by_seq), w_up, gain_ffn
         )
-        order.before = (t_gain_two,)
-        t_qkv, *shorts = close(side, q_sum, order.arrive(q_other), w_qkv, gain_attn, heads_here)
         t_gain_one, t_gate, t_slopes, t_gain_two = (value.reshape(-1) for value in (*shorts, t_gain_two))
     else:
         h_far = add_low(h2, swap(h3, "wt", 1))

time: 157 us -> 155 us (0.987)
  transfers between devices with their start and end apart: 30 -> 30, of which waited for: 14 -> 13; matrix products, arithmetic and copies ran while one was open for 6% -> 6% of each run, Pallas kernels for 39% -> 39%
where the time goes in v3:
time: 155 us; the launch traced here: 154 us
  Pallas kernels  78.9 us (51%)
  starting transfers between devices  33.8 us (22%)
  waiting for transfers between devices  28.9 us (19%)
  other arithmetic  10.8 us (7%)
    ppermute x30, starting transfers between devices, swap(): return lax.ppermute(value, axis, [(i, i ^ bit) for i in range(size)])  33.8 us
    ppermute x30, waiting for transfers between devices, swap(): return lax.ppermute(value, axis, [(i, i ^ bit) for i in range(size)])  28.9 us
    pallas_call x1, Pallas kernels, attend_backward(): pl.pallas_call(functools.partial(backward_body, several, 256), grid=(pair...  19.6 us
    pallas_call x1, Pallas kernels, attend_forward(): pl.pallas_call(functools.partial(forward_body, rows), grid=(pairs, row_co...  16.6 us
    pallas_call x1, Pallas kernels, middle(): pl.pallas_call(functools.partial(middle_body, slices), in_specs=[scalar()...  15.1 us
    pallas_call x1, Pallas kernels, project(): pl.pallas_call(project_body, grid=(steps,), in_specs=[scalar(), pl.BlockS...  6.34 us
    pallas_call x1, Pallas kernels, row_grads(): pl.pallas_call(rows_body, in_specs=[vmem] * 4, out_specs=[vmem] * 2, out_...  4.77 us
    pallas_call x1, Pallas kernels, weight_grads(): pl.pallas_call(weights_body, in_specs=[scalar()] + [vmem] * 6, out_specs=...  4.63 us
  transfers between devices with their start and end apart: 30, of which 13 were waited for; matrix products, arithmetic and copies ran while one was open for 6% of the time, Pallas kernels for 39%

profile of v3, /device:TPU:0, one launch (start us, length us, event | category | flops | bytes accessed | tf_op | source)
XLA Modules:
  0.0 154.4 jit_solution(8286647095989804014)
XLA Ops:
  3.0 3.0 %collective-permute-start.1 = (bf16[128,1664]{1,0:T(8,128)(2,1)S(1)}, bf16[128,1664]{1,0:T(8,128)(2,1)S(1)}, u32[]{:S(2)}, u32[]{:S(2)}) collective-permute-start(bf16[128,1664]{1,0:T(8,128)(2,1)S(1)} %pad_maximum_fusion.1.p0), channel_id=1, source_target_pairs={{0,2},{1,3},{2,0},{3,1},{4,6},{5,7},{6,4},{7,5},{8,10},{9,11},{10,... | collective-permute-start | bytes 1277960 | tf_op jit(solution)/shard_map/ppermute | solution.py:48
  8.6 3.1 %lay_rows.1.p0 = bf16[1280,512]{1,0:T(8,128)(2,1)} custom-call(bf16[128,512]{1,0:T(8,128)(2,1)} %refs_0_.1, bf16[128,512]{1,0:T(8,128)(2,1)} %refs_1_.1, bf16[128,2048]{1,0:T(8,128)(2,1)} %up_w_ref.1, bf16[128,2048]{1,0:T(8,128)(2,1)} %up_w_ref.1, bf16[128,2048]{1,0:T(8,128)(2,1)} %up_w_ref.1, bf16[128,2048]{1,0:T(8,128)(2,1)} %up_w_ref.1, ...), custom_call_target="tpu_custom_call" | custom-call | bytes 2621440 | tf_op jit(solution)/shard_map/lay_rows/pallas_call | solution.py:173
  11.9 2.9 %select_select_fusion.c_ref = f32[512,1024]{1,0:T(8,128)} fusion(s32[1024]{0:T(1024)S(1)} %bitcast.80, s32[512]{0:T(512)S(1)} %bitcast.87, s32[512]{0:T(512)S(1)} %bitcast.88, s32[512]{0:T(512)S(1)} %bitcast.89, s32[512]{0:T(512)S(1)} %bitcast.86), kind=kLoop, calls=%fused_computation.1 | loop fusion | flops 9961472 | bytes 2109440 | tf_op jit(solution)/shard_map/jit(_where)/select_n | solution.py:747
  15.9 1.7 %collective-permute-start.5 = (bf16[1280,512]{1,0:T(8,128)(2,1)S(1)}, bf16[1280,512]{1,0:T(8,128)(2,1)S(1)}, u32[]{:S(2)}, u32[]{:S(2)}) collective-permute-start(bf16[1280,512]{1,0:T(8,128)(2,1)S(1)} %copy-done), channel_id=1, source_target_pairs={{0,2},{1,3},{2,0},{3,1},{4,6},{5,7},{6,4},{7,5},{8,10},{9,11},{10,... | collective-permute-start | bytes 3932168 | tf_op jit(solution)/shard_map/ppermute | solution.py:48
  18.5 2.3 %log_select_fusion.b_ref = f32[512,1024]{1,0:T(8,128)} fusion(s32[512]{0:T(512)S(1)} %bitcast.82, s32[1024]{0:T(1024)S(1)} %bitcast.81, s32[512]{0:T(512)S(1)} %bitcast.84, s32[512]{0:T(512)S(1)} %bitcast.83), kind=kLoop, calls=%fused_computation | loop fusion | flops 4194304 | bytes 2107392 | tf_op jit(solution)/shard_map/jit(_where)/select_n | solution.py:755
  20.8 6.3 %project.1 = (bf16[512,512]{1,0:T(8,128)(2,1)}, bf16[1024,512]{1,0:T(8,128)(2,1)}, bf16[1024,512]{1,0:T(8,128)(2,1)}, bf16[512,1024]{1,0:T(8,128)(2,1)}, bf16[512,1536]{1,0:T(8,128)(2,1)}, /*index=5*/f32[16,512]{1,0:T(8,128)}) custom-call(s32[1]{0:T(128)} %bitcast.me_ref, bf16[512,512]{1,0:T(8,128)(2,1)} %bitcast.77, ...), custom_call_target="tpu_custom_call" | custom-call | flops 1610612736 | bytes 6000000 | tf_op jit(solution)/shard_map/project/pallas_call | solution.py:230
  27.1 16.6 %attend_forward.1 = (f32[512,512]{1,0:T(8,128)}, f32[512,512]{1,0:T(8,128)}, f32[512,512]{1,0:T(8,128)}, f32[512,512]{1,0:T(8,128)}, bf16[8,512,1024]{2,1,0:T(8,128)(2,1)}, /*index=5*/bf16[8,512,1024]{2,1,0:T(8,128)(2,1)}) custom-call(f32[16,512]{1,0:T(8,128)} %get-tuple-element.94.small_ref, bf16[512,512]{1,0:T(8,128)(2,1)} %get-tuple-element.95.q_ref, ...), custom_call_target="tpu_custom_call" | custom-call | flops 1610612736 | bytes 16777216 | tf_op jit(solution)/shard_map/attend_forward/pallas_call | solution.py:303
  43.7 2.3 %collective-permute-done.5.p2 = bf16[1280,512]{1,0:T(8,128)(2,1)S(1)} collective-permute-done((bf16[1280,512]{1,0:T(8,128)(2,1)S(1)}, bf16[1280,512]{1,0:T(8,128)(2,1)S(1)}, u32[]{:S(2)}, u32[]{:S(2)}) %collective-permute-start.5) | collective-permute-done | bytes 1310752 | tf_op jit(solution)/shard_map/ppermute | solution.py:48
  46.0 3.0 %collective-permute-done.6.p3 = bf16[1280,512]{1,0:T(8,128)(2,1)S(1)} collective-permute-done((bf16[1280,512]{1,0:T(8,128)(2,1)S(1)}, bf16[1280,512]{1,0:T(8,128)(2,1)S(1)}, u32[]{:S(2)}, u32[]{:S(2)}) %collective-permute-start.6) | collective-permute-done | bytes 1310752 | tf_op jit(solution)/shard_map/ppermute | solution.py:48
  49.0 15.1 %middle.1 = (bf16[512,512]{1,0:T(8,128)(2,1)}, f32[512,512]{1,0:T(8,128)}, bf16[512,512]{1,0:T(8,128)(2,1)}, bf16[512,512]{1,0:T(8,128)(2,1)}, f32[8,512]{1,0:T(...) custom-call(s32[1]{0:T(128)} %bitcast.me_ref, ...), custom_call_target="tpu_custom_call" | custom-call | flops 8053063680 | bytes 16000000 | tf_op jit(solution)/shard_map/middle/pallas_call | solution.py:417
  69.3 1.6 %collective-permute-start.12 = (bf16[256,512]{1,0:T(8,128)(2,1)S(1)}, bf16[256,512]{1,0:T(8,128)(2,1)S(1)}, u32[]{:S(2)}, u32[]{:S(2)}) collective-permute-start(bf16[256,512]{1,0:T(8,128)(2,1)S(1)} %dynamic-slice_bitcast_fusion.4), channel_id=1, source_target_pairs={{0,4},{4,0},{1,5},{5,1},{2,6},{6,2},{3,7},{7,3},{8,12},{12,8},{9,1... | collective-permute-start | bytes 786440 | tf_op jit(solution)/shard_map/ppermute | solution.py:48
  71.7 19.6 %attend_backward.1 = (bf16[512,512]{1,0:T(8,128)(2,1)}, bf16[1024,512]{1,0:T(8,128)(2,1)}, bf16[1024,512]{1,0:T(8,128)(2,1)}, f32[4,8,128]{2,1,0:T(8,128)}) custom-call(bf16[512,512]{1,0:T(8,128)(2,1)} %get-tuple-element.95.q_ref, bf16[1024,512]{1,0:T(8,128)(2,1)} %get-tuple-element.96.k_ref, bf16[1024,512]{1,0:T(8,128)(2,1)} %get-tuple-element.97.v_ref, ...), custom_call_target="tpu_custom_call" | custom-call | flops 3221225472 | bytes 16777216 | tf_op jit(solution)/shard_map/attend_backward/pallas_call | solution.py:516
  91.7 1.6 %collective-permute-start.14 = (bf16[384,512]{1,0:T(8,128)(2,1)S(1)}, bf16[384,512]{1,0:T(8,128)(2,1)S(1)}, u32[]{:S(2)}, u32[]{:S(2)}) collective-permute-start(bf16[384,512]{1,0:T(8,128)(2,1)S(1)} %get-tuple-element.169), channel_id=1, source_target_pairs={{0,4},{4,0},{1,5},{5,1},{2,6},{6,2},{3,7},{7,3},{8,12},{12,8},{9,1... | collective-permute-start | bytes 1179656 | tf_op jit(solution)/shard_map/ppermute | solution.py:48
  93.8 4.6 %weight_grads.1 = (bf16[128,1664]{1,0:T(8,128)(2,1)}, bf16[128,1664]{1,0:T(8,128)(2,1)}, bf16[128,1664]{1,0:T(8,128)(2,1)}, bf16[128,1664]{1,0:T(8,128)(2,1)}) custom-call(s32[1]{0:T(128)} %bitcast.me_ref, bf16[512,1024]{1,0:T(8,128)(2,1)} %get-tuple-element.122.turned_ref, bf16[512,512]{1,0:T(8,128)(2,1)} %get-tuple-element.140.gq_ref, ...), custom_call_target="tpu_custom_call" | custom-call | flops 1610612736 | bytes 6000000 | tf_op jit(solution)/shard_map/weight_grads/pallas_call | solution.py:564
  99.0 1.6 %collective-permute-done.15 = bf16[256,512]{1,0:T(8,128)(2,1)S(1)} collective-permute-done((bf16[256,512]{1,0:T(8,128)(2,1)S(1)}, bf16[256,512]{1,0:T(8,128)(2,1)S(1)}, u32[]{:S(2)}, u32[]{:S(2)}) %collective-permute-start.15) | collective-permute-done | bytes 262176 | tf_op jit(solution)/shard_map/ppermute | solution.py:48
  103.1 1.6 %collective-permute-start.17 = (bf16[320,512]{1,0:T(8,128)(2,1)S(1)}, bf16[320,512]{1,0:T(8,128)(2,1)S(1)}, u32[]{:S(2)}, u32[]{:S(2)}) collective-permute-start(bf16[320,512]{1,0:T(8,128)(2,1)S(1)} %get-tuple-element.171), channel_id=1, source_target_pairs={{0,8},{8,0},{16,24},{24,16},{1,9},{9,1},{17,25},{25,17},{2,10},{10... | collective-permute-start | bytes 983048 | tf_op jit(solution)/shard_map/ppermute | solution.py:48
  104.7 4.8 %row_grads.1 = (bf16[512,512]{1,0:T(8,128)(2,1)}, f32[512,512]{1,0:T(8,128)}) custom-call(bf16[512,512]{1,0:T(8,128)(2,1)} %get-tuple-element.140.gq_ref, bf16[1024,512]{1,0:T(8,128)(2,1)} %get-tuple-element.127.gk_ref, bf16[1024,512]{1,0:T(8,128)(2,1)} %get-tuple-element.128.gv_ref, bf16[512,1536]{1,0:T(8,128)(2,1)} %get-tuple-element.141.w_ref), custom_call_target="tpu_custom_call" | custom-call | flops 1610612736 | bytes 6000000 | tf_op jit(solution)/shard_map/row_grads/pallas_call | solution.py:592
  109.5 2.3 %collective-permute-done.17 = bf16[320,512]{1,0:T(8,128)(2,1)S(1)} collective-permute-done((bf16[320,512]{1,0:T(8,128)(2,1)S(1)}, bf16[320,512]{1,0:T(8,128)(2,1)S(1)}, u32[]{:S(2)}, u32[]{:S(2)}) %collective-permute-start.17) | collective-permute-done | bytes 327712 | tf_op jit(solution)/shard_map/ppermute | solution.py:48
  112.8 1.5 collective-permute-start.20
  114.4 2.7 %collective-permute-start.22 = (bf16[320,512]{1,0:T(8,128)(2,1)S(1)}, bf16[320,512]{1,0:T(8,128)(2,1)S(1)}, u32[]{:S(2)}, u32[]{:S(2)}) collective-permute-start(bf16[320,512]{1,0:T(8,128)(2,1)S(1)} %add_convert_fusion.8), channel_id=1, source_target_pairs={{0,16},{8,24},{16,0},{24,8},{1,17},{9,25},{17,1},{25,9},{2,18},{10... | collective-permute-start | bytes 983048 | tf_op jit(solution)/shard_map/ppermute | solution.py:48
  117.1 1.6 %collective-permute-done.20 = bf16[64,1664]{1,0:T(8,128)(2,1)S(1)} collective-permute-done((bf16[64,1664]{1,0:T(8,128)(2,1)S(1)}, bf16[64,1664]{1,0:T(8,128)(2,1)S(1)}, u32[]{:S(2)}, u32[]{:S(2)}) %collective-permute-start.20) | collective-permute-done | bytes 213024 | tf_op jit(solution)/shard_map/ppermute | solution.py:48
  118.8 2.4 %collective-permute-start.23 = (bf16[64,1664]{1,0:T(8,128)(2,1)S(1)}, bf16[64,1664]{1,0:T(8,128)(2,1)S(1)}, u32[]{:S(2)}, u32[]{:S(2)}) collective-permute-start(bf16[64,1664]{1,0:T(8,128)(2,1)S(1)} %fusion.3), channel_id=1, source_target_pairs={{0,8},{8,0},{16,24},{24,16},{1,9},{9,1},{17,25},{25,17},{2,10},{10... | collective-permute-start | bytes 638984 | tf_op jit(solution)/shard_map/ppermute | solution.py:48
  121.2 1.5 collective-permute-start.21
  122.7 6.6 %collective-permute-done.23 = bf16[64,1664]{1,0:T(8,128)(2,1)S(1)} collective-permute-done((bf16[64,1664]{1,0:T(8,128)(2,1)S(1)}, bf16[64,1664]{1,0:T(8,128)(2,1)S(1)}, u32[]{:S(2)}, u32[]{:S(2)}) %collective-permute-start.23) | collective-permute-done | bytes 213024 | tf_op jit(solution)/shard_map/ppermute | solution.py:48
  129.3 2.6 %collective-permute-start.24 = (bf16[64,1664]{1,0:T(8,128)(2,1)S(1)}, bf16[64,1664]{1,0:T(8,128)(2,1)S(1)}, u32[]{:S(2)}, u32[]{:S(2)}) collective-permute-start(bf16[64,1664]{1,0:T(8,128)(2,1)S(1)} %add_convert_fusion.10), channel_id=1, source_target_pairs={{0,16},{8,24},{16,0},{24,8},{1,17},{9,25},{17,1},{25,9},{2,18},{10... | collective-permute-start | bytes 638984 | tf_op jit(solution)/shard_map/ppermute | solution.py:48
  132.0 2.5 %collective-permute-start.27 = (bf16[320,512]{1,0:T(8,128)(2,1)S(1)}, bf16[320,512]{1,0:T(8,128)(2,1)S(1)}, u32[]{:S(2)}, u32[]{:S(2)}) collective-permute-start(bf16[320,512]{1,0:T(8,128)(2,1)S(1)} %add_convert_fusion.7.own_a), channel_id=1, source_target_pairs={{0,8},{8,0},{16,24},{24,16},{1,9},{9,1},{17,25},{25,17},{2,10},{10... | collective-permute-start | bytes 983048 | tf_op jit(solution)/shard_map/ppermute | solution.py:48
  134.5 1.5 collective-permute-start.26
  136.1 3.4 %finish.1 = f32[512,512]{1,0:T(8,128)} custom-call(bf16[512,512]{1,0:T(8,128)(2,1)} %bitcast.79, f32[16,512]{1,0:T(8,128)} %get-tuple-element.94.small_ref, f32[512,512]{1,0:T(8,128)} %get-tuple-element.103.gh1_ref, f32[512,512]{1,0:T(8,128)} %get-tuple-element.142.own_ref, bf16[512,512]{1,0:T(8,128)(2,1)S(1)} %collective-permute-done.21.away_ref), custom_call_target="tpu_custom_call" | custom-call | bytes 4000000 | tf_op jit(solution)/shard_map/finish/pallas_call | solution.py:687
  141.5 2.2 %collective-permute-done.27.own_b = bf16[320,512]{1,0:T(8,128)(2,1)S(1)} collective-permute-done((bf16[320,512]{1,0:T(8,128)(2,1)S(1)}, bf16[320,512]{1,0:T(8,128)(2,1)S(1)}, u32[]{:S(2)}, u32[]{:S(2)}) %collective-permute-start.27) | collective-permute-done | bytes 327712 | tf_op jit(solution)/shard_map/ppermute | solution.py:48
  145.9 3.2 %collective-permute-done.28.by_seq = bf16[160,512]{1,0:T(8,128)(2,1)S(1)} collective-permute-done((bf16[160,512]{1,0:T(8,128)(2,1)S(1)}, bf16[160,512]{1,0:T(8,128)(2,1)S(1)}, u32[]{:S(2)}, u32[]{:S(2)}) %collective-permute-start.28) | collective-permute-done | bytes 163872 | tf_op jit(solution)/shard_map/ppermute | solution.py:48
  149.0 2.3 %close.1 = (f32[128,1536]{1,0:T(8,128)}, f32[1,128]{1,0:T(1,128)}, f32[1,128]{1,0:T(1,128)}, f32[1,2]{1,0:T(1,128)}) custom-call(s32[1]{0:T(128)} %bitcast.32.near_ref, bf16[64,1664]{1,0:T(8,128)(2,1)S(1)} %add_convert_fusion.9.own_ref, bf16[64,1664]{1,0:T(8,128)(2,1)S(1)} %collective-permute-done.25.other_ref, bf16[128,1536]{1,0:T(8,128)(2,1)} %w_ref.1, ...), custom_call_target="tpu_custom_call" | custom-call | bytes 2000000 | tf_op jit(solution)/shard_map/close/pallas_call | solution.py:668
  151.4 3.1 %assemble.1 = (f32[128,512]{1,0:T(8,128)}, f32[128,512]{1,0:T(8,128)}, f32[512,512]{1,0:T(8,128)}, f32[128,2048]{1,0:T(8,128)}, f32[1,128]{1,0:T(1,128)}) custom-call(s32[1]{0:T(128)} %bitcast.32.near_ref, s32[1]{0:T(128)} %bitcast.33.far_ref, bf16[320,512]{1,0:T(8,128)(2,1)S(1)} %add_convert_fusion.7.own_a, ...), custom_call_target="tpu_custom_call" | custom-call | bytes 4000000 | tf_op jit(solution)/shard_map/assemble/pallas_call | solution.py:641
  (106 shorter events, 22.5 us)
Async XLA Ops:
  3.0 12.8 %collective-permute-start.1 = (bf16[128,1664]{1,0:T(8,128)(2,1)S(1)}, bf16[128,1664]{1,0:T(8,128)(2,1)S(1)}, u32[]{:S(2)}, u32[]{:S(2)}) collective-permute-start(bf16[128,1664]{1,0:T(8,128)(2,1)S(1)} %pad_maximum_fusion.1.p0), channel_id=1, source_target_pairs={{0,2},{1,3},{2,0},{3,1},{4,6},{5,7},{6,4},{7,5},{8,10},{9,11},{10,... | collective-permute-start | bytes 1277960 | tf_op jit(solution)/shard_map/ppermute | solution.py:48
  6.1 14.7 %collective-permute-start.2 = (bf16[128,1664]{1,0:T(8,128)(2,1)S(1)}, bf16[128,1664]{1,0:T(8,128)(2,1)}, u32[]{:S(2)}, u32[]{:S(2)}) collective-permute-start(bf16[128,1664]{1,0:T(8,128)(2,1)S(1)} %pad_maximum_fusion.1.p0), channel_id=1, source_target_pairs={{0,1},{1,0},{2,3},{3,2},{4,5},{5,4},{6,7},{7,6},{8,9},{9,8},{10,11... | collective-permute-start | bytes 1277960 | tf_op jit(solution)/shard_map/ppermute | solution.py:48
  6.1 14.7 %collective-permute-start = (bf16[512,512]{1,0:T(8,128)(2,1)}, bf16[512,512]{1,0:T(8,128)(2,1)}, u32[]{:S(2)}, u32[]{:S(2)}) collective-permute-start(bf16[512,512]{1,0:T(8,128)(2,1)} %bitcast.76), channel_id=1, source_target_pairs={{0,4},{4,0},{1,5},{5,1},{2,6},{6,2},{3,7},{7,3},{8,12},{12,8},{9,1... | collective-permute-start | bytes 1572872 | tf_op jit(solution)/shard_map/ppermute | solution.py:48
  15.9 30.1 %collective-permute-start.5 = (bf16[1280,512]{1,0:T(8,128)(2,1)S(1)}, bf16[1280,512]{1,0:T(8,128)(2,1)S(1)}, u32[]{:S(2)}, u32[]{:S(2)}) collective-permute-start(bf16[1280,512]{1,0:T(8,128)(2,1)S(1)} %copy-done), channel_id=1, source_target_pairs={{0,2},{1,3},{2,0},{3,1},{4,6},{5,7},{6,4},{7,5},{8,10},{9,11},{10,... | collective-permute-start | bytes 3932168 | tf_op jit(solution)/shard_map/ppermute | solution.py:48
  17.9 2.9 %collective-permute-start.3 = (bf16[128,1664]{1,0:T(8,128)(2,1)S(1)}, bf16[128,1664]{1,0:T(8,128)(2,1)}, u32[]{:S(2)}, u32[]{:S(2)}) collective-permute-start(bf16[128,1664]{1,0:T(8,128)(2,1)S(1)} %collective-permute-done.1.p2), channel_id=1, source_target_pairs={{0,1},{1,0},{2,3},{3,2},{4,5},{5,4},{6,7},{7,6},{8,9},{9,8},{10,11... | collective-permute-start | bytes 1277960 | tf_op jit(solution)/shard_map/ppermute | solution.py:48
  18.0 28.0 %collective-permute-start.4 = (bf16[1280,512]{1,0:T(8,128)(2,1)S(1)}, bf16[1280,512]{1,0:T(8,128)(2,1)S(1)}, u32[]{:S(2)}, u32[]{:S(2)}) collective-permute-start(bf16[1280,512]{1,0:T(8,128)(2,1)S(1)} %copy-done), channel_id=1, source_target_pairs={{0,1},{1,0},{2,3},{3,2},{4,5},{5,4},{6,7},{7,6},{8,9},{9,8},{10,11... | collective-permute-start | bytes 3932168 | tf_op jit(solution)/shard_map/ppermute | solution.py:48
  46.0 3.0 %collective-permute-start.6 = (bf16[1280,512]{1,0:T(8,128)(2,1)S(1)}, bf16[1280,512]{1,0:T(8,128)(2,1)S(1)}, u32[]{:S(2)}, u32[]{:S(2)}) collective-permute-start(bf16[1280,512]{1,0:T(8,128)(2,1)S(1)} %collective-permute-done.5.p2), channel_id=1, source_target_pairs={{0,1},{1,0},{2,3},{3,2},{4,5},{5,4},{6,7},{7,6},{8,9},{9,8},{10,11... | collective-permute-start | bytes 3932168 | tf_op jit(solution)/shard_map/ppermute | solution.py:48
  64.2 2.2 %collective-permute-start.9 = (bf16[512,512]{1,0:T(8,128)(2,1)}, bf16[512,512]{1,0:T(8,128)(2,1)S(1)}, u32[]{:S(2)}, u32[]{:S(2)}) collective-permute-start(bf16[512,512]{1,0:T(8,128)(2,1)} %get-tuple-element.110), channel_id=1, source_target_pairs={{0,1},{1,0},{2,3},{3,2},{4,5},{5,4},{6,7},{7,6},{8,9},{9,8},{10,11... | collective-permute-start | bytes 1572872 | tf_op jit(solution)/shard_map/ppermute | solution.py:48
  64.3 3.2 %collective-permute-start.7 = (bf16[768,512]{1,0:T(8,128)(2,1)}, bf16[768,512]{1,0:T(8,128)(2,1)S(1)}, u32[]{:S(2)}, u32[]{:S(2)}) collective-permute-start(bf16[768,512]{1,0:T(8,128)(2,1)} %get-tuple-element.106), channel_id=1, source_target_pairs={{0,1},{1,0},{2,3},{3,2},{4,5},{5,4},{6,7},{7,6},{8,9},{9,8},{10,11... | collective-permute-start | bytes 2359304 | tf_op jit(solution)/shard_map/ppermute | solution.py:48
  64.7 6.2 %collective-permute-start.8 = (bf16[512,512]{1,0:T(8,128)(2,1)}, bf16[512,512]{1,0:T(8,128)(2,1)S(1)}, u32[]{:S(2)}, u32[]{:S(2)}) collective-permute-start(bf16[512,512]{1,0:T(8,128)(2,1)} %get-tuple-element.108), channel_id=1, source_target_pairs={{0,1},{1,0},{2,3},{3,2},{4,5},{5,4},{6,7},{7,6},{8,9},{9,8},{10,11... | collective-permute-start | bytes 1572872 | tf_op jit(solution)/shard_map/ppermute | solution.py:48
  64.8 26.4 %collective-permute-start.13 = (bf16[768,512]{1,0:T(8,128)(2,1)}, bf16[768,512]{1,0:T(8,128)(2,1)S(1)}, u32[]{:S(2)}, u32[]{:S(2)}) collective-permute-start(bf16[768,512]{1,0:T(8,128)(2,1)} %get-tuple-element.124), channel_id=1, source_target_pairs={{0,1},{1,0},{2,3},{3,2},{4,5},{5,4},{6,7},{7,6},{8,9},{9,8},{10,11... | collective-permute-start | bytes 2359304 | tf_op jit(solution)/shard_map/ppermute | solution.py:48
  67.8 23.4 %collective-permute-start.10 = (bf16[768,512]{1,0:T(8,128)(2,1)S(1)}, bf16[768,512]{1,0:T(8,128)(2,1)S(1)}, u32[]{:S(2)}, u32[]{:S(2)}) collective-permute-start(bf16[768,512]{1,0:T(8,128)(2,1)S(1)} %add_convert_fusion.1), channel_id=1, source_target_pairs={{0,2},{1,3},{2,0},{3,1},{4,6},{5,7},{6,4},{7,5},{8,10},{9,11},{10,... | collective-permute-start | bytes 2359304 | tf_op jit(solution)/shard_map/ppermute | solution.py:48
  69.3 21.9 %collective-permute-start.12 = (bf16[256,512]{1,0:T(8,128)(2,1)S(1)}, bf16[256,512]{1,0:T(8,128)(2,1)S(1)}, u32[]{:S(2)}, u32[]{:S(2)}) collective-permute-start(bf16[256,512]{1,0:T(8,128)(2,1)S(1)} %dynamic-slice_bitcast_fusion.4), channel_id=1, source_target_pairs={{0,4},{4,0},{1,5},{5,1},{2,6},{6,2},{3,7},{7,3},{8,12},{12,8},{9,1... | collective-permute-start | bytes 786440 | tf_op jit(solution)/shard_map/ppermute | solution.py:48
  71.1 20.2 %collective-permute-start.11 = (bf16[256,512]{1,0:T(8,128)(2,1)S(1)}, bf16[256,512]{1,0:T(8,128)(2,1)S(1)}, u32[]{:S(2)}, u32[]{:S(2)}) collective-permute-start(bf16[256,512]{1,0:T(8,128)(2,1)S(1)} %dynamic-slice_bitcast_fusion.5), channel_id=1, source_target_pairs={{0,4},{4,0},{1,5},{5,1},{2,6},{6,2},{3,7},{7,3},{8,12},{12,8},{9,1... | collective-permute-start | bytes 786440 | tf_op jit(solution)/shard_map/ppermute | solution.py:48
  71.7 19.6 %copy-start.1 = (bf16[768,512]{1,0:T(8,128)(2,1)S(1)}, bf16[768,512]{1,0:T(8,128)(2,1)}, u32[]{:S(2)}) copy-start(bf16[768,512]{1,0:T(8,128)(2,1)} %get-tuple-element.123) | copy-start | bytes 2359300
  91.7 10.4 %collective-permute-start.14 = (bf16[384,512]{1,0:T(8,128)(2,1)S(1)}, bf16[384,512]{1,0:T(8,128)(2,1)S(1)}, u32[]{:S(2)}, u32[]{:S(2)}) collective-permute-start(bf16[384,512]{1,0:T(8,128)(2,1)S(1)} %get-tuple-element.169), channel_id=1, source_target_pairs={{0,4},{4,0},{1,5},{5,1},{2,6},{6,2},{3,7},{7,3},{8,12},{12,8},{9,1... | collective-permute-start | bytes 1179656 | tf_op jit(solution)/shard_map/ppermute | solution.py:48
  93.3 7.3 %collective-permute-start.15 = (bf16[256,512]{1,0:T(8,128)(2,1)S(1)}, bf16[256,512]{1,0:T(8,128)(2,1)S(1)}, u32[]{:S(2)}, u32[]{:S(2)}) collective-permute-start(bf16[256,512]{1,0:T(8,128)(2,1)S(1)} %fusion.2), channel_id=1, source_target_pairs={{0,2},{1,3},{2,0},{3,1},{4,6},{5,7},{6,4},{7,5},{8,10},{9,11},{10,... | collective-permute-start | bytes 786440 | tf_op jit(solution)/shard_map/ppermute | solution.py:48
  98.5 3.8 %collective-permute-start.16 = (bf16[128,1664]{1,0:T(8,128)(2,1)}, bf16[128,1664]{1,0:T(8,128)(2,1)S(1)}, u32[]{:S(2)}, u32[]{:S(2)}) collective-permute-start(bf16[128,1664]{1,0:T(8,128)(2,1)} %get-tuple-element.136), channel_id=1, source_target_pairs={{0,1},{1,0},{2,3},{3,2},{4,5},{5,4},{6,7},{7,6},{8,9},{9,8},{10,11... | collective-permute-start | bytes 1277960 | tf_op jit(solution)/shard_map/ppermute | solution.py:48
  98.5 14.1 %collective-permute-start.18 = (bf16[128,1664]{1,0:T(8,128)(2,1)}, bf16[128,1664]{1,0:T(8,128)(2,1)S(1)}, u32[]{:S(2)}, u32[]{:S(2)}) collective-permute-start(bf16[128,1664]{1,0:T(8,128)(2,1)} %get-tuple-element.146), channel_id=1, source_target_pairs={{0,1},{1,0},{2,3},{3,2},{4,5},{5,4},{6,7},{7,6},{8,9},{9,8},{10,11... | collective-permute-start | bytes 1277960 | tf_op jit(solution)/shard_map/ppermute | solution.py:48
  102.4 10.2 %collective-permute-start.19 = (bf16[128,1664]{1,0:T(8,128)(2,1)S(1)}, bf16[128,1664]{1,0:T(8,128)(2,1)S(1)}, u32[]{:S(2)}, u32[]{:S(2)}) collective-permute-start(bf16[128,1664]{1,0:T(8,128)(2,1)S(1)} %add_convert_fusion.5), channel_id=1, source_target_pairs={{0,2},{1,3},{2,0},{3,1},{4,6},{5,7},{6,4},{7,5},{8,10},{9,11},{10,... | collective-permute-start | bytes 1277960 | tf_op jit(solution)/shard_map/ppermute | solution.py:48
  103.1 8.6 %collective-permute-start.17 = (bf16[320,512]{1,0:T(8,128)(2,1)S(1)}, bf16[320,512]{1,0:T(8,128)(2,1)S(1)}, u32[]{:S(2)}, u32[]{:S(2)}) collective-permute-start(bf16[320,512]{1,0:T(8,128)(2,1)S(1)} %get-tuple-element.171), channel_id=1, source_target_pairs={{0,8},{8,0},{16,24},{24,16},{1,9},{9,1},{17,25},{25,17},{2,10},{10... | collective-permute-start | bytes 983048 | tf_op jit(solution)/shard_map/ppermute | solution.py:48
  109.5 11.7 %copy-start.10 = (bf16[512,512]{1,0:T(8,128)(2,1)S(1)}, bf16[512,512]{1,0:T(8,128)(2,1)}, u32[]{:S(2)}) copy-start(bf16[512,512]{1,0:T(8,128)(2,1)} %get-tuple-element.149) | copy-start | bytes 1572868
  112.8 5.9 %collective-permute-start.20 = (bf16[64,1664]{1,0:T(8,128)(2,1)S(1)}, bf16[64,1664]{1,0:T(8,128)(2,1)S(1)}, u32[]{:S(2)}, u32[]{:S(2)}) collective-permute-start(bf16[64,1664]{1,0:T(8,128)(2,1)S(1)} %dynamic-slice_bitcast_fusion.6), channel_id=1, source_target_pairs={{0,4},{4,0},{1,5},{5,1},{2,6},{6,2},{3,7},{7,3},{8,12},{12,8},{9,1... | collective-permute-start | bytes 638984 | tf_op jit(solution)/shard_map/ppermute | solution.py:48
  114.4 14.9 %collective-permute-start.22 = (bf16[320,512]{1,0:T(8,128)(2,1)S(1)}, bf16[320,512]{1,0:T(8,128)(2,1)S(1)}, u32[]{:S(2)}, u32[]{:S(2)}) collective-permute-start(bf16[320,512]{1,0:T(8,128)(2,1)S(1)} %add_convert_fusion.8), channel_id=1, source_target_pairs={{0,16},{8,24},{16,0},{24,8},{1,17},{9,25},{17,1},{25,9},{2,18},{10... | collective-permute-start | bytes 983048 | tf_op jit(solution)/shard_map/ppermute | solution.py:48
  118.8 10.5 %collective-permute-start.23 = (bf16[64,1664]{1,0:T(8,128)(2,1)S(1)}, bf16[64,1664]{1,0:T(8,128)(2,1)S(1)}, u32[]{:S(2)}, u32[]{:S(2)}) collective-permute-start(bf16[64,1664]{1,0:T(8,128)(2,1)S(1)} %fusion.3), channel_id=1, source_target_pairs={{0,8},{8,0},{16,24},{24,16},{1,9},{9,1},{17,25},{25,17},{2,10},{10... | collective-permute-start | bytes 638984 | tf_op jit(solution)/shard_map/ppermute | solution.py:48
  121.2 14.9 %collective-permute-start.21 = (bf16[512,512]{1,0:T(8,128)(2,1)S(1)}, bf16[512,512]{1,0:T(8,128)(2,1)S(1)}, u32[]{:S(2)}, u32[]{:S(2)}) collective-permute-start(bf16[512,512]{1,0:T(8,128)(2,1)S(1)} %copy-done.10), channel_id=1, source_target_pairs={{0,4},{4,0},{1,5},{5,1},{2,6},{6,2},{3,7},{7,3},{8,12},{12,8},{9,1... | collective-permute-start | bytes 1572872 | tf_op jit(solution)/shard_map/ppermute | solution.py:48
  129.3 11.6 %collective-permute-start.24 = (bf16[64,1664]{1,0:T(8,128)(2,1)S(1)}, bf16[64,1664]{1,0:T(8,128)(2,1)S(1)}, u32[]{:S(2)}, u32[]{:S(2)}) collective-permute-start(bf16[64,1664]{1,0:T(8,128)(2,1)S(1)} %add_convert_fusion.10), channel_id=1, source_target_pairs={{0,16},{8,24},{16,0},{24,8},{1,17},{9,25},{17,1},{25,9},{2,18},{10... | collective-permute-start | bytes 638984 | tf_op jit(solution)/shard_map/ppermute | solution.py:48
  132.0 11.7 %collective-permute-start.27 = (bf16[320,512]{1,0:T(8,128)(2,1)S(1)}, bf16[320,512]{1,0:T(8,128)(2,1)S(1)}, u32[]{:S(2)}, u32[]{:S(2)}) collective-permute-start(bf16[320,512]{1,0:T(8,128)(2,1)S(1)} %add_convert_fusion.7.own_a), channel_id=1, source_target_pairs={{0,8},{8,0},{16,24},{24,16},{1,9},{9,1},{17,25},{25,17},{2,10},{10... | collective-permute-start | bytes 983048 | tf_op jit(solution)/shard_map/ppermute | solution.py:48
  134.5 9.1 %collective-permute-start.26 = (bf16[320,512]{1,0:T(8,128)(2,1)S(1)}, bf16[320,512]{1,0:T(8,128)(2,1)S(1)}, u32[]{:S(2)}, u32[]{:S(2)}) collective-permute-start(bf16[320,512]{1,0:T(8,128)(2,1)S(1)} %add_convert_fusion.7.own_a), channel_id=1, source_target_pairs={{0,4},{4,0},{1,5},{5,1},{2,6},{6,2},{3,7},{7,3},{8,12},{12,8},{9,1... | collective-permute-start | bytes 983048 | tf_op jit(solution)/shard_map/ppermute | solution.py:48
  141.0 8.0 %collective-permute-start.25 = (bf16[64,1664]{1,0:T(8,128)(2,1)S(1)}, bf16[64,1664]{1,0:T(8,128)(2,1)S(1)}, u32[]{:S(2)}, u32[]{:S(2)}) collective-permute-start(bf16[64,1664]{1,0:T(8,128)(2,1)S(1)} %add_convert_fusion.9.own_ref), channel_id=1, source_target_pairs={{0,4},{4,0},{1,5},{5,1},{2,6},{6,2},{3,7},{7,3},{8,12},{12,8},{9,1... | collective-permute-start | bytes 638984 | tf_op jit(solution)/shard_map/ppermute | solution.py:48
  143.7 5.4 %collective-permute-start.28 = (bf16[160,512]{1,0:T(8,128)(2,1)S(1)}, bf16[160,512]{1,0:T(8,128)(2,1)S(1)}, u32[]{:S(2)}, u32[]{:S(2)}) collective-permute-start(bf16[160,512]{1,0:T(8,128)(2,1)S(1)} %slice.34), channel_id=1, source_target_pairs={{0,8},{8,0},{16,24},{24,16},{1,9},{9,1},{17,25},{25,17},{2,10},{10... | collective-permute-start | bytes 491528 | tf_op jit(solution)/shard_map/ppermute | solution.py:48
  145.0 6.3 %collective-permute-start.29 = (bf16[160,512]{1,0:T(8,128)(2,1)S(1)}, bf16[160,512]{1,0:T(8,128)(2,1)S(1)}, u32[]{:S(2)}, u32[]{:S(2)}) collective-permute-start(bf16[160,512]{1,0:T(8,128)(2,1)S(1)} %slice.35), channel_id=1, source_target_pairs={{0,4},{4,0},{1,5},{5,1},{2,6},{6,2},{3,7},{7,3},{8,12},{12,8},{9,1... | collective-permute-start | bytes 491528 | tf_op jit(solution)/shard_map/ppermute | solution.py:48
  (11 other events, 52.6 us)

commit v4 on v3

--- a/solution.py
+++ b/solution.py
@@ -771,12 +771,13 @@
         h_far = add_low(h2, swap(h3, "wt", 1))
         h_own = add_low(h0, swap(h1, "wt", 1))
         g_got = swap(g_far, "wt", 2)
-        far_keep, far_got = send_half(h_far, "ctx", 1)
-        own_keep, own_got = send_half(h_own, "ctx", 1)
-        gq, gk, gv, gs = attend_backward(q, k, v, hold(go, g_far, h_far, h_own), gm, saved, bias, 0, all_pairs)
-        gq, gk, gv, gs, g_got, far_got, own_got = lax.optimization_barrier(
-            (gq, gk, gv, gs, g_got, far_got, own_got)
-        )
+        both = jnp.concatenate([h_far.reshape(2, -1, width), h_own.reshape(2, -1, width)], axis=1)
+        both_keep, both_got = send_half(both.reshape(-1, width), "ctx", 1)
+        gq, gk, gv, gs = attend_backward(q, k, v, hold(go, g_far, both_keep), gm, saved, bias, 0, all_pairs)
+        gq, gk, gv, gs, g_got, both_got = lax.optimization_barrier((gq, gk, gv, gs, g_got, both_got))
+        cut = both_got.shape[0] // 2
+        far_keep, own_keep = both_keep[:cut], both_keep[cut:]
+        far_got, own_got = both_got[:cut], both_got[cut:]
         h_got = swap(add_low(far_keep, far_got), "wt", 2)
         g_keep, g_near = send_half(add_all(g0, [g_one, g_got]), "ctx", 1)
         q0, q1, q2, q3 = weight_grads(me, turned, hold(gq, g_keep), gk, gv, gs, gate)
@@ -796,9 +797,10 @@
         q_sum = add_low(q_keep, order.arrive(q_got))
         q_got = swap(q_sum, "seq", 1)
         away = swap(hold(near, q_sum), "ctx", 1)
-        q_sum = add_low(q_sum, order.arrive(q_got))
-        q_got = swap(q_sum, "seq", 2)
-        own_a = add_low(gh, order.arrive(gh_got))
+        q_got, gh_got = order.arrive(q_got, gh_got)
+        own_a = add_low(gh, gh_got)
+        q_sum = add_low(q_sum, q_got)
+        q_got = swap(hold(q_sum, own_a), "seq", 2)
         own_b = swap(own_a, "seq", 1)
         other_a = swap(own_a, "ctx", 1)
         away = order.arrive(away)
@@ -813,10 +815,9 @@
         by_ctx = swap(own_b[:cut], "ctx", 1)
         side = lax.axis_index("ctx").astype(jnp.int32).reshape(1)
         pair = side_of("seq", 1).astype(jnp.int32).reshape(1)
-        by_seq = order.arrive(by_seq)
         t_qkv, *shorts = close(side, q_sum, order.arrive(q_other), w_qkv, gain_attn, heads_here)
         order.before = (t_qkv,)
-        by_ctx = order.arrive(by_ctx)
+        by_ctx, by_seq = order.arrive(by_ctx, by_seq)
         t_out, t_memory, t_down, t_up, t_gain_two = assemble(
             side, pair, (own_a, own_b, other_a, by_ctx, by_seq), w_up, gain_ffn
         )

time: 155 us -> 154 us (level)
  starting transfers between devices: 33.8 us -> 29.3 us
  waiting for transfers between devices: 28.9 us -> 32.5 us
    ppermute x30 -> x29, starting transfers between devices: 33.8 us -> 29.3 us  [swap(): return lax.ppermute(value, axis, [(i, i ^ bit) for i in range(size)])]
    ppermute x30 -> x29, waiting for transfers between devices: 28.9 us -> 32.5 us  [swap(): return lax.ppermute(value, axis, [(i, i ^ bit) for i in range(size)])]
  transfers between devices with their start and end apart: 30 -> 29, of which waited for: 13 -> 15; matrix products, arithmetic and copies ran while one was open for 6% -> 6% of each run, Pallas kernels for 39% -> 40%
where the time goes in v4:
time: 154 us
  Pallas kernels  78.9 us (51%)
  waiting for transfers between devices  32.5 us (21%)
  starting transfers between devices  29.3 us (19%)
  other arithmetic  10.8 us (7%)
    ppermute x29, waiting for transfers between devices, swap(): return lax.ppermute(value, axis, [(i, i ^ bit) for i in range(size)])  32.5 us
    ppermute x29, starting transfers between devices, swap(): return lax.ppermute(value, axis, [(i, i ^ bit) for i in range(size)])  29.3 us
    pallas_call x1, Pallas kernels, attend_backward(): pl.pallas_call(functools.partial(backward_body, several, 256), grid=(pair...  19.5 us
    pallas_call x1, Pallas kernels, attend_forward(): pl.pallas_call(functools.partial(forward_body, rows), grid=(pairs, row_co...  16.6 us
    pallas_call x1, Pallas kernels, middle(): pl.pallas_call(functools.partial(middle_body, slices), in_specs=[scalar()...  15.1 us
    pallas_call x1, Pallas kernels, project(): pl.pallas_call(project_body, grid=(steps,), in_specs=[scalar(), pl.BlockS...  6.34 us
    pallas_call x1, Pallas kernels, row_grads(): pl.pallas_call(rows_body, in_specs=[vmem] * 4, out_specs=[vmem] * 2, out_...  4.77 us
    pallas_call x1, Pallas kernels, weight_grads(): pl.pallas_call(weights_body, in_specs=[scalar()] + [vmem] * 6, out_specs=...  4.62 us
  transfers between devices with their start and end apart: 29, of which 15 were waited for; matrix products, arithmetic and copies ran while one was open for 6% of the time, Pallas kernels for 40%

profile of v4, /device:TPU:0, one launch (start us, length us, event | category | flops | bytes accessed | tf_op | source)
XLA Modules:
  0.0 153.6 jit_solution(3468873921888400387)
XLA Ops:
  3.0 3.0 %collective-permute-start.1 = (bf16[128,1664]{1,0:T(8,128)(2,1)S(1)}, bf16[128,1664]{1,0:T(8,128)(2,1)S(1)}, u32[]{:S(2)}, u32[]{:S(2)}) collective-permute-start(bf16[128,1664]{1,0:T(8,128)(2,1)S(1)} %pad_maximum_fusion.1.p0), channel_id=1, source_target_pairs={{0,2},{1,3},{2,0},{3,1},{4,6},{5,7},{6,4},{7,5},{8,10},{9,11},{10,... | collective-permute-start | bytes 1277960 | tf_op jit(solution)/shard_map/ppermute | solution.py:48
  6.1 1.5 collective-permute-start
  8.6 3.1 %lay_rows.1.p0 = bf16[1280,512]{1,0:T(8,128)(2,1)} custom-call(bf16[128,512]{1,0:T(8,128)(2,1)} %refs_0_.1, bf16[128,512]{1,0:T(8,128)(2,1)} %refs_1_.1, bf16[128,2048]{1,0:T(8,128)(2,1)} %up_w_ref.1, bf16[128,2048]{1,0:T(8,128)(2,1)} %up_w_ref.1, bf16[128,2048]{1,0:T(8,128)(2,1)} %up_w_ref.1, bf16[128,2048]{1,0:T(8,128)(2,1)} %up_w_ref.1, ...), custom_call_target="tpu_custom_call" | custom-call | bytes 2621440 | tf_op jit(solution)/shard_map/lay_rows/pallas_call | solution.py:173
  11.9 2.9 %select_select_fusion.c_ref = f32[512,1024]{1,0:T(8,128)} fusion(s32[1024]{0:T(1024)S(1)} %bitcast.80, s32[512]{0:T(512)S(1)} %bitcast.87, s32[512]{0:T(512)S(1)} %bitcast.88, s32[512]{0:T(512)S(1)} %bitcast.89, s32[512]{0:T(512)S(1)} %bitcast.86), kind=kLoop, calls=%fused_computation.1 | loop fusion | flops 9961472 | bytes 2109440 | tf_op jit(solution)/shard_map/jit(_where)/select_n | solution.py:747
  15.9 1.7 %collective-permute-start.5 = (bf16[1280,512]{1,0:T(8,128)(2,1)S(1)}, bf16[1280,512]{1,0:T(8,128)(2,1)S(1)}, u32[]{:S(2)}, u32[]{:S(2)}) collective-permute-start(bf16[1280,512]{1,0:T(8,128)(2,1)S(1)} %copy-done), channel_id=1, source_target_pairs={{0,2},{1,3},{2,0},{3,1},{4,6},{5,7},{6,4},{7,5},{8,10},{9,11},{10,... | collective-permute-start | bytes 3932168 | tf_op jit(solution)/shard_map/ppermute | solution.py:48
  18.5 2.3 %log_select_fusion.b_ref = f32[512,1024]{1,0:T(8,128)} fusion(s32[512]{0:T(512)S(1)} %bitcast.82, s32[1024]{0:T(1024)S(1)} %bitcast.81, s32[512]{0:T(512)S(1)} %bitcast.84, s32[512]{0:T(512)S(1)} %bitcast.83), kind=kLoop, calls=%fused_computation | loop fusion | flops 4194304 | bytes 2107392 | tf_op jit(solution)/shard_map/jit(_where)/select_n | solution.py:755
  20.8 6.3 %project.1 = (bf16[512,512]{1,0:T(8,128)(2,1)}, bf16[1024,512]{1,0:T(8,128)(2,1)}, bf16[1024,512]{1,0:T(8,128)(2,1)}, bf16[512,1024]{1,0:T(8,128)(2,1)}, bf16[512,1536]{1,0:T(8,128)(2,1)}, /*index=5*/f32[16,512]{1,0:T(8,128)}) custom-call(s32[1]{0:T(128)} %bitcast.me_ref, bf16[512,512]{1,0:T(8,128)(2,1)} %bitcast.77, ...), custom_call_target="tpu_custom_call" | custom-call | flops 1610612736 | bytes 6000000 | tf_op jit(solution)/shard_map/project/pallas_call | solution.py:230
  27.1 16.6 %attend_forward.1 = (f32[512,512]{1,0:T(8,128)}, f32[512,512]{1,0:T(8,128)}, f32[512,512]{1,0:T(8,128)}, f32[512,512]{1,0:T(8,128)}, bf16[8,512,1024]{2,1,0:T(8,128)(2,1)}, /*index=5*/bf16[8,512,1024]{2,1,0:T(8,128)(2,1)}) custom-call(f32[16,512]{1,0:T(8,128)} %get-tuple-element.94.small_ref, bf16[512,512]{1,0:T(8,128)(2,1)} %get-tuple-element.95.q_ref, ...), custom_call_target="tpu_custom_call" | custom-call | flops 1610612736 | bytes 16777216 | tf_op jit(solution)/shard_map/attend_forward/pallas_call | solution.py:303
  43.7 2.3 %collective-permute-done.5.p2 = bf16[1280,512]{1,0:T(8,128)(2,1)S(1)} collective-permute-done((bf16[1280,512]{1,0:T(8,128)(2,1)S(1)}, bf16[1280,512]{1,0:T(8,128)(2,1)S(1)}, u32[]{:S(2)}, u32[]{:S(2)}) %collective-permute-start.5) | collective-permute-done | bytes 1310752 | tf_op jit(solution)/shard_map/ppermute | solution.py:48
  46.0 3.0 %collective-permute-done.6.p3 = bf16[1280,512]{1,0:T(8,128)(2,1)S(1)} collective-permute-done((bf16[1280,512]{1,0:T(8,128)(2,1)S(1)}, bf16[1280,512]{1,0:T(8,128)(2,1)S(1)}, u32[]{:S(2)}, u32[]{:S(2)}) %collective-permute-start.6) | collective-permute-done | bytes 1310752 | tf_op jit(solution)/shard_map/ppermute | solution.py:48
  49.0 15.1 %middle.1 = (bf16[512,512]{1,0:T(8,128)(2,1)}, f32[512,512]{1,0:T(8,128)}, bf16[512,512]{1,0:T(8,128)(2,1)}, bf16[512,512]{1,0:T(8,128)(2,1)}, f32[8,512]{1,0:T(...) custom-call(s32[1]{0:T(128)} %bitcast.me_ref, ...), custom_call_target="tpu_custom_call" | custom-call | flops 8053063680 | bytes 16000000 | tf_op jit(solution)/shard_map/middle/pallas_call | solution.py:417
  67.8 1.5 collective-permute-start.8
  69.5 1.5 %collective-permute-start.11 = (bf16[512,512]{1,0:T(8,128)(2,1)S(1)}, bf16[512,512]{1,0:T(8,128)(2,1)S(1)}, u32[]{:S(2)}, u32[]{:S(2)}) collective-permute-start(bf16[512,512]{1,0:T(8,128)(2,1)S(1)} %get-tuple-element.170), channel_id=1, source_target_pairs={{0,4},{4,0},{1,5},{5,1},{2,6},{6,2},{3,7},{7,3},{8,12},{12,8},{9,1... | collective-permute-start | bytes 1572872 | tf_op jit(solution)/shard_map/ppermute | solution.py:48
  71.0 19.5 %attend_backward.1 = (bf16[512,512]{1,0:T(8,128)(2,1)}, bf16[1024,512]{1,0:T(8,128)(2,1)}, bf16[1024,512]{1,0:T(8,128)(2,1)}, f32[4,8,128]{2,1,0:T(8,128)}) custom-call(bf16[512,512]{1,0:T(8,128)(2,1)} %get-tuple-element.95.q_ref, bf16[1024,512]{1,0:T(8,128)(2,1)} %get-tuple-element.96.k_ref, bf16[1024,512]{1,0:T(8,128)(2,1)} %get-tuple-element.97.v_ref, ...), custom_call_target="tpu_custom_call" | custom-call | flops 3221225472 | bytes 16777216 | tf_op jit(solution)/shard_map/attend_backward/pallas_call | solution.py:516
  92.4 4.6 %weight_grads.1 = (bf16[128,1664]{1,0:T(8,128)(2,1)}, bf16[128,1664]{1,0:T(8,128)(2,1)}, bf16[128,1664]{1,0:T(8,128)(2,1)}, bf16[128,1664]{1,0:T(8,128)(2,1)}) custom-call(s32[1]{0:T(128)} %bitcast.me_ref, bf16[512,1024]{1,0:T(8,128)(2,1)} %get-tuple-element.122.turned_ref, bf16[512,512]{1,0:T(8,128)(2,1)} %get-tuple-element.139.gq_ref, ...), custom_call_target="tpu_custom_call" | custom-call | flops 1610612736 | bytes 6000000 | tf_op jit(solution)/shard_map/weight_grads/pallas_call | solution.py:564
  97.5 1.8 %collective-permute-done.14 = bf16[256,512]{1,0:T(8,128)(2,1)S(1)} collective-permute-done((bf16[256,512]{1,0:T(8,128)(2,1)S(1)}, bf16[256,512]{1,0:T(8,128)(2,1)S(1)}, u32[]{:S(2)}, u32[]{:S(2)}) %collective-permute-start.14) | collective-permute-done | bytes 262176 | tf_op jit(solution)/shard_map/ppermute | solution.py:48
  99.3 2.4 %collective-permute-done.13 = bf16[384,512]{1,0:T(8,128)(2,1)S(1)} collective-permute-done((bf16[384,512]{1,0:T(8,128)(2,1)S(1)}, bf16[384,512]{1,0:T(8,128)(2,1)S(1)}, u32[]{:S(2)}, u32[]{:S(2)}) %collective-permute-start.13) | collective-permute-done | bytes 393248 | tf_op jit(solution)/shard_map/ppermute | solution.py:48
  102.8 1.7 %collective-permute-start.16 = (bf16[320,512]{1,0:T(8,128)(2,1)S(1)}, bf16[320,512]{1,0:T(8,128)(2,1)S(1)}, u32[]{:S(2)}, u32[]{:S(2)}) collective-permute-start(bf16[320,512]{1,0:T(8,128)(2,1)S(1)} %get-tuple-element.173), channel_id=1, source_target_pairs={{0,8},{8,0},{16,24},{24,16},{1,9},{9,1},{17,25},{25,17},{2,10},{10... | collective-permute-start | bytes 983048 | tf_op jit(solution)/shard_map/ppermute | solution.py:48
  104.5 4.8 %row_grads.1 = (bf16[512,512]{1,0:T(8,128)(2,1)}, f32[512,512]{1,0:T(8,128)}) custom-call(bf16[512,512]{1,0:T(8,128)(2,1)} %get-tuple-element.139.gq_ref, bf16[1024,512]{1,0:T(8,128)(2,1)} %get-tuple-element.127.gk_ref, bf16[1024,512]{1,0:T(8,128)(2,1)} %get-tuple-element.128.gv_ref, bf16[512,1536]{1,0:T(8,128)(2,1)} %get-tuple-element.140.w_ref), custom_call_target="tpu_custom_call" | custom-call | flops 1610612736 | bytes 6000000 | tf_op jit(solution)/shard_map/row_grads/pallas_call | solution.py:592
  109.3 1.8 %collective-permute-done.16 = bf16[320,512]{1,0:T(8,128)(2,1)S(1)} collective-permute-done((bf16[320,512]{1,0:T(8,128)(2,1)S(1)}, bf16[320,512]{1,0:T(8,128)(2,1)S(1)}, u32[]{:S(2)}, u32[]{:S(2)}) %collective-permute-start.16) | collective-permute-done | bytes 327712 | tf_op jit(solution)/shard_map/ppermute | solution.py:48
  113.4 2.7 %collective-permute-start.22 = (bf16[320,512]{1,0:T(8,128)(2,1)S(1)}, bf16[320,512]{1,0:T(8,128)(2,1)S(1)}, u32[]{:S(2)}, u32[]{:S(2)}) collective-permute-start(bf16[320,512]{1,0:T(8,128)(2,1)S(1)} %add_convert_fusion.8), channel_id=1, source_target_pairs={{0,16},{8,24},{16,0},{24,8},{1,17},{9,25},{17,1},{25,9},{2,18},{10... | collective-permute-start | bytes 983048 | tf_op jit(solution)/shard_map/ppermute | solution.py:48
  116.1 2.6 %collective-permute-done.19 = bf16[64,1664]{1,0:T(8,128)(2,1)S(1)} collective-permute-done((bf16[64,1664]{1,0:T(8,128)(2,1)S(1)}, bf16[64,1664]{1,0:T(8,128)(2,1)S(1)}, u32[]{:S(2)}, u32[]{:S(2)}) %collective-permute-start.19) | collective-permute-done | bytes 213024 | tf_op jit(solution)/shard_map/ppermute | solution.py:48
  118.7 2.2 %collective-permute-start.21 = (bf16[64,1664]{1,0:T(8,128)(2,1)S(1)}, bf16[64,1664]{1,0:T(8,128)(2,1)S(1)}, u32[]{:S(2)}, u32[]{:S(2)}) collective-permute-start(bf16[64,1664]{1,0:T(8,128)(2,1)S(1)} %fusion.6), channel_id=1, source_target_pairs={{0,8},{8,0},{16,24},{24,16},{1,9},{9,1},{17,25},{25,17},{2,10},{10... | collective-permute-start | bytes 638984 | tf_op jit(solution)/shard_map/ppermute | solution.py:48
  121.4 7.2 %collective-permute-done.22 = bf16[320,512]{1,0:T(8,128)(2,1)S(1)} collective-permute-done((bf16[320,512]{1,0:T(8,128)(2,1)S(1)}, bf16[320,512]{1,0:T(8,128)(2,1)S(1)}, u32[]{:S(2)}, u32[]{:S(2)}) %collective-permute-start.22) | collective-permute-done | bytes 327712 | tf_op jit(solution)/shard_map/ppermute | solution.py:48
  129.5 2.2 %collective-permute-start.23 = (bf16[64,1664]{1,0:T(8,128)(2,1)S(1)}, bf16[64,1664]{1,0:T(8,128)(2,1)S(1)}, u32[]{:S(2)}, u32[]{:S(2)}) collective-permute-start(bf16[64,1664]{1,0:T(8,128)(2,1)S(1)} %add_convert_fusion.10), channel_id=1, source_target_pairs={{0,16},{8,24},{16,0},{24,8},{1,17},{9,25},{17,1},{25,9},{2,18},{10... | collective-permute-start | bytes 638984 | tf_op jit(solution)/shard_map/ppermute | solution.py:48
  131.7 2.5 %collective-permute-start.26 = (bf16[320,512]{1,0:T(8,128)(2,1)S(1)}, bf16[320,512]{1,0:T(8,128)(2,1)S(1)}, u32[]{:S(2)}, u32[]{:S(2)}) collective-permute-start(bf16[320,512]{1,0:T(8,128)(2,1)S(1)} %add_convert_fusion.7.own_a), channel_id=1, source_target_pairs={{0,8},{8,0},{16,24},{24,16},{1,9},{9,1},{17,25},{25,17},{2,10},{10... | collective-permute-start | bytes 983048 | tf_op jit(solution)/shard_map/ppermute | solution.py:48
  135.0 3.4 %finish.1 = f32[512,512]{1,0:T(8,128)} custom-call(bf16[512,512]{1,0:T(8,128)(2,1)} %bitcast.79, f32[16,512]{1,0:T(8,128)} %get-tuple-element.94.small_ref, f32[512,512]{1,0:T(8,128)} %get-tuple-element.103.gh1_ref, f32[512,512]{1,0:T(8,128)} %get-tuple-element.141.own_ref, bf16[512,512]{1,0:T(8,128)(2,1)S(1)} %collective-permute-done.20.away_ref), custom_call_target="tpu_custom_call" | custom-call | bytes 4000000 | tf_op jit(solution)/shard_map/finish/pallas_call | solution.py:687
  138.4 2.0 %collective-permute-done.23 = bf16[64,1664]{1,0:T(8,128)(2,1)S(1)} collective-permute-done((bf16[64,1664]{1,0:T(8,128)(2,1)S(1)}, bf16[64,1664]{1,0:T(8,128)(2,1)S(1)}, u32[]{:S(2)}, u32[]{:S(2)}) %collective-permute-start.23) | collective-permute-done | bytes 213024 | tf_op jit(solution)/shard_map/ppermute | solution.py:48
  140.4 1.5 collective-permute-start.24
  145.4 2.7 %collective-permute-done.24.other_ref = bf16[64,1664]{1,0:T(8,128)(2,1)S(1)} collective-permute-done((bf16[64,1664]{1,0:T(8,128)(2,1)S(1)}, bf16[64,1664]{1,0:T(8,128)(2,1)S(1)}, u32[]{:S(2)}, u32[]{:S(2)}) %collective-permute-start.24) | collective-permute-done | bytes 213024 | tf_op jit(solution)/shard_map/ppermute | solution.py:48
  148.2 2.3 %close.1 = (f32[128,1536]{1,0:T(8,128)}, f32[1,128]{1,0:T(1,128)}, f32[1,128]{1,0:T(1,128)}, f32[1,2]{1,0:T(1,128)}) custom-call(s32[1]{0:T(128)} %bitcast.31.near_ref, bf16[64,1664]{1,0:T(8,128)(2,1)S(1)} %add_convert_fusion.9.own_ref, bf16[64,1664]{1,0:T(8,128)(2,1)S(1)} %collective-permute-done.24.other_ref, bf16[128,1536]{1,0:T(8,128)(2,1)} %w_ref.1, ...), custom_call_target="tpu_custom_call" | custom-call | bytes 2000000 | tf_op jit(solution)/shard_map/close/pallas_call | solution.py:668
  150.5 3.1 %assemble.1 = (f32[128,512]{1,0:T(8,128)}, f32[128,512]{1,0:T(8,128)}, f32[512,512]{1,0:T(8,128)}, f32[128,2048]{1,0:T(8,128)}, f32[1,128]{1,0:T(1,128)}) custom-call(s32[1]{0:T(128)} %bitcast.31.near_ref, s32[1]{0:T(128)} %bitcast.32.far_ref, bf16[320,512]{1,0:T(8,128)(2,1)S(1)} %add_convert_fusion.7.own_a, ...), custom_call_target="tpu_custom_call" | custom-call | bytes 4000000 | tf_op jit(solution)/shard_map/assemble/pallas_call | solution.py:641
  (103 shorter events, 20.9 us)
Async XLA Ops:
  3.0 8.7 %copy-start.5 = (bf16[128,1664]{1,0:T(8,128)(2,1)}, bf16[128,1664]{1,0:T(8,128)(2,1)S(1)}, u32[]{:S(2)}) copy-start(bf16[128,1664]{1,0:T(8,128)(2,1)S(1)} %pad_maximum_fusion.1.p0) | copy-start | bytes 1277956
  3.0 12.8 %collective-permute-start.1 = (bf16[128,1664]{1,0:T(8,128)(2,1)S(1)}, bf16[128,1664]{1,0:T(8,128)(2,1)S(1)}, u32[]{:S(2)}, u32[]{:S(2)}) collective-permute-start(bf16[128,1664]{1,0:T(8,128)(2,1)S(1)} %pad_maximum_fusion.1.p0), channel_id=1, source_target_pairs={{0,2},{1,3},{2,0},{3,1},{4,6},{5,7},{6,4},{7,5},{8,10},{9,11},{10,... | collective-permute-start | bytes 1277960 | tf_op jit(solution)/shard_map/ppermute | solution.py:48
  6.1 14.7 %collective-permute-start.2 = (bf16[128,1664]{1,0:T(8,128)(2,1)S(1)}, bf16[128,1664]{1,0:T(8,128)(2,1)}, u32[]{:S(2)}, u32[]{:S(2)}) collective-permute-start(bf16[128,1664]{1,0:T(8,128)(2,1)S(1)} %pad_maximum_fusion.1.p0), channel_id=1, source_target_pairs={{0,1},{1,0},{2,3},{3,2},{4,5},{5,4},{6,7},{7,6},{8,9},{9,8},{10,11... | collective-permute-start | bytes 1277960 | tf_op jit(solution)/shard_map/ppermute | solution.py:48
  6.1 14.7 %collective-permute-start = (bf16[512,512]{1,0:T(8,128)(2,1)}, bf16[512,512]{1,0:T(8,128)(2,1)}, u32[]{:S(2)}, u32[]{:S(2)}) collective-permute-start(bf16[512,512]{1,0:T(8,128)(2,1)} %bitcast.76), channel_id=1, source_target_pairs={{0,4},{4,0},{1,5},{5,1},{2,6},{6,2},{3,7},{7,3},{8,12},{12,8},{9,1... | collective-permute-start | bytes 1572872 | tf_op jit(solution)/shard_map/ppermute | solution.py:48
  15.9 30.1 %collective-permute-start.5 = (bf16[1280,512]{1,0:T(8,128)(2,1)S(1)}, bf16[1280,512]{1,0:T(8,128)(2,1)S(1)}, u32[]{:S(2)}, u32[]{:S(2)}) collective-permute-start(bf16[1280,512]{1,0:T(8,128)(2,1)S(1)} %copy-done), channel_id=1, source_target_pairs={{0,2},{1,3},{2,0},{3,1},{4,6},{5,7},{6,4},{7,5},{8,10},{9,11},{10,... | collective-permute-start | bytes 3932168 | tf_op jit(solution)/shard_map/ppermute | solution.py:48
  17.9 2.9 %collective-permute-start.3 = (bf16[128,1664]{1,0:T(8,128)(2,1)S(1)}, bf16[128,1664]{1,0:T(8,128)(2,1)}, u32[]{:S(2)}, u32[]{:S(2)}) collective-permute-start(bf16[128,1664]{1,0:T(8,128)(2,1)S(1)} %collective-permute-done.1.p2), channel_id=1, source_target_pairs={{0,1},{1,0},{2,3},{3,2},{4,5},{5,4},{6,7},{7,6},{8,9},{9,8},{10,11... | collective-permute-start | bytes 1277960 | tf_op jit(solution)/shard_map/ppermute | solution.py:48
  18.0 28.0 %collective-permute-start.4 = (bf16[1280,512]{1,0:T(8,128)(2,1)S(1)}, bf16[1280,512]{1,0:T(8,128)(2,1)S(1)}, u32[]{:S(2)}, u32[]{:S(2)}) collective-permute-start(bf16[1280,512]{1,0:T(8,128)(2,1)S(1)} %copy-done), channel_id=1, source_target_pairs={{0,1},{1,0},{2,3},{3,2},{4,5},{5,4},{6,7},{7,6},{8,9},{9,8},{10,11... | collective-permute-start | bytes 3932168 | tf_op jit(solution)/shard_map/ppermute | solution.py:48
  46.0 3.0 %collective-permute-start.6 = (bf16[1280,512]{1,0:T(8,128)(2,1)S(1)}, bf16[1280,512]{1,0:T(8,128)(2,1)S(1)}, u32[]{:S(2)}, u32[]{:S(2)}) collective-permute-start(bf16[1280,512]{1,0:T(8,128)(2,1)S(1)} %collective-permute-done.5.p2), channel_id=1, source_target_pairs={{0,1},{1,0},{2,3},{3,2},{4,5},{5,4},{6,7},{7,6},{8,9},{9,8},{10,11... | collective-permute-start | bytes 3932168 | tf_op jit(solution)/shard_map/ppermute | solution.py:48
  64.2 2.2 %collective-permute-start.10 = (bf16[512,512]{1,0:T(8,128)(2,1)}, bf16[512,512]{1,0:T(8,128)(2,1)S(1)}, u32[]{:S(2)}, u32[]{:S(2)}) collective-permute-start(bf16[512,512]{1,0:T(8,128)(2,1)} %get-tuple-element.120), channel_id=1, source_target_pairs={{0,1},{1,0},{2,3},{3,2},{4,5},{5,4},{6,7},{7,6},{8,9},{9,8},{10,11... | collective-permute-start | bytes 1572872 | tf_op jit(solution)/shard_map/ppermute | solution.py:48
  64.3 3.2 %collective-permute-start.7 = (bf16[768,512]{1,0:T(8,128)(2,1)}, bf16[768,512]{1,0:T(8,128)(2,1)S(1)}, u32[]{:S(2)}, u32[]{:S(2)}) collective-permute-start(bf16[768,512]{1,0:T(8,128)(2,1)} %get-tuple-element.106), channel_id=1, source_target_pairs={{0,1},{1,0},{2,3},{3,2},{4,5},{5,4},{6,7},{7,6},{8,9},{9,8},{10,11... | collective-permute-start | bytes 2359304 | tf_op jit(solution)/shard_map/ppermute | solution.py:48
  64.7 4.5 %collective-permute-start.9 = (bf16[512,512]{1,0:T(8,128)(2,1)}, bf16[512,512]{1,0:T(8,128)(2,1)S(1)}, u32[]{:S(2)}, u32[]{:S(2)}) collective-permute-start(bf16[512,512]{1,0:T(8,128)(2,1)} %get-tuple-element.118), channel_id=1, source_target_pairs={{0,1},{1,0},{2,3},{3,2},{4,5},{5,4},{6,7},{7,6},{8,9},{9,8},{10,11... | collective-permute-start | bytes 1572872 | tf_op jit(solution)/shard_map/ppermute | solution.py:48
  64.9 25.7 %collective-permute-start.12 = (bf16[768,512]{1,0:T(8,128)(2,1)}, bf16[768,512]{1,0:T(8,128)(2,1)S(1)}, u32[]{:S(2)}, u32[]{:S(2)}) collective-permute-start(bf16[768,512]{1,0:T(8,128)(2,1)} %get-tuple-element.124), channel_id=1, source_target_pairs={{0,1},{1,0},{2,3},{3,2},{4,5},{5,4},{6,7},{7,6},{8,9},{9,8},{10,11... | collective-permute-start | bytes 2359304 | tf_op jit(solution)/shard_map/ppermute | solution.py:48
  67.8 22.8 %collective-permute-start.8 = (bf16[768,512]{1,0:T(8,128)(2,1)S(1)}, bf16[768,512]{1,0:T(8,128)(2,1)S(1)}, u32[]{:S(2)}, u32[]{:S(2)}) collective-permute-start(bf16[768,512]{1,0:T(8,128)(2,1)S(1)} %add_convert_fusion.1), channel_id=1, source_target_pairs={{0,2},{1,3},{2,0},{3,1},{4,6},{5,7},{6,4},{7,5},{8,10},{9,11},{10,... | collective-permute-start | bytes 2359304 | tf_op jit(solution)/shard_map/ppermute | solution.py:48
  69.5 21.1 %collective-permute-start.11 = (bf16[512,512]{1,0:T(8,128)(2,1)S(1)}, bf16[512,512]{1,0:T(8,128)(2,1)S(1)}, u32[]{:S(2)}, u32[]{:S(2)}) collective-permute-start(bf16[512,512]{1,0:T(8,128)(2,1)S(1)} %get-tuple-element.170), channel_id=1, source_target_pairs={{0,4},{4,0},{1,5},{5,1},{2,6},{6,2},{3,7},{7,3},{8,12},{12,8},{9,1... | collective-permute-start | bytes 1572872 | tf_op jit(solution)/shard_map/ppermute | solution.py:48
  71.0 19.6 %copy-start.1 = (bf16[768,512]{1,0:T(8,128)(2,1)S(1)}, bf16[768,512]{1,0:T(8,128)(2,1)}, u32[]{:S(2)}) copy-start(bf16[768,512]{1,0:T(8,128)(2,1)} %get-tuple-element.123) | copy-start | bytes 2359300
  91.0 10.7 %collective-permute-start.13 = (bf16[384,512]{1,0:T(8,128)(2,1)S(1)}, bf16[384,512]{1,0:T(8,128)(2,1)S(1)}, u32[]{:S(2)}, u32[]{:S(2)}) collective-permute-start(bf16[384,512]{1,0:T(8,128)(2,1)S(1)} %get-tuple-element.171), channel_id=1, source_target_pairs={{0,4},{4,0},{1,5},{5,1},{2,6},{6,2},{3,7},{7,3},{8,12},{12,8},{9,1... | collective-permute-start | bytes 1179656 | tf_op jit(solution)/shard_map/ppermute | solution.py:48
  91.7 7.6 %collective-permute-start.14 = (bf16[256,512]{1,0:T(8,128)(2,1)S(1)}, bf16[256,512]{1,0:T(8,128)(2,1)S(1)}, u32[]{:S(2)}, u32[]{:S(2)}) collective-permute-start(bf16[256,512]{1,0:T(8,128)(2,1)S(1)} %fusion.5), channel_id=1, source_target_pairs={{0,2},{1,3},{2,0},{3,1},{4,6},{5,7},{6,4},{7,5},{8,10},{9,11},{10,... | collective-permute-start | bytes 786440 | tf_op jit(solution)/shard_map/ppermute | solution.py:48
  97.0 5.0 %collective-permute-start.15 = (bf16[128,1664]{1,0:T(8,128)(2,1)}, bf16[128,1664]{1,0:T(8,128)(2,1)S(1)}, u32[]{:S(2)}, u32[]{:S(2)}) collective-permute-start(bf16[128,1664]{1,0:T(8,128)(2,1)} %get-tuple-element.136), channel_id=1, source_target_pairs={{0,1},{1,0},{2,3},{3,2},{4,5},{5,4},{6,7},{7,6},{8,9},{9,8},{10,11... | collective-permute-start | bytes 1277960 | tf_op jit(solution)/shard_map/ppermute | solution.py:48
  97.0 15.5 %collective-permute-start.17 = (bf16[128,1664]{1,0:T(8,128)(2,1)}, bf16[128,1664]{1,0:T(8,128)(2,1)S(1)}, u32[]{:S(2)}, u32[]{:S(2)}) collective-permute-start(bf16[128,1664]{1,0:T(8,128)(2,1)} %get-tuple-element.145), channel_id=1, source_target_pairs={{0,1},{1,0},{2,3},{3,2},{4,5},{5,4},{6,7},{7,6},{8,9},{9,8},{10,11... | collective-permute-start | bytes 1277960 | tf_op jit(solution)/shard_map/ppermute | solution.py:48
  102.1 10.4 %collective-permute-start.18 = (bf16[128,1664]{1,0:T(8,128)(2,1)S(1)}, bf16[128,1664]{1,0:T(8,128)(2,1)S(1)}, u32[]{:S(2)}, u32[]{:S(2)}) collective-permute-start(bf16[128,1664]{1,0:T(8,128)(2,1)S(1)} %add_convert_fusion.5), channel_id=1, source_target_pairs={{0,2},{1,3},{2,0},{3,1},{4,6},{5,7},{6,4},{7,5},{8,10},{9,11},{10,... | collective-permute-start | bytes 1277960 | tf_op jit(solution)/shard_map/ppermute | solution.py:48
  102.8 8.3 %collective-permute-start.16 = (bf16[320,512]{1,0:T(8,128)(2,1)S(1)}, bf16[320,512]{1,0:T(8,128)(2,1)S(1)}, u32[]{:S(2)}, u32[]{:S(2)}) collective-permute-start(bf16[320,512]{1,0:T(8,128)(2,1)S(1)} %get-tuple-element.173), channel_id=1, source_target_pairs={{0,8},{8,0},{16,24},{24,16},{1,9},{9,1},{17,25},{25,17},{2,10},{10... | collective-permute-start | bytes 983048 | tf_op jit(solution)/shard_map/ppermute | solution.py:48
  109.3 11.6 %copy-start.10 = (bf16[512,512]{1,0:T(8,128)(2,1)S(1)}, bf16[512,512]{1,0:T(8,128)(2,1)}, u32[]{:S(2)}) copy-start(bf16[512,512]{1,0:T(8,128)(2,1)} %get-tuple-element.148) | copy-start | bytes 1572868
  112.7 5.9 %collective-permute-start.19 = (bf16[64,1664]{1,0:T(8,128)(2,1)S(1)}, bf16[64,1664]{1,0:T(8,128)(2,1)S(1)}, u32[]{:S(2)}, u32[]{:S(2)}) collective-permute-start(bf16[64,1664]{1,0:T(8,128)(2,1)S(1)} %dynamic-slice_bitcast_fusion.4), channel_id=1, source_target_pairs={{0,4},{4,0},{1,5},{5,1},{2,6},{6,2},{3,7},{7,3},{8,12},{12,8},{9,1... | collective-permute-start | bytes 638984 | tf_op jit(solution)/shard_map/ppermute | solution.py:48
  113.4 15.2 %collective-permute-start.22 = (bf16[320,512]{1,0:T(8,128)(2,1)S(1)}, bf16[320,512]{1,0:T(8,128)(2,1)S(1)}, u32[]{:S(2)}, u32[]{:S(2)}) collective-permute-start(bf16[320,512]{1,0:T(8,128)(2,1)S(1)} %add_convert_fusion.8), channel_id=1, source_target_pairs={{0,16},{8,24},{16,0},{24,8},{1,17},{9,25},{17,1},{25,9},{2,18},{10... | collective-permute-start | bytes 983048 | tf_op jit(solution)/shard_map/ppermute | solution.py:48
  118.7 10.7 %collective-permute-start.21 = (bf16[64,1664]{1,0:T(8,128)(2,1)S(1)}, bf16[64,1664]{1,0:T(8,128)(2,1)S(1)}, u32[]{:S(2)}, u32[]{:S(2)}) collective-permute-start(bf16[64,1664]{1,0:T(8,128)(2,1)S(1)} %fusion.6), channel_id=1, source_target_pairs={{0,8},{8,0},{16,24},{24,16},{1,9},{9,1},{17,25},{25,17},{2,10},{10... | collective-permute-start | bytes 638984 | tf_op jit(solution)/shard_map/ppermute | solution.py:48
  120.8 14.1 %collective-permute-start.20 = (bf16[512,512]{1,0:T(8,128)(2,1)S(1)}, bf16[512,512]{1,0:T(8,128)(2,1)S(1)}, u32[]{:S(2)}, u32[]{:S(2)}) collective-permute-start(bf16[512,512]{1,0:T(8,128)(2,1)S(1)} %copy-done.10), channel_id=1, source_target_pairs={{0,4},{4,0},{1,5},{5,1},{2,6},{6,2},{3,7},{7,3},{8,12},{12,8},{9,1... | collective-permute-start | bytes 1572872 | tf_op jit(solution)/shard_map/ppermute | solution.py:48
  129.5 10.8 %collective-permute-start.23 = (bf16[64,1664]{1,0:T(8,128)(2,1)S(1)}, bf16[64,1664]{1,0:T(8,128)(2,1)S(1)}, u32[]{:S(2)}, u32[]{:S(2)}) collective-permute-start(bf16[64,1664]{1,0:T(8,128)(2,1)S(1)} %add_convert_fusion.10), channel_id=1, source_target_pairs={{0,16},{8,24},{16,0},{24,8},{1,17},{9,25},{17,1},{25,9},{2,18},{10... | collective-permute-start | bytes 638984 | tf_op jit(solution)/shard_map/ppermute | solution.py:48
  131.7 11.2 %collective-permute-start.26 = (bf16[320,512]{1,0:T(8,128)(2,1)S(1)}, bf16[320,512]{1,0:T(8,128)(2,1)S(1)}, u32[]{:S(2)}, u32[]{:S(2)}) collective-permute-start(bf16[320,512]{1,0:T(8,128)(2,1)S(1)} %add_convert_fusion.7.own_a), channel_id=1, source_target_pairs={{0,8},{8,0},{16,24},{24,16},{1,9},{9,1},{17,25},{25,17},{2,10},{10... | collective-permute-start | bytes 983048 | tf_op jit(solution)/shard_map/ppermute | solution.py:48
  134.2 9.9 %collective-permute-start.25 = (bf16[320,512]{1,0:T(8,128)(2,1)S(1)}, bf16[320,512]{1,0:T(8,128)(2,1)S(1)}, u32[]{:S(2)}, u32[]{:S(2)}) collective-permute-start(bf16[320,512]{1,0:T(8,128)(2,1)S(1)} %add_convert_fusion.7.own_a), channel_id=1, source_target_pairs={{0,4},{4,0},{1,5},{5,1},{2,6},{6,2},{3,7},{7,3},{8,12},{12,8},{9,1... | collective-permute-start | bytes 983048 | tf_op jit(solution)/shard_map/ppermute | solution.py:48
  140.4 7.8 %collective-permute-start.24 = (bf16[64,1664]{1,0:T(8,128)(2,1)S(1)}, bf16[64,1664]{1,0:T(8,128)(2,1)S(1)}, u32[]{:S(2)}, u32[]{:S(2)}) collective-permute-start(bf16[64,1664]{1,0:T(8,128)(2,1)S(1)} %add_convert_fusion.9.own_ref), channel_id=1, source_target_pairs={{0,4},{4,0},{1,5},{5,1},{2,6},{6,2},{3,7},{7,3},{8,12},{12,8},{9,1... | collective-permute-start | bytes 638984 | tf_op jit(solution)/shard_map/ppermute | solution.py:48
  144.1 6.4 %collective-permute-start.28 = (bf16[160,512]{1,0:T(8,128)(2,1)S(1)}, bf16[160,512]{1,0:T(8,128)(2,1)S(1)}, u32[]{:S(2)}, u32[]{:S(2)}) collective-permute-start(bf16[160,512]{1,0:T(8,128)(2,1)S(1)} %slice.53), channel_id=1, source_target_pairs={{0,8},{8,0},{16,24},{24,16},{1,9},{9,1},{17,25},{25,17},{2,10},{10... | collective-permute-start | bytes 491528 | tf_op jit(solution)/shard_map/ppermute | solution.py:48
  144.5 6.0 %collective-permute-start.27 = (bf16[160,512]{1,0:T(8,128)(2,1)S(1)}, bf16[160,512]{1,0:T(8,128)(2,1)S(1)}, u32[]{:S(2)}, u32[]{:S(2)}) collective-permute-start(bf16[160,512]{1,0:T(8,128)(2,1)S(1)} %slice.52), channel_id=1, source_target_pairs={{0,4},{4,0},{1,5},{5,1},{2,6},{6,2},{3,7},{7,3},{8,12},{12,8},{9,1... | collective-permute-start | bytes 491528 | tf_op jit(solution)/shard_map/ppermute | solution.py:48
  (10 other events, 45.7 us)

commit v5 on v4

--- a/solution.py
+++ b/solution.py
@@ -796,7 +796,7 @@
         q_keep, q_got = send_half(add_all(q0, [q_one, order.arrive(q_far)]), "ctx", 1)
         q_sum = add_low(q_keep, order.arrive(q_got))
         q_got = swap(q_sum, "seq", 1)
-        away = swap(hold(near, q_sum), "ctx", 1)
+        away = swap(hold(near, gh), "ctx", 1)
         q_got, gh_got = order.arrive(q_got, gh_got)
         own_a = add_low(gh, gh_got)
         q_sum = add_low(q_sum, q_got)

time: 154 us -> 154 us (level)
  no operation moved by 1% of the time
where the time goes in v5:
time: 154 us
  Pallas kernels  78.9 us (51%)
  waiting for transfers between devices  32.5 us (21%)
  starting transfers between devices  29.3 us (19%)
  other arithmetic  10.8 us (7%)
    ppermute x29, waiting for transfers between devices, swap(): return lax.ppermute(value, axis, [(i, i ^ bit) for i in range(size)])  32.5 us
    ppermute x29, starting transfers between devices, swap(): return lax.ppermute(value, axis, [(i, i ^ bit) for i in range(size)])  29.3 us
    pallas_call x1, Pallas kernels, attend_backward(): pl.pallas_call(functools.partial(backward_body, several, 256), grid=(pair...  19.5 us
    pallas_call x1, Pallas kernels, attend_forward(): pl.pallas_call(functools.partial(forward_body, rows), grid=(pairs, row_co...  16.6 us
    pallas_call x1, Pallas kernels, middle(): pl.pallas_call(functools.partial(middle_body, slices), in_specs=[scalar()...  15.1 us
    pallas_call x1, Pallas kernels, project(): pl.pallas_call(project_body, grid=(steps,), in_specs=[scalar(), pl.BlockS...  6.34 us
    pallas_call x1, Pallas kernels, row_grads(): pl.pallas_call(rows_body, in_specs=[vmem] * 4, out_specs=[vmem] * 2, out_...  4.77 us
    pallas_call x1, Pallas kernels, weight_grads(): pl.pallas_call(weights_body, in_specs=[scalar()] + [vmem] * 6, out_specs=...  4.62 us
  transfers between devices with their start and end apart: 29, of which 15 were waited for; matrix products, arithmetic and copies ran while one was open for 6% of the time, Pallas kernels for 40%

profile of v5, /device:TPU:0, one launch (start us, length us, event | category | flops | bytes accessed | tf_op | source)
XLA Modules:
  0.0 153.6 jit_solution(3468873921888400387)
XLA Ops:
  3.0 3.0 %collective-permute-start.1 = (bf16[128,1664]{1,0:T(8,128)(2,1)S(1)}, bf16[128,1664]{1,0:T(8,128)(2,1)S(1)}, u32[]{:S(2)}, u32[]{:S(2)}) collective-permute-start(bf16[128,1664]{1,0:T(8,128)(2,1)S(1)} %pad_maximum_fusion.1.p0), channel_id=1, source_target_pairs={{0,2},{1,3},{2,0},{3,1},{4,6},{5,7},{6,4},{7,5},{8,10},{9,11},{10,... | collective-permute-start | bytes 1277960 | tf_op jit(solution)/shard_map/ppermute | solution.py:48
  6.1 1.5 collective-permute-start
  8.6 3.1 %lay_rows.1.p0 = bf16[1280,512]{1,0:T(8,128)(2,1)} custom-call(bf16[128,512]{1,0:T(8,128)(2,1)} %refs_0_.1, bf16[128,512]{1,0:T(8,128)(2,1)} %refs_1_.1, bf16[128,2048]{1,0:T(8,128)(2,1)} %up_w_ref.1, bf16[128,2048]{1,0:T(8,128)(2,1)} %up_w_ref.1, bf16[128,2048]{1,0:T(8,128)(2,1)} %up_w_ref.1, bf16[128,2048]{1,0:T(8,128)(2,1)} %up_w_ref.1, ...), custom_call_target="tpu_custom_call" | custom-call | bytes 2621440 | tf_op jit(solution)/shard_map/lay_rows/pallas_call | solution.py:173
  11.9 2.9 %select_select_fusion.c_ref = f32[512,1024]{1,0:T(8,128)} fusion(s32[1024]{0:T(1024)S(1)} %bitcast.80, s32[512]{0:T(512)S(1)} %bitcast.87, s32[512]{0:T(512)S(1)} %bitcast.88, s32[512]{0:T(512)S(1)} %bitcast.89, s32[512]{0:T(512)S(1)} %bitcast.86), kind=kLoop, calls=%fused_computation.1 | loop fusion | flops 9961472 | bytes 2109440 | tf_op jit(solution)/shard_map/jit(_where)/select_n | solution.py:747
  15.9 1.7 %collective-permute-start.5 = (bf16[1280,512]{1,0:T(8,128)(2,1)S(1)}, bf16[1280,512]{1,0:T(8,128)(2,1)S(1)}, u32[]{:S(2)}, u32[]{:S(2)}) collective-permute-start(bf16[1280,512]{1,0:T(8,128)(2,1)S(1)} %copy-done), channel_id=1, source_target_pairs={{0,2},{1,3},{2,0},{3,1},{4,6},{5,7},{6,4},{7,5},{8,10},{9,11},{10,... | collective-permute-start | bytes 3932168 | tf_op jit(solution)/shard_map/ppermute | solution.py:48
  18.5 2.3 %log_select_fusion.b_ref = f32[512,1024]{1,0:T(8,128)} fusion(s32[512]{0:T(512)S(1)} %bitcast.82, s32[1024]{0:T(1024)S(1)} %bitcast.81, s32[512]{0:T(512)S(1)} %bitcast.84, s32[512]{0:T(512)S(1)} %bitcast.83), kind=kLoop, calls=%fused_computation | loop fusion | flops 4194304 | bytes 2107392 | tf_op jit(solution)/shard_map/jit(_where)/select_n | solution.py:755
  20.8 6.3 %project.1 = (bf16[512,512]{1,0:T(8,128)(2,1)}, bf16[1024,512]{1,0:T(8,128)(2,1)}, bf16[1024,512]{1,0:T(8,128)(2,1)}, bf16[512,1024]{1,0:T(8,128)(2,1)}, bf16[512,1536]{1,0:T(8,128)(2,1)}, /*index=5*/f32[16,512]{1,0:T(8,128)}) custom-call(s32[1]{0:T(128)} %bitcast.me_ref, bf16[512,512]{1,0:T(8,128)(2,1)} %bitcast.77, ...), custom_call_target="tpu_custom_call" | custom-call | flops 1610612736 | bytes 6000000 | tf_op jit(solution)/shard_map/project/pallas_call | solution.py:230
  27.1 16.6 %attend_forward.1 = (f32[512,512]{1,0:T(8,128)}, f32[512,512]{1,0:T(8,128)}, f32[512,512]{1,0:T(8,128)}, f32[512,512]{1,0:T(8,128)}, bf16[8,512,1024]{2,1,0:T(8,128)(2,1)}, /*index=5*/bf16[8,512,1024]{2,1,0:T(8,128)(2,1)}) custom-call(f32[16,512]{1,0:T(8,128)} %get-tuple-element.94.small_ref, bf16[512,512]{1,0:T(8,128)(2,1)} %get-tuple-element.95.q_ref, ...), custom_call_target="tpu_custom_call" | custom-call | flops 1610612736 | bytes 16777216 | tf_op jit(solution)/shard_map/attend_forward/pallas_call | solution.py:303
  43.7 2.3 %collective-permute-done.5.p2 = bf16[1280,512]{1,0:T(8,128)(2,1)S(1)} collective-permute-done((bf16[1280,512]{1,0:T(8,128)(2,1)S(1)}, bf16[1280,512]{1,0:T(8,128)(2,1)S(1)}, u32[]{:S(2)}, u32[]{:S(2)}) %collective-permute-start.5) | collective-permute-done | bytes 1310752 | tf_op jit(solution)/shard_map/ppermute | solution.py:48
  46.0 3.0 %collective-permute-done.6.p3 = bf16[1280,512]{1,0:T(8,128)(2,1)S(1)} collective-permute-done((bf16[1280,512]{1,0:T(8,128)(2,1)S(1)}, bf16[1280,512]{1,0:T(8,128)(2,1)S(1)}, u32[]{:S(2)}, u32[]{:S(2)}) %collective-permute-start.6) | collective-permute-done | bytes 1310752 | tf_op jit(solution)/shard_map/ppermute | solution.py:48
  49.0 15.1 %middle.1 = (bf16[512,512]{1,0:T(8,128)(2,1)}, f32[512,512]{1,0:T(8,128)}, bf16[512,512]{1,0:T(8,128)(2,1)}, bf16[512,512]{1,0:T(8,128)(2,1)}, f32[8,512]{1,0:T(...) custom-call(s32[1]{0:T(128)} %bitcast.me_ref, ...), custom_call_target="tpu_custom_call" | custom-call | flops 8053063680 | bytes 16000000 | tf_op jit(solution)/shard_map/middle/pallas_call | solution.py:417
  67.8 1.5 collective-permute-start.8
  69.5 1.5 %collective-permute-start.11 = (bf16[512,512]{1,0:T(8,128)(2,1)S(1)}, bf16[512,512]{1,0:T(8,128)(2,1)S(1)}, u32[]{:S(2)}, u32[]{:S(2)}) collective-permute-start(bf16[512,512]{1,0:T(8,128)(2,1)S(1)} %get-tuple-element.170), channel_id=1, source_target_pairs={{0,4},{4,0},{1,5},{5,1},{2,6},{6,2},{3,7},{7,3},{8,12},{12,8},{9,1... | collective-permute-start | bytes 1572872 | tf_op jit(solution)/shard_map/ppermute | solution.py:48
  71.0 19.5 %attend_backward.1 = (bf16[512,512]{1,0:T(8,128)(2,1)}, bf16[1024,512]{1,0:T(8,128)(2,1)}, bf16[1024,512]{1,0:T(8,128)(2,1)}, f32[4,8,128]{2,1,0:T(8,128)}) custom-call(bf16[512,512]{1,0:T(8,128)(2,1)} %get-tuple-element.95.q_ref, bf16[1024,512]{1,0:T(8,128)(2,1)} %get-tuple-element.96.k_ref, bf16[1024,512]{1,0:T(8,128)(2,1)} %get-tuple-element.97.v_ref, ...), custom_call_target="tpu_custom_call" | custom-call | flops 3221225472 | bytes 16777216 | tf_op jit(solution)/shard_map/attend_backward/pallas_call | solution.py:516
  92.4 4.6 %weight_grads.1 = (bf16[128,1664]{1,0:T(8,128)(2,1)}, bf16[128,1664]{1,0:T(8,128)(2,1)}, bf16[128,1664]{1,0:T(8,128)(2,1)}, bf16[128,1664]{1,0:T(8,128)(2,1)}) custom-call(s32[1]{0:T(128)} %bitcast.me_ref, bf16[512,1024]{1,0:T(8,128)(2,1)} %get-tuple-element.122.turned_ref, bf16[512,512]{1,0:T(8,128)(2,1)} %get-tuple-element.139.gq_ref, ...), custom_call_target="tpu_custom_call" | custom-call | flops 1610612736 | bytes 6000000 | tf_op jit(solution)/shard_map/weight_grads/pallas_call | solution.py:564
  97.5 1.8 %collective-permute-done.14 = bf16[256,512]{1,0:T(8,128)(2,1)S(1)} collective-permute-done((bf16[256,512]{1,0:T(8,128)(2,1)S(1)}, bf16[256,512]{1,0:T(8,128)(2,1)S(1)}, u32[]{:S(2)}, u32[]{:S(2)}) %collective-permute-start.14) | collective-permute-done | bytes 262176 | tf_op jit(solution)/shard_map/ppermute | solution.py:48
  99.3 2.4 %collective-permute-done.13 = bf16[384,512]{1,0:T(8,128)(2,1)S(1)} collective-permute-done((bf16[384,512]{1,0:T(8,128)(2,1)S(1)}, bf16[384,512]{1,0:T(8,128)(2,1)S(1)}, u32[]{:S(2)}, u32[]{:S(2)}) %collective-permute-start.13) | collective-permute-done | bytes 393248 | tf_op jit(solution)/shard_map/ppermute | solution.py:48
  102.8 1.7 %collective-permute-start.16 = (bf16[320,512]{1,0:T(8,128)(2,1)S(1)}, bf16[320,512]{1,0:T(8,128)(2,1)S(1)}, u32[]{:S(2)}, u32[]{:S(2)}) collective-permute-start(bf16[320,512]{1,0:T(8,128)(2,1)S(1)} %get-tuple-element.173), channel_id=1, source_target_pairs={{0,8},{8,0},{16,24},{24,16},{1,9},{9,1},{17,25},{25,17},{2,10},{10... | collective-permute-start | bytes 983048 | tf_op jit(solution)/shard_map/ppermute | solution.py:48
  104.5 4.8 %row_grads.1 = (bf16[512,512]{1,0:T(8,128)(2,1)}, f32[512,512]{1,0:T(8,128)}) custom-call(bf16[512,512]{1,0:T(8,128)(2,1)} %get-tuple-element.139.gq_ref, bf16[1024,512]{1,0:T(8,128)(2,1)} %get-tuple-element.127.gk_ref, bf16[1024,512]{1,0:T(8,128)(2,1)} %get-tuple-element.128.gv_ref, bf16[512,1536]{1,0:T(8,128)(2,1)} %get-tuple-element.140.w_ref), custom_call_target="tpu_custom_call" | custom-call | flops 1610612736 | bytes 6000000 | tf_op jit(solution)/shard_map/row_grads/pallas_call | solution.py:592
  109.3 1.8 %collective-permute-done.16 = bf16[320,512]{1,0:T(8,128)(2,1)S(1)} collective-permute-done((bf16[320,512]{1,0:T(8,128)(2,1)S(1)}, bf16[320,512]{1,0:T(8,128)(2,1)S(1)}, u32[]{:S(2)}, u32[]{:S(2)}) %collective-permute-start.16) | collective-permute-done | bytes 327712 | tf_op jit(solution)/shard_map/ppermute | solution.py:48
  113.4 2.7 %collective-permute-start.22 = (bf16[320,512]{1,0:T(8,128)(2,1)S(1)}, bf16[320,512]{1,0:T(8,128)(2,1)S(1)}, u32[]{:S(2)}, u32[]{:S(2)}) collective-permute-start(bf16[320,512]{1,0:T(8,128)(2,1)S(1)} %add_convert_fusion.8), channel_id=1, source_target_pairs={{0,16},{8,24},{16,0},{24,8},{1,17},{9,25},{17,1},{25,9},{2,18},{10... | collective-permute-start | bytes 983048 | tf_op jit(solution)/shard_map/ppermute | solution.py:48
  116.1 2.6 %collective-permute-done.20 = bf16[64,1664]{1,0:T(8,128)(2,1)S(1)} collective-permute-done((bf16[64,1664]{1,0:T(8,128)(2,1)S(1)}, bf16[64,1664]{1,0:T(8,128)(2,1)S(1)}, u32[]{:S(2)}, u32[]{:S(2)}) %collective-permute-start.20) | collective-permute-done | bytes 213024 | tf_op jit(solution)/shard_map/ppermute | solution.py:48
  118.7 2.2 %collective-permute-start.21 = (bf16[64,1664]{1,0:T(8,128)(2,1)S(1)}, bf16[64,1664]{1,0:T(8,128)(2,1)S(1)}, u32[]{:S(2)}, u32[]{:S(2)}) collective-permute-start(bf16[64,1664]{1,0:T(8,128)(2,1)S(1)} %fusion.6), channel_id=1, source_target_pairs={{0,8},{8,0},{16,24},{24,16},{1,9},{9,1},{17,25},{25,17},{2,10},{10... | collective-permute-start | bytes 638984 | tf_op jit(solution)/shard_map/ppermute | solution.py:48
  121.4 7.2 %collective-permute-done.22 = bf16[320,512]{1,0:T(8,128)(2,1)S(1)} collective-permute-done((bf16[320,512]{1,0:T(8,128)(2,1)S(1)}, bf16[320,512]{1,0:T(8,128)(2,1)S(1)}, u32[]{:S(2)}, u32[]{:S(2)}) %collective-permute-start.22) | collective-permute-done | bytes 327712 | tf_op jit(solution)/shard_map/ppermute | solution.py:48
  129.5 2.2 %collective-permute-start.23 = (bf16[64,1664]{1,0:T(8,128)(2,1)S(1)}, bf16[64,1664]{1,0:T(8,128)(2,1)S(1)}, u32[]{:S(2)}, u32[]{:S(2)}) collective-permute-start(bf16[64,1664]{1,0:T(8,128)(2,1)S(1)} %add_convert_fusion.10), channel_id=1, source_target_pairs={{0,16},{8,24},{16,0},{24,8},{1,17},{9,25},{17,1},{25,9},{2,18},{10... | collective-permute-start | bytes 638984 | tf_op jit(solution)/shard_map/ppermute | solution.py:48
  131.7 2.5 %collective-permute-start.26 = (bf16[320,512]{1,0:T(8,128)(2,1)S(1)}, bf16[320,512]{1,0:T(8,128)(2,1)S(1)}, u32[]{:S(2)}, u32[]{:S(2)}) collective-permute-start(bf16[320,512]{1,0:T(8,128)(2,1)S(1)} %add_convert_fusion.7.own_a), channel_id=1, source_target_pairs={{0,8},{8,0},{16,24},{24,16},{1,9},{9,1},{17,25},{25,17},{2,10},{10... | collective-permute-start | bytes 983048 | tf_op jit(solution)/shard_map/ppermute | solution.py:48
  135.0 3.4 %finish.1 = f32[512,512]{1,0:T(8,128)} custom-call(bf16[512,512]{1,0:T(8,128)(2,1)} %bitcast.79, f32[16,512]{1,0:T(8,128)} %get-tuple-element.94.small_ref, f32[512,512]{1,0:T(8,128)} %get-tuple-element.103.gh1_ref, f32[512,512]{1,0:T(8,128)} %get-tuple-element.141.own_ref, bf16[512,512]{1,0:T(8,128)(2,1)S(1)} %collective-permute-done.17.away_ref), custom_call_target="tpu_custom_call" | custom-call | bytes 4000000 | tf_op jit(solution)/shard_map/finish/pallas_call | solution.py:687
  138.4 2.0 %collective-permute-done.23 = bf16[64,1664]{1,0:T(8,128)(2,1)S(1)} collective-permute-done((bf16[64,1664]{1,0:T(8,128)(2,1)S(1)}, bf16[64,1664]{1,0:T(8,128)(2,1)S(1)}, u32[]{:S(2)}, u32[]{:S(2)}) %collective-permute-start.23) | collective-permute-done | bytes 213024 | tf_op jit(solution)/shard_map/ppermute | solution.py:48
  140.4 1.5 collective-permute-start.24
  145.4 2.7 %collective-permute-done.24.other_ref = bf16[64,1664]{1,0:T(8,128)(2,1)S(1)} collective-permute-done((bf16[64,1664]{1,0:T(8,128)(2,1)S(1)}, bf16[64,1664]{1,0:T(8,128)(2,1)S(1)}, u32[]{:S(2)}, u32[]{:S(2)}) %collective-permute-start.24) | collective-permute-done | bytes 213024 | tf_op jit(solution)/shard_map/ppermute | solution.py:48
  148.2 2.3 %close.1 = (f32[128,1536]{1,0:T(8,128)}, f32[1,128]{1,0:T(1,128)}, f32[1,128]{1,0:T(1,128)}, f32[1,2]{1,0:T(1,128)}) custom-call(s32[1]{0:T(128)} %bitcast.31.near_ref, bf16[64,1664]{1,0:T(8,128)(2,1)S(1)} %add_convert_fusion.9.own_ref, bf16[64,1664]{1,0:T(8,128)(2,1)S(1)} %collective-permute-done.24.other_ref, bf16[128,1536]{1,0:T(8,128)(2,1)} %w_ref.1, ...), custom_call_target="tpu_custom_call" | custom-call | bytes 2000000 | tf_op jit(solution)/shard_map/close/pallas_call | solution.py:668
  150.5 3.1 %assemble.1 = (f32[128,512]{1,0:T(8,128)}, f32[128,512]{1,0:T(8,128)}, f32[512,512]{1,0:T(8,128)}, f32[128,2048]{1,0:T(8,128)}, f32[1,128]{1,0:T(1,128)}) custom-call(s32[1]{0:T(128)} %bitcast.31.near_ref, s32[1]{0:T(128)} %bitcast.32.far_ref, bf16[320,512]{1,0:T(8,128)(2,1)S(1)} %add_convert_fusion.7.own_a, ...), custom_call_target="tpu_custom_call" | custom-call | bytes 4000000 | tf_op jit(solution)/shard_map/assemble/pallas_call | solution.py:641
  (103 shorter events, 20.9 us)
Async XLA Ops:
  3.0 8.7 %copy-start.5 = (bf16[128,1664]{1,0:T(8,128)(2,1)}, bf16[128,1664]{1,0:T(8,128)(2,1)S(1)}, u32[]{:S(2)}) copy-start(bf16[128,1664]{1,0:T(8,128)(2,1)S(1)} %pad_maximum_fusion.1.p0) | copy-start | bytes 1277956
  3.0 12.8 %collective-permute-start.1 = (bf16[128,1664]{1,0:T(8,128)(2,1)S(1)}, bf16[128,1664]{1,0:T(8,128)(2,1)S(1)}, u32[]{:S(2)}, u32[]{:S(2)}) collective-permute-start(bf16[128,1664]{1,0:T(8,128)(2,1)S(1)} %pad_maximum_fusion.1.p0), channel_id=1, source_target_pairs={{0,2},{1,3},{2,0},{3,1},{4,6},{5,7},{6,4},{7,5},{8,10},{9,11},{10,... | collective-permute-start | bytes 1277960 | tf_op jit(solution)/shard_map/ppermute | solution.py:48
  6.1 14.7 %collective-permute-start.2 = (bf16[128,1664]{1,0:T(8,128)(2,1)S(1)}, bf16[128,1664]{1,0:T(8,128)(2,1)}, u32[]{:S(2)}, u32[]{:S(2)}) collective-permute-start(bf16[128,1664]{1,0:T(8,128)(2,1)S(1)} %pad_maximum_fusion.1.p0), channel_id=1, source_target_pairs={{0,1},{1,0},{2,3},{3,2},{4,5},{5,4},{6,7},{7,6},{8,9},{9,8},{10,11... | collective-permute-start | bytes 1277960 | tf_op jit(solution)/shard_map/ppermute | solution.py:48
  6.1 14.7 %collective-permute-start = (bf16[512,512]{1,0:T(8,128)(2,1)}, bf16[512,512]{1,0:T(8,128)(2,1)}, u32[]{:S(2)}, u32[]{:S(2)}) collective-permute-start(bf16[512,512]{1,0:T(8,128)(2,1)} %bitcast.76), channel_id=1, source_target_pairs={{0,4},{4,0},{1,5},{5,1},{2,6},{6,2},{3,7},{7,3},{8,12},{12,8},{9,1... | collective-permute-start | bytes 1572872 | tf_op jit(solution)/shard_map/ppermute | solution.py:48
  15.9 30.1 %collective-permute-start.5 = (bf16[1280,512]{1,0:T(8,128)(2,1)S(1)}, bf16[1280,512]{1,0:T(8,128)(2,1)S(1)}, u32[]{:S(2)}, u32[]{:S(2)}) collective-permute-start(bf16[1280,512]{1,0:T(8,128)(2,1)S(1)} %copy-done), channel_id=1, source_target_pairs={{0,2},{1,3},{2,0},{3,1},{4,6},{5,7},{6,4},{7,5},{8,10},{9,11},{10,... | collective-permute-start | bytes 3932168 | tf_op jit(solution)/shard_map/ppermute | solution.py:48
  17.9 2.9 %collective-permute-start.3 = (bf16[128,1664]{1,0:T(8,128)(2,1)S(1)}, bf16[128,1664]{1,0:T(8,128)(2,1)}, u32[]{:S(2)}, u32[]{:S(2)}) collective-permute-start(bf16[128,1664]{1,0:T(8,128)(2,1)S(1)} %collective-permute-done.1.p2), channel_id=1, source_target_pairs={{0,1},{1,0},{2,3},{3,2},{4,5},{5,4},{6,7},{7,6},{8,9},{9,8},{10,11... | collective-permute-start | bytes 1277960 | tf_op jit(solution)/shard_map/ppermute | solution.py:48
  18.0 28.0 %collective-permute-start.4 = (bf16[1280,512]{1,0:T(8,128)(2,1)S(1)}, bf16[1280,512]{1,0:T(8,128)(2,1)S(1)}, u32[]{:S(2)}, u32[]{:S(2)}) collective-permute-start(bf16[1280,512]{1,0:T(8,128)(2,1)S(1)} %copy-done), channel_id=1, source_target_pairs={{0,1},{1,0},{2,3},{3,2},{4,5},{5,4},{6,7},{7,6},{8,9},{9,8},{10,11... | collective-permute-start | bytes 3932168 | tf_op jit(solution)/shard_map/ppermute | solution.py:48
  46.0 3.0 %collective-permute-start.6 = (bf16[1280,512]{1,0:T(8,128)(2,1)S(1)}, bf16[1280,512]{1,0:T(8,128)(2,1)S(1)}, u32[]{:S(2)}, u32[]{:S(2)}) collective-permute-start(bf16[1280,512]{1,0:T(8,128)(2,1)S(1)} %collective-permute-done.5.p2), channel_id=1, source_target_pairs={{0,1},{1,0},{2,3},{3,2},{4,5},{5,4},{6,7},{7,6},{8,9},{9,8},{10,11... | collective-permute-start | bytes 3932168 | tf_op jit(solution)/shard_map/ppermute | solution.py:48
  64.2 2.2 %collective-permute-start.10 = (bf16[512,512]{1,0:T(8,128)(2,1)}, bf16[512,512]{1,0:T(8,128)(2,1)S(1)}, u32[]{:S(2)}, u32[]{:S(2)}) collective-permute-start(bf16[512,512]{1,0:T(8,128)(2,1)} %get-tuple-element.120), channel_id=1, source_target_pairs={{0,1},{1,0},{2,3},{3,2},{4,5},{5,4},{6,7},{7,6},{8,9},{9,8},{10,11... | collective-permute-start | bytes 1572872 | tf_op jit(solution)/shard_map/ppermute | solution.py:48
  64.3 3.2 %collective-permute-start.7 = (bf16[768,512]{1,0:T(8,128)(2,1)}, bf16[768,512]{1,0:T(8,128)(2,1)S(1)}, u32[]{:S(2)}, u32[]{:S(2)}) collective-permute-start(bf16[768,512]{1,0:T(8,128)(2,1)} %get-tuple-element.106), channel_id=1, source_target_pairs={{0,1},{1,0},{2,3},{3,2},{4,5},{5,4},{6,7},{7,6},{8,9},{9,8},{10,11... | collective-permute-start | bytes 2359304 | tf_op jit(solution)/shard_map/ppermute | solution.py:48
  64.7 4.5 %collective-permute-start.9 = (bf16[512,512]{1,0:T(8,128)(2,1)}, bf16[512,512]{1,0:T(8,128)(2,1)S(1)}, u32[]{:S(2)}, u32[]{:S(2)}) collective-permute-start(bf16[512,512]{1,0:T(8,128)(2,1)} %get-tuple-element.118), channel_id=1, source_target_pairs={{0,1},{1,0},{2,3},{3,2},{4,5},{5,4},{6,7},{7,6},{8,9},{9,8},{10,11... | collective-permute-start | bytes 1572872 | tf_op jit(solution)/shard_map/ppermute | solution.py:48
  64.9 25.7 %collective-permute-start.12 = (bf16[768,512]{1,0:T(8,128)(2,1)}, bf16[768,512]{1,0:T(8,128)(2,1)S(1)}, u32[]{:S(2)}, u32[]{:S(2)}) collective-permute-start(bf16[768,512]{1,0:T(8,128)(2,1)} %get-tuple-element.124), channel_id=1, source_target_pairs={{0,1},{1,0},{2,3},{3,2},{4,5},{5,4},{6,7},{7,6},{8,9},{9,8},{10,11... | collective-permute-start | bytes 2359304 | tf_op jit(solution)/shard_map/ppermute | solution.py:48
  67.8 22.8 %collective-permute-start.8 = (bf16[768,512]{1,0:T(8,128)(2,1)S(1)}, bf16[768,512]{1,0:T(8,128)(2,1)S(1)}, u32[]{:S(2)}, u32[]{:S(2)}) collective-permute-start(bf16[768,512]{1,0:T(8,128)(2,1)S(1)} %add_convert_fusion.1), channel_id=1, source_target_pairs={{0,2},{1,3},{2,0},{3,1},{4,6},{5,7},{6,4},{7,5},{8,10},{9,11},{10,... | collective-permute-start | bytes 2359304 | tf_op jit(solution)/shard_map/ppermute | solution.py:48
  69.5 21.1 %collective-permute-start.11 = (bf16[512,512]{1,0:T(8,128)(2,1)S(1)}, bf16[512,512]{1,0:T(8,128)(2,1)S(1)}, u32[]{:S(2)}, u32[]{:S(2)}) collective-permute-start(bf16[512,512]{1,0:T(8,128)(2,1)S(1)} %get-tuple-element.170), channel_id=1, source_target_pairs={{0,4},{4,0},{1,5},{5,1},{2,6},{6,2},{3,7},{7,3},{8,12},{12,8},{9,1... | collective-permute-start | bytes 1572872 | tf_op jit(solution)/shard_map/ppermute | solution.py:48
  71.0 19.6 %copy-start.1 = (bf16[768,512]{1,0:T(8,128)(2,1)S(1)}, bf16[768,512]{1,0:T(8,128)(2,1)}, u32[]{:S(2)}) copy-start(bf16[768,512]{1,0:T(8,128)(2,1)} %get-tuple-element.123) | copy-start | bytes 2359300
  91.0 10.7 %collective-permute-start.13 = (bf16[384,512]{1,0:T(8,128)(2,1)S(1)}, bf16[384,512]{1,0:T(8,128)(2,1)S(1)}, u32[]{:S(2)}, u32[]{:S(2)}) collective-permute-start(bf16[384,512]{1,0:T(8,128)(2,1)S(1)} %get-tuple-element.171), channel_id=1, source_target_pairs={{0,4},{4,0},{1,5},{5,1},{2,6},{6,2},{3,7},{7,3},{8,12},{12,8},{9,1... | collective-permute-start | bytes 1179656 | tf_op jit(solution)/shard_map/ppermute | solution.py:48
  91.7 7.6 %collective-permute-start.14 = (bf16[256,512]{1,0:T(8,128)(2,1)S(1)}, bf16[256,512]{1,0:T(8,128)(2,1)S(1)}, u32[]{:S(2)}, u32[]{:S(2)}) collective-permute-start(bf16[256,512]{1,0:T(8,128)(2,1)S(1)} %fusion.5), channel_id=1, source_target_pairs={{0,2},{1,3},{2,0},{3,1},{4,6},{5,7},{6,4},{7,5},{8,10},{9,11},{10,... | collective-permute-start | bytes 786440 | tf_op jit(solution)/shard_map/ppermute | solution.py:48
  97.0 5.0 %collective-permute-start.15 = (bf16[128,1664]{1,0:T(8,128)(2,1)}, bf16[128,1664]{1,0:T(8,128)(2,1)S(1)}, u32[]{:S(2)}, u32[]{:S(2)}) collective-permute-start(bf16[128,1664]{1,0:T(8,128)(2,1)} %get-tuple-element.136), channel_id=1, source_target_pairs={{0,1},{1,0},{2,3},{3,2},{4,5},{5,4},{6,7},{7,6},{8,9},{9,8},{10,11... | collective-permute-start | bytes 1277960 | tf_op jit(solution)/shard_map/ppermute | solution.py:48
  97.0 15.5 %collective-permute-start.18 = (bf16[128,1664]{1,0:T(8,128)(2,1)}, bf16[128,1664]{1,0:T(8,128)(2,1)S(1)}, u32[]{:S(2)}, u32[]{:S(2)}) collective-permute-start(bf16[128,1664]{1,0:T(8,128)(2,1)} %get-tuple-element.147), channel_id=1, source_target_pairs={{0,1},{1,0},{2,3},{3,2},{4,5},{5,4},{6,7},{7,6},{8,9},{9,8},{10,11... | collective-permute-start | bytes 1277960 | tf_op jit(solution)/shard_map/ppermute | solution.py:48
  102.1 10.4 %collective-permute-start.19 = (bf16[128,1664]{1,0:T(8,128)(2,1)S(1)}, bf16[128,1664]{1,0:T(8,128)(2,1)S(1)}, u32[]{:S(2)}, u32[]{:S(2)}) collective-permute-start(bf16[128,1664]{1,0:T(8,128)(2,1)S(1)} %add_convert_fusion.5), channel_id=1, source_target_pairs={{0,2},{1,3},{2,0},{3,1},{4,6},{5,7},{6,4},{7,5},{8,10},{9,11},{10,... | collective-permute-start | bytes 1277960 | tf_op jit(solution)/shard_map/ppermute | solution.py:48
  102.8 8.3 %collective-permute-start.16 = (bf16[320,512]{1,0:T(8,128)(2,1)S(1)}, bf16[320,512]{1,0:T(8,128)(2,1)S(1)}, u32[]{:S(2)}, u32[]{:S(2)}) collective-permute-start(bf16[320,512]{1,0:T(8,128)(2,1)S(1)} %get-tuple-element.173), channel_id=1, source_target_pairs={{0,8},{8,0},{16,24},{24,16},{1,9},{9,1},{17,25},{25,17},{2,10},{10... | collective-permute-start | bytes 983048 | tf_op jit(solution)/shard_map/ppermute | solution.py:48
  109.3 11.6 %copy-start.10 = (bf16[512,512]{1,0:T(8,128)(2,1)S(1)}, bf16[512,512]{1,0:T(8,128)(2,1)}, u32[]{:S(2)}) copy-start(bf16[512,512]{1,0:T(8,128)(2,1)} %get-tuple-element.145) | copy-start | bytes 1572868
  112.7 5.9 %collective-permute-start.20 = (bf16[64,1664]{1,0:T(8,128)(2,1)S(1)}, bf16[64,1664]{1,0:T(8,128)(2,1)S(1)}, u32[]{:S(2)}, u32[]{:S(2)}) collective-permute-start(bf16[64,1664]{1,0:T(8,128)(2,1)S(1)} %dynamic-slice_bitcast_fusion.4), channel_id=1, source_target_pairs={{0,4},{4,0},{1,5},{5,1},{2,6},{6,2},{3,7},{7,3},{8,12},{12,8},{9,1... | collective-permute-start | bytes 638984 | tf_op jit(solution)/shard_map/ppermute | solution.py:48
  113.4 15.2 %collective-permute-start.22 = (bf16[320,512]{1,0:T(8,128)(2,1)S(1)}, bf16[320,512]{1,0:T(8,128)(2,1)S(1)}, u32[]{:S(2)}, u32[]{:S(2)}) collective-permute-start(bf16[320,512]{1,0:T(8,128)(2,1)S(1)} %add_convert_fusion.8), channel_id=1, source_target_pairs={{0,16},{8,24},{16,0},{24,8},{1,17},{9,25},{17,1},{25,9},{2,18},{10... | collective-permute-start | bytes 983048 | tf_op jit(solution)/shard_map/ppermute | solution.py:48
  118.7 10.7 %collective-permute-start.21 = (bf16[64,1664]{1,0:T(8,128)(2,1)S(1)}, bf16[64,1664]{1,0:T(8,128)(2,1)S(1)}, u32[]{:S(2)}, u32[]{:S(2)}) collective-permute-start(bf16[64,1664]{1,0:T(8,128)(2,1)S(1)} %fusion.6), channel_id=1, source_target_pairs={{0,8},{8,0},{16,24},{24,16},{1,9},{9,1},{17,25},{25,17},{2,10},{10... | collective-permute-start | bytes 638984 | tf_op jit(solution)/shard_map/ppermute | solution.py:48
  120.8 14.1 %collective-permute-start.17 = (bf16[512,512]{1,0:T(8,128)(2,1)S(1)}, bf16[512,512]{1,0:T(8,128)(2,1)S(1)}, u32[]{:S(2)}, u32[]{:S(2)}) collective-permute-start(bf16[512,512]{1,0:T(8,128)(2,1)S(1)} %copy-done.10), channel_id=1, source_target_pairs={{0,4},{4,0},{1,5},{5,1},{2,6},{6,2},{3,7},{7,3},{8,12},{12,8},{9,1... | collective-permute-start | bytes 1572872 | tf_op jit(solution)/shard_map/ppermute | solution.py:48
  129.5 10.8 %collective-permute-start.23 = (bf16[64,1664]{1,0:T(8,128)(2,1)S(1)}, bf16[64,1664]{1,0:T(8,128)(2,1)S(1)}, u32[]{:S(2)}, u32[]{:S(2)}) collective-permute-start(bf16[64,1664]{1,0:T(8,128)(2,1)S(1)} %add_convert_fusion.10), channel_id=1, source_target_pairs={{0,16},{8,24},{16,0},{24,8},{1,17},{9,25},{17,1},{25,9},{2,18},{10... | collective-permute-start | bytes 638984 | tf_op jit(solution)/shard_map/ppermute | solution.py:48
  131.7 11.2 %collective-permute-start.26 = (bf16[320,512]{1,0:T(8,128)(2,1)S(1)}, bf16[320,512]{1,0:T(8,128)(2,1)S(1)}, u32[]{:S(2)}, u32[]{:S(2)}) collective-permute-start(bf16[320,512]{1,0:T(8,128)(2,1)S(1)} %add_convert_fusion.7.own_a), channel_id=1, source_target_pairs={{0,8},{8,0},{16,24},{24,16},{1,9},{9,1},{17,25},{25,17},{2,10},{10... | collective-permute-start | bytes 983048 | tf_op jit(solution)/shard_map/ppermute | solution.py:48
  134.2 9.9 %collective-permute-start.25 = (bf16[320,512]{1,0:T(8,128)(2,1)S(1)}, bf16[320,512]{1,0:T(8,128)(2,1)S(1)}, u32[]{:S(2)}, u32[]{:S(2)}) collective-permute-start(bf16[320,512]{1,0:T(8,128)(2,1)S(1)} %add_convert_fusion.7.own_a), channel_id=1, source_target_pairs={{0,4},{4,0},{1,5},{5,1},{2,6},{6,2},{3,7},{7,3},{8,12},{12,8},{9,1... | collective-permute-start | bytes 983048 | tf_op jit(solution)/shard_map/ppermute | solution.py:48
  140.4 7.8 %collective-permute-start.24 = (bf16[64,1664]{1,0:T(8,128)(2,1)S(1)}, bf16[64,1664]{1,0:T(8,128)(2,1)S(1)}, u32[]{:S(2)}, u32[]{:S(2)}) collective-permute-start(bf16[64,1664]{1,0:T(8,128)(2,1)S(1)} %add_convert_fusion.9.own_ref), channel_id=1, source_target_pairs={{0,4},{4,0},{1,5},{5,1},{2,6},{6,2},{3,7},{7,3},{8,12},{12,8},{9,1... | collective-permute-start | bytes 638984 | tf_op jit(solution)/shard_map/ppermute | solution.py:48
  144.1 6.4 %collective-permute-start.28 = (bf16[160,512]{1,0:T(8,128)(2,1)S(1)}, bf16[160,512]{1,0:T(8,128)(2,1)S(1)}, u32[]{:S(2)}, u32[]{:S(2)}) collective-permute-start(bf16[160,512]{1,0:T(8,128)(2,1)S(1)} %slice.53), channel_id=1, source_target_pairs={{0,8},{8,0},{16,24},{24,16},{1,9},{9,1},{17,25},{25,17},{2,10},{10... | collective-permute-start | bytes 491528 | tf_op jit(solution)/shard_map/ppermute | solution.py:48
  144.5 6.0 %collective-permute-start.27 = (bf16[160,512]{1,0:T(8,128)(2,1)S(1)}, bf16[160,512]{1,0:T(8,128)(2,1)S(1)}, u32[]{:S(2)}, u32[]{:S(2)}) collective-permute-start(bf16[160,512]{1,0:T(8,128)(2,1)S(1)} %slice.52), channel_id=1, source_target_pairs={{0,4},{4,0},{1,5},{5,1},{2,6},{6,2},{3,7},{7,3},{8,12},{12,8},{9,1... | collective-permute-start | bytes 491528 | tf_op jit(solution)/shard_map/ppermute | solution.py:48
  (10 other events, 45.7 us)
